TPU v7x, 128 devices: a whole 4x4x4 slice. The times are simulated.
128 devices in a mesh: row: 8 (over z, core), col: 16 (over y, x).
Axes of the slice: x: 4, y: 4, z: 4, core: 2. Of those that a mesh axis runs over, the one named last changes fastest.
Arguments:
- a_matrix: float32 [16384, 16384], P('row', 'col'), may hold values from -2.25 to 2.25
- b_matrix: float32 [16384, 16384], P('row', 'col'), may hold values from -0.1 to 3.1
- x_block: float32 [16384, 64], P('row'), may hold values from -6 to 6
- r_block: float32 [16384, 64], P('row'), may hold values from -6 to 6
- p_block: float32 [16384, 64], P('row'), may hold values from -6 to 6
Outputs:
- x_next: float32 [16384, 64], P('row')
- r_next: float32 [16384, 64], P('row')
- p_next: float32 [16384, 64], P('row')
All inputs are finite; a program needn't handle non-finite values.
Results may differ from a plain program's by a relative error of at most 0.0003.
Values sent between devices are 32-bit elements; how exact they have to be, the bound alone decides.
No kernel may reach another device: no remote copies, remote signals or barrier semaphores. Data moves between devices by JAX's collectives and lax.ppermute only.
A program may use at most 128 MiB of HBM per device.

v0:
```python
import math

import jax
import jax.numpy as jnp
from jax import lax
from jax.sharding import PartitionSpec as P

N = 16384
ITERS = 2
NS_STEPS = 8


def padded_to(lines, size):
    spare = -len(lines) % size
    return jnp.pad(lines, [(0, spare)] + [(0, 0)] * (lines.ndim - 1))


def broadcast_by_parts(x, axis, root):
    lines = jnp.where(lax.axis_index(axis) == root, x, jnp.zeros_like(x)).reshape(
        -1, *x.shape[1:][-1:]
    )
    padded = padded_to(lines, lax.axis_size(axis))
    own = lax.psum_scatter(padded, axis, scatter_dimension=0, tiled=True)
    return lax.all_gather(own, axis, axis=0, tiled=True)[: len(lines)].reshape(x.shape)


def over_pieces(x, axis):
    return lax.all_gather(x, axis).sum(0)


def matmul(left, right):
    return jnp.dot(left, right, precision=lax.Precision.HIGHEST, preferred_element_type=jnp.float32)


def ritz_step(gram_a, gram_b, count):
    gram_a = 0.5 * (gram_a + gram_a.T)
    gram_b = 0.5 * (gram_b + gram_b.T)
    lower = jnp.linalg.cholesky(gram_b)
    half = lax.linalg.triangular_solve(lower, gram_a, left_side=True, lower=True)
    middle = lax.linalg.triangular_solve(lower, half.T, left_side=True, lower=True)
    middle = 0.5 * (middle + middle.T)
    extent = middle.shape[0]
    ident = jnp.eye(extent, dtype=middle.dtype)
    shift = jnp.trace(middle) / extent
    centred = middle - shift * ident
    sign_est = centred / jnp.sqrt(jnp.sum(centred * centred) + 1e-06)
    for turn in range(NS_STEPS):
        sign_est = 1.5 * sign_est - 0.5 * matmul(sign_est, matmul(sign_est, sign_est))
    filtered = (0.5 * (ident - sign_est))[:, :count]
    coords = lax.linalg.triangular_solve(
        lower, filtered, left_side=True, lower=True, transpose_a=True
    ) * math.sqrt(N)
    reduced = matmul(filtered.T, matmul(middle, filtered))
    return (coords, reduced)


def local(a_matrix, b_matrix, x_block, r_block, p_block):
    ratio = lax.axis_size("col") // lax.axis_size("row")
    col_index = lax.axis_index("col")
    tile_cols = a_matrix.shape[1]
    width = x_block.shape[1]
    for turn in range(ITERS):
        panel = jnp.concatenate([x_block, r_block, p_block], axis=1)
        own_part = lax.dynamic_slice_in_dim(panel, col_index % ratio * tile_cols, tile_cols, 0)
        matched = broadcast_by_parts(own_part, "row", col_index // ratio)
        products = lax.psum(
            jnp.concatenate([matmul(a_matrix, matched), matmul(b_matrix, matched)], axis=1), "col"
        )
        grams = over_pieces(matmul(panel.T, products), "row")
        coords, reduced = ritz_step(grams[:, : 3 * width], grams[:, 3 * width :], width)
        new_resid = matmul(products[:, : 3 * width], coords) - matmul(
            matmul(products[:, 3 * width :], coords), reduced
        )
        x_block = matmul(panel, coords)
        p_block = matmul(panel[:, width:], coords[width:])
        r_block = new_resid
    return (x_block, r_block, p_block)


def solution(mesh):
    return jax.shard_map(
        local,
        mesh=mesh,
        in_specs=(P("row", "col"), P("row", "col"), P("row", None), P("row", None), P("row", None)),
        out_specs=(P("row", None), P("row", None), P("row", None)),
        check_vma=False,
    )
```

profile of v0, /device:TPU:0, one launch (start us, length us, event | category | flops | bytes accessed | tf_op | source)
XLA Modules:
  0.0 569.1 jit_solution(13567429440212739692)
XLA Ops:
  10.5 34.1 %reduce-scatter.3.cloned.1.call-done = f32[128,192]{0,1:T(8,128)} async-done(((f32[1024,192]{0,1:T(8,128)}), f32[128,192]{0,1:T(8,128)}) %reduce-scatter.3.cloned.1.call-update) | async-done | bytes 98320 | tf_op jit(solution)/shard_map/reduce_scatter | solution.py:23
  44.7 13.7 %all_gather.18 = f32[1024,192]{0,1:T(8,128)S(1)} all-gather(f32[128,192]{0,1:T(8,128)} %reduce-scatter.3.cloned.1.call-done), channel_id=1, replica_groups=mesh['row'=8,'col'=16] {'row'}, dimensions={0}, use_global_device_ids=true | all-gather | bytes 884736 | tf_op jit(solution)/shard_map/all_gather | solution.py:24
  58.3 10.9 %convolution_bitcast_fusion.2 = f32[2048,192]{0,1:T(8,128)S(1)} fusion(f32[1024,192]{0,1:T(8,128)S(1)} %all_gather.18, f32[2048,1024]{1,0:T(8,128)} %param.11), kind=kOutput, calls=%fused_computation.4 | convolution fusion | flops 4831838208 | bytes 10747904 | tf_op jit(solution)/shard_map/dot_general | solution.py:32
  69.3 10.9 %convolution_bitcast_fusion.3 = f32[2048,192]{0,1:T(8,128)S(1)} fusion(f32[1024,192]{0,1:T(8,128)S(1)} %all_gather.18, f32[2048,1024]{1,0:T(8,128)} %param.10), kind=kOutput, calls=%fused_computation.5 | convolution fusion | flops 4831838208 | bytes 10747904 | tf_op jit(solution)/shard_map/dot_general | solution.py:32
  82.4 95.4 %all-reduce.8.cloned.1.call-done = f32[2048,384]{0,1:T(8,128)} async-done(((f32[2048,384]{0,1:T(8,128)}), f32[2048,384]{0,1:T(8,128)}) %all-reduce.8.cloned.1.call-update) | async-done | bytes 3145744 | tf_op jit(solution)/shard_map/psum | solution.py:66
  177.7 5.9 %fusion.104 = f32[192,384]{1,0:T(8,128)} fusion(f32[2048,192]{0,1:T(8,128)S(1)} %constant_dynamic-update-slice_fusion, f32[2048,384]{0,1:T(8,128)} %all-reduce.8.cloned.1.call-done), kind=kOutput, calls=%fused_computation.191 | convolution fusion | flops 1811939328 | bytes 5013504 | tf_op jit(solution)/shard_map/dot_general | solution.py:32
  183.9 24.8 %all-gather.5.cloned.1.call-done = f32[1536,384]{1,0:T(8,128)} async-done(((f32[192,384]{1,0:T(8,128)}), f32[1536,384]{1,0:T(8,128)}) %all-gather.5.cloned.1.call-update) | async-done | bytes 2359312 | tf_op jit(solution)/shard_map/all_gather | solution.py:28
  211.1 11.7 %cholesky.136 = f32[128,128]{1,0:T(8,128)S(1)} custom-call(f32[128,128]{1,0:T(8,128)S(1)} %copy.11), custom_call_target="Cholesky" | custom-call | tf_op jit(solution)/shard_map/jit(cholesky)/cholesky | solution.py:38
  222.9 9.8 %custom-call.19 = f32[1,128,128]{1,2,0:T(8,128)S(1)} custom-call(f32[1,128,128]{2,1,0:T(8,128)S(1)} %get-tuple-element.81), custom_call_target="InvertDiagBlocksLowerTriangular" | custom-call | tf_op jit(solution)/shard_map/jit(cholesky)/cholesky | solution.py:38
  233.2 5.9 %cholesky.156 = f32[64,64]{1,0:T(8,128)S(1)} custom-call(f32[64,64]{1,0:T(8,128)S(1)} %copy.13), custom_call_target="Cholesky" | custom-call | tf_op jit(solution)/shard_map/jit(cholesky)/cholesky | solution.py:38
  241.9 19.9 %custom-call.22 = f32[2,128,128]{1,2,0:T(8,128)S(1)} custom-call(f32[2,128,128]{2,1,0:T(8,128)S(1)} %pad_maximum_fusion.5), custom_call_target="InvertDiagBlocksLowerTriangular" | custom-call | tf_op jit(solution)/shard_map/triangular_solve/custom-call.4 | solution.py:50
  279.2 3.9 fusion.4
  286.8 32.2 %reduce-scatter.5.cloned.1.call-done = f32[128,192]{0,1:T(8,128)} async-done(((f32[1024,192]{0,1:T(8,128)}), f32[128,192]{0,1:T(8,128)}) %reduce-scatter.5.cloned.1.call-update) | async-done | bytes 98320 | tf_op jit(solution)/shard_map/reduce_scatter | solution.py:23
  318.9 13.7 %all_gather.21 = f32[1024,192]{0,1:T(8,128)S(1)} all-gather(f32[128,192]{0,1:T(8,128)} %reduce-scatter.5.cloned.1.call-done), channel_id=1, replica_groups=mesh['row'=8,'col'=16] {'row'}, dimensions={0}, use_global_device_ids=true | all-gather | bytes 884736 | tf_op jit(solution)/shard_map/all_gather | solution.py:24
  332.6 10.9 %convolution_bitcast_fusion = f32[2048,192]{0,1:T(8,128)S(1)} fusion(f32[1024,192]{0,1:T(8,128)S(1)} %all_gather.21, f32[2048,1024]{1,0:T(8,128)} %param.11), kind=kOutput, calls=%fused_computation.2 | convolution fusion | flops 4831838208 | bytes 10747904 | tf_op jit(solution)/shard_map/dot_general | solution.py:32
  343.6 10.9 %convolution_bitcast_fusion.1 = f32[2048,192]{0,1:T(8,128)S(1)} fusion(f32[1024,192]{0,1:T(8,128)S(1)} %all_gather.21, f32[2048,1024]{1,0:T(8,128)} %param.10), kind=kOutput, calls=%fused_computation.3 | convolution fusion | flops 4831838208 | bytes 10747904 | tf_op jit(solution)/shard_map/dot_general | solution.py:32
  356.8 95.1 %all-reduce.10.cloned.1.call-done = f32[2048,384]{0,1:T(8,128)} async-done(((f32[2048,384]{0,1:T(8,128)}), f32[2048,384]{0,1:T(8,128)}) %all-reduce.10.cloned.1.call-update) | async-done | bytes 3145744 | tf_op jit(solution)/shard_map/psum | solution.py:66
  451.9 5.9 %fusion.101 = f32[192,384]{1,0:T(8,128)} fusion(f32[2048,384]{0,1:T(8,128)} %all-reduce.10.cloned.1.call-done, f32[2048,64]{0,1:T(8,128)S(1)} %fusion.28, f32[2048,64]{0,1:T(8,128)S(1)} %convolution_subtract_fusion.1, f32[2048,64]{0,1:T(8,128)S(1)} %fusion.100), kind=kOutput, calls=%fused_computation.190 | convolution fusion | flops 1812725760 | bytes 5013504 | tf_op jit(solution)/shard_map/dot_general | solution.py:32
  457.8 25.0 %all-gather.7.cloned.1.call-done = f32[1536,384]{1,0:T(8,128)} async-done(((f32[192,384]{1,0:T(8,128)}), f32[1536,384]{1,0:T(8,128)}) %all-gather.7.cloned.1.call-update) | async-done | bytes 2359312 | tf_op jit(solution)/shard_map/all_gather | solution.py:28
  485.3 11.7 %cholesky.174 = f32[128,128]{1,0:T(8,128)S(1)} custom-call(f32[128,128]{1,0:T(8,128)S(1)} %cholesky.211), custom_call_target="Cholesky" | custom-call | tf_op jit(solution)/shard_map/jit(cholesky)/cholesky | solution.py:38
  497.1 9.8 %custom-call.23 = f32[1,128,128]{1,2,0:T(8,128)S(1)} custom-call(f32[1,128,128]{2,1,0:T(8,128)S(1)} %get-tuple-element.79), custom_call_target="InvertDiagBlocksLowerTriangular" | custom-call | tf_op jit(solution)/shard_map/jit(cholesky)/cholesky | solution.py:38
  507.3 5.8 %cholesky.194 = f32[64,64]{1,0:T(8,128)S(1)} custom-call(f32[64,64]{1,0:T(8,128)S(1)} %convolution_subtract_fusion.7), custom_call_target="Cholesky" | custom-call | tf_op jit(solution)/shard_map/jit(cholesky)/cholesky | solution.py:38
  515.9 19.9 %custom-call.26 = f32[2,128,128]{1,2,0:T(8,128)S(1)} custom-call(f32[2,128,128]{2,1,0:T(8,128)S(1)} %pad_maximum_fusion.6), custom_call_target="InvertDiagBlocksLowerTriangular" | custom-call | tf_op jit(solution)/shard_map/triangular_solve/custom-call.4 | solution.py:50
  554.8 3.7 fusion
  (151 shorter events, 56.9 us)
Async XLA Ops:
  7.2 2.3 copy-start.3
  7.2 37.5 %reduce-scatter.3.cloned.1.call-start = ((), (), s32[]{:S(2)}) async-start(), calls=%async_computation.2 | async-start | bytes 884736 | tf_op jit(solution)/shard_map/reduce_scatter | solution.py:23
  10.5 167.3 %all-reduce.8.cloned.1.call-start = ((), (), s32[]{:S(2)}) async-start(), calls=%async_computation.3 | async-start | bytes 6291456 | tf_op jit(solution)/shard_map/psum | solution.py:66
  82.3 126.4 %all-gather.5.cloned.1.call-start = ((), (), s32[]{:S(2)}) async-start(), calls=%async_computation.6 | async-start | bytes 2654208 | tf_op jit(solution)/shard_map/all_gather | solution.py:28
  183.7 135.3 %reduce-scatter.5.cloned.1.call-start = ((), (), s32[]{:S(2)}) async-start(), calls=%async_computation.4 | async-start | bytes 884736 | tf_op jit(solution)/shard_map/reduce_scatter | solution.py:23
  276.1 2.4 copy-start.2
  277.1 2.2 copy-start
  286.7 165.2 %all-reduce.10.cloned.1.call-start = ((), (), s32[]{:S(2)}) async-start(), calls=%async_computation.5 | async-start | bytes 6291456 | tf_op jit(solution)/shard_map/psum | solution.py:66
  356.6 126.2 %all-gather.7.cloned.1.call-start = ((), (), s32[]{:S(2)}) async-start(), calls=%async_computation.7 | async-start | bytes 2654208 | tf_op jit(solution)/shard_map/all_gather | solution.py:28
  551.1 3.7 copy-start.1
Sparse Core Ops, SparseCore 0:
  10.6 34.0 reduce-scatter.2
  82.4 95.2 all-reduce.7
  183.8 24.8 all-gather.4
  286.9 32.0 reduce-scatter.4
  356.7 95.1 all-reduce.9
  457.9 24.8 all-gather.6
where the time goes:
time: 579 us; the launch traced here: 569 us
  waiting for transfers between devices  307 us (53%)
  other arithmetic  110 us (19%)
  matrix products  99.7 us (17%)
  blocking collectives  27.3 us (5%)
  between operations  20.7 us (4%)
    psum x2, waiting for transfers between devices, local(): lax.psum(jnp.concatenate([matmul(a_matrix, matched), matmul(b_matrix, mat...  190 us
    dot_general x52, matrix products, matmul(): jnp.dot(left, right, precision=lax.Precision.HIGHEST, preferred_element_t...  94.4 us
    reduce_scatter x2, waiting for transfers between devices, broadcast_by_parts(): own = lax.psum_scatter(padded, axis, scatter_dimension=0, tiled=True)  66.3 us
    another operation x14, other arithmetic, ritz_step(): lower = jnp.linalg.cholesky(gram_b)  57.4 us
    all_gather x2, waiting for transfers between devices, over_pieces(): return lax.all_gather(x, axis).sum(0)  49.8 us
    another operation x10, other arithmetic, ritz_step(): lax.linalg.triangular_solve(lower, filtered, left_side=True, lower=True,...  40 us
    all_gather x2, blocking collectives, broadcast_by_parts(): lax.all_gather(own, axis, axis=0, tiled=True)[:len(lines)].reshape(x.shape)  27.3 us
  transfers between devices with their start and end apart: 6, of which 6 were waited for; matrix products, arithmetic and copies ran while one was open for 0% of the time, Pallas kernels for 0%

commit v1 on v0

v1 whole, which is shorter than its diff:
```python
import math

import jax
import jax.numpy as jnp
from jax import lax
from jax.sharding import PartitionSpec as P

NS_STEPS = 8
BOTH = ("row", "col")


def mm(left, right, dims=((1,), (0,)), precision=lax.Precision.HIGHEST):
    return lax.dot_general(
        left, right, (dims, ((), ())), precision=precision, preferred_element_type=jnp.float32
    )


def share(x, axis):
    copies = jnp.broadcast_to(x[None], (lax.axis_size(axis),) + x.shape)
    return lax.all_to_all(copies, axis, 0, 0)


def sum_everywhere(x):
    parts = x.reshape(lax.axis_size("row"), -1, x.shape[-1])
    own = lax.all_to_all(parts, "row", 0, 0).sum(0)
    own = share(own, "col").sum(0)
    return share(own, "row").reshape(x.shape)


def sides(gram, k):
    return [gram[i * k : (i + 1) * k, j * k : (j + 1) * k] for i in range(3) for j in range(i + 1)]


def whole(blocks):
    b00, b10, b11, b20, b21, b22 = blocks
    return jnp.concatenate(
        [
            jnp.concatenate([b00, b10.T, b20.T], 1),
            jnp.concatenate([b10, b11, b21.T], 1),
            jnp.concatenate([b20, b21, b22], 1),
        ],
        0,
    )


def ritz_step(gram_a, gram_b, count, order):
    lower = jnp.linalg.cholesky(gram_b)
    half = lax.linalg.triangular_solve(lower, gram_a, left_side=True, lower=True)
    middle = lax.linalg.triangular_solve(lower, half.T, left_side=True, lower=True)
    middle = 0.5 * (middle + middle.T)
    extent = middle.shape[0]
    ident = jnp.eye(extent, dtype=middle.dtype)
    shift = jnp.trace(middle) / extent
    centred = middle - shift * ident
    sign_est = centred / jnp.sqrt(jnp.sum(centred * centred) + 1e-06)
    for turn in range(NS_STEPS):
        sign_est = 1.5 * sign_est - 0.5 * mm(sign_est, mm(sign_est, sign_est))
    filtered = (0.5 * (ident - sign_est))[:, :count]
    coords = lax.linalg.triangular_solve(
        lower, filtered, left_side=True, lower=True, transpose_a=True
    ) * math.sqrt(order)
    reduced = mm(filtered.T, mm(middle, filtered))
    return (coords, reduced)


def symmetric(x):
    return 0.5 * (x + x.T)


def local(a_matrix, b_matrix, x_block, r_block, p_block):
    rows, cols = lax.axis_size("row"), lax.axis_size("col")
    count = rows * cols
    k = x_block.shape[1]
    order = x_block.shape[0] * rows
    piece = order // count
    high = lax.Precision.HIGH
    to_col = [(b, (b % rows) * cols + b // rows) for b in range(count)]
    to_row = [(d, s) for s, d in to_col]

    panel = jnp.concatenate([x_block.T, r_block.T, p_block.T], 0)
    start = lax.axis_index("col") * piece
    own_row = lax.dynamic_slice_in_dim(panel, start, piece, 1)
    own_col = lax.ppermute(own_row, BOTH, to_col)

    prods = jnp.concatenate(
        [mm(panel, a_matrix, precision=high), mm(panel, b_matrix, precision=high)], 0
    )
    prods_by_piece = prods.reshape(6 * k, rows, piece).transpose(1, 0, 2)
    prod_col = lax.psum_scatter(prods_by_piece, "row", scatter_dimension=0)
    prod_row = lax.ppermute(prod_col, BOTH, to_row)
    matched = share(own_col, "row").transpose(1, 0, 2).reshape(3 * k, -1)
    grams = mm(prods, matched, ((1,), (1,)), high)
    packed = jnp.concatenate(
        [
            jnp.concatenate([ga, gb], 1)
            for ga, gb in zip(
                sides(symmetric(grams[: 3 * k]), k), sides(symmetric(grams[3 * k :]), k)
            )
        ],
        0,
    )
    packed = sum_everywhere(packed).reshape(6, k, 2 * k)
    gram_a = whole([packed[i, :, :k] for i in range(6)])
    gram_b = whole([packed[i, :, k:] for i in range(6)])
    coords, reduced = ritz_step(gram_a, gram_b, k, order)

    turn = jnp.concatenate([coords, -mm(coords, reduced)], 0)
    resid_col = mm(turn, prod_col, ((0,), (0,)))
    resid_row = mm(turn, prod_row, ((0,), (0,)))
    resid = share(resid_col, "row").transpose(1, 0, 2).reshape(k, -1)
    parts = jnp.concatenate(
        [
            mm(resid, a_matrix, ((1,), (1,)), high),
            mm(resid, b_matrix, ((1,), (1,)), high),
        ],
        0,
    )
    parts = parts.reshape(2 * k, cols, piece).transpose(1, 0, 2)
    more_row = lax.all_to_all(parts, "col", 0, 0).sum(0)

    shift_coords = jnp.concatenate([jnp.zeros_like(coords[:k]), coords[k:]], 0)
    basis = jnp.concatenate([coords, shift_coords], 1)
    kept = mm(basis, own_row, ((0,), (0,)))
    tests = jnp.concatenate([kept[:k], resid_row, kept[k:]], 0)
    fresh = mm(tests, more_row, ((1,), (1,)))
    fresh = sum_everywhere(fresh)
    old_a = symmetric(mm(basis, mm(gram_a, basis), ((0,), (0,))))
    old_b = symmetric(mm(basis, mm(gram_b, basis), ((0,), (0,))))

    def joined(old, new):
        return whole(
            [
                old[:k, :k],
                new[:k].T,
                symmetric(new[k : 2 * k]),
                old[k:, :k],
                new[2 * k :],
                old[k:, k:],
            ]
        )

    coords2, reduced2 = ritz_step(
        joined(old_a, fresh[:, :k]), joined(old_b, fresh[:, k:]), k, order
    )
    from_x, from_r, from_p = coords2[:k], coords2[k : 2 * k], coords2[2 * k :]
    move_p = mm(shift_coords, from_p)
    move_x = mm(coords, from_x) + move_p
    part_r = mm(from_r, resid_row, ((0,), (0,)))
    x_own = mm(move_x, own_row, ((0,), (0,))) + part_r
    p_own = mm(move_p, own_row, ((0,), (0,))) + part_r
    r_own = (
        mm(jnp.concatenate([move_x, -mm(move_x, reduced2)], 0), prod_row, ((0,), (0,)))
        + mm(jnp.concatenate([from_r, -mm(from_r, reduced2)], 0), more_row, ((0,), (0,)))
    )
    outs = share(jnp.concatenate([x_own, r_own, p_own], 0), "col")
    outs = outs.transpose(1, 0, 2).reshape(3 * k, -1)
    return (outs[:k].T, outs[k : 2 * k].T, outs[2 * k :].T)


def solution(mesh):
    return jax.shard_map(
        local,
        mesh=mesh,
        in_specs=(P("row", "col"), P("row", "col"), P("row", None), P("row", None), P("row", None)),
        out_specs=(P("row", None), P("row", None), P("row", None)),
        check_vma=False,
    )
```

time: 579 us -> 356 us (0.61)
  waiting for transfers between devices: 307 us -> 62.5 us
  starting transfers between devices: 0.59 us -> 56.3 us
  matrix products: 99.7 us -> 58.2 us
  blocking collectives: 27.3 us -> 34.8 us
  local copies, waits for them, and re-layouts: 3.89 us -> 11 us
    psum x2 -> x0, waiting for transfers between devices: 190 us -> none  [local(): lax.psum(jnp.concatenate([matmul(a_matrix, matched), matmul(b_matrix, mat...]
    reduce_scatter x2 -> x1, waiting for transfers between devices: 66.3 us -> 0.02 us  [local(): prod_col = lax.psum_scatter(prods_by_piece, 'row', scatter_dimension=0)]
    all_to_all x0 -> x8, waiting for transfers between devices: none -> 62.4 us  [the longest x6 40.1 us: share(): return lax.all_to_all(copies, axis, 0, 0)]
    all_to_all x0 -> x8, starting transfers between devices: none -> 54.8 us  [the longest x6 41.2 us: share(): return lax.all_to_all(copies, axis, 0, 0)]
    all_gather x2 -> x0, waiting for transfers between devices: 49.8 us -> none  [over_pieces(): return lax.all_gather(x, axis).sum(0)]
    dot_general x52 -> x59, matrix products: 94.4 us -> 52.2 us  [mm(): lax.dot_general(left, right, (dims, ((), ())), precision=precision, prefe...]
    all_to_all x0 -> x2, blocking collectives: none -> 34.8 us  [the longest x1 25.6 us: share(): return lax.all_to_all(copies, axis, 0, 0)]
    all_gather x2 -> x0, blocking collectives: 27.3 us -> none  [broadcast_by_parts(): lax.all_gather(own, axis, axis=0, tiled=True)[:len(lines)].reshape(x.shape)]
  transfers between devices with their start and end apart: 6 -> 11, of which waited for: 6 -> 8; matrix products, arithmetic and copies ran while one was open for 0% -> 23% of each run, Pallas kernels for 0% -> 0%
where the time goes in v1:
time: 356 us; the launch traced here: 349 us
  other arithmetic  105 us (29%)
  waiting for transfers between devices  62.5 us (18%)
  matrix products  58.2 us (16%)
  starting transfers between devices  56.3 us (16%)
  blocking collectives  34.8 us (10%)
  between operations  20.9 us (6%)
  local copies, waits for them, and re-layouts  11 us (3%)
    another operation x14, other arithmetic, ritz_step(): lower = jnp.linalg.cholesky(gram_b)  57.4 us
    dot_general x59, matrix products, mm(): lax.dot_general(left, right, (dims, ((), ())), precision=precision, prefe...  52.2 us
    all_to_all x6, starting transfers between devices, share(): return lax.all_to_all(copies, axis, 0, 0)  41.2 us
    another operation x10, other arithmetic, ritz_step(): lax.linalg.triangular_solve(lower, filtered, left_side=True, lower=True,...  40.3 us
    all_to_all x6, waiting for transfers between devices, share(): return lax.all_to_all(copies, axis, 0, 0)  40.1 us
    all_to_all x1, blocking collectives, share(): return lax.all_to_all(copies, axis, 0, 0)  25.6 us
    all_to_all x1, waiting for transfers between devices, local(): more_row = lax.all_to_all(parts, 'col', 0, 0).sum(0)  16.5 us
    all_to_all x1, starting transfers between devices, sum_everywhere(): own = lax.all_to_all(parts, 'row', 0, 0).sum(0)  9.81 us
  transfers between devices with their start and end apart: 11, of which 8 were waited for; matrix products, arithmetic and copies ran while one was open for 23% of the time, Pallas kernels for 0%

profile of v1, /device:TPU:0, one launch (start us, length us, event | category | flops | bytes accessed | tf_op | source)
XLA Modules:
  0.0 349.1 jit_solution(6963319498418338156)
XLA Ops:
  10.5 17.8 %all-to-all-start = ((f32[8,192,128]{2,1,0:T(8,128)}), f32[8,192,128]{2,1,0:T(8,128)}, u32[]{:S(2)}, u32[]{:S(2)}) async-start(f32[8,192,128]{2,1,0:T(8,128)} %broadcast_in_dim.20), calls=%async_computation | async-start | bytes 1572864 | tf_op jit(solution)/shard_map/all_to_all | solution.py:20
  28.4 5.8 %fusion.154 = f32[192,1024]{1,0:T(8,128)S(1)} fusion(f32[2048,1024]{1,0:T(8,128)} %param.11, f32[64,2048]{1,0:T(8,128)S(1)} %bitcast.323, f32[64,2048]{1,0:T(8,128)S(1)} %bitcast.326, f32[64,2048]{1,0:T(8,128)S(1)} %bitcast.329), kind=kOutput, calls=%fused_computation.279 | convolution fusion | flops 2416705536 | bytes 10747904 | tf_op jit(solution)/shard_map/dot_general | solution.py:13
  44.6 9.2 %all_to_all.50 = f32[8,48,128]{2,1,0:T(8,128)S(1)} all-to-all(f32[8,48,128]{2,1,0:T(8,128)S(1)} %bitcast.334), channel_id=1, replica_groups=mesh['row'=8,'col'=16] {'row'}, dimensions={0} | all-to-all | bytes 393216 | tf_op jit(solution)/shard_map/all_to_all | solution.py:25
  54.6 7.8 %all-to-all-start.2 = ((f32[16,48,128]{2,1,0:T(8,128)}), f32[16,48,128]{2,1,0:T(8,128)S(1)}, u32[]{:S(2)}, u32[]{:S(2)}) async-start(f32[16,48,128]{2,1,0:T(8,128)} %broadcast_in_dim.21), calls=%async_computation.2 | async-start | bytes 786432 | tf_op jit(solution)/shard_map/all_to_all | solution.py:20
  63.7 8.5 %all-to-all-done.2 = f32[16,48,128]{2,1,0:T(8,128)S(1)} async-done(((f32[16,48,128]{2,1,0:T(8,128)}), f32[16,48,128]{2,1,0:T(8,128)S(1)}, u32[]{:S(2)}, u32[]{:S(2)}) %all-to-all-start.2) | async-done | bytes 393248 | tf_op jit(solution)/shard_map/all_to_all | solution.py:20
  76.6 7.5 %all-to-all-done.3 = f32[8,48,128]{2,1,0:T(8,128)S(1)} async-done(((f32[8,48,128]{2,1,0:T(8,128)}), f32[8,48,128]{2,1,0:T(8,128)S(1)}, u32[]{:S(2)}, u32[]{:S(2)}) %all-to-all-start.3) | async-done | bytes 196640 | tf_op jit(solution)/shard_map/all_to_all | solution.py:20
  85.1 11.7 %cholesky.136 = f32[128,128]{1,0:T(8,128)S(1)} custom-call(f32[128,128]{1,0:T(8,128)S(1)} %cholesky.208), custom_call_target="Cholesky" | custom-call | tf_op jit(solution)/shard_map/jit(cholesky)/cholesky | solution.py:47
  96.9 9.8 %custom-call.19 = f32[1,128,128]{1,2,0:T(8,128)S(1)} custom-call(f32[1,128,128]{2,1,0:T(8,128)S(1)} %get-tuple-element.132), custom_call_target="InvertDiagBlocksLowerTriangular" | custom-call | tf_op jit(solution)/shard_map/jit(cholesky)/cholesky | solution.py:47
  107.1 5.8 %cholesky.156 = f32[64,64]{1,0:T(8,128)S(1)} custom-call(f32[64,64]{1,0:T(8,128)S(1)} %convolution_subtract_fusion.7), custom_call_target="Cholesky" | custom-call | tf_op jit(solution)/shard_map/jit(cholesky)/cholesky | solution.py:47
  116.0 20.1 %custom-call.22 = f32[2,128,128]{1,2,0:T(8,128)S(1)} custom-call(f32[2,128,128]{2,1,0:T(8,128)S(1)} %pad_maximum_fusion.5), custom_call_target="InvertDiagBlocksLowerTriangular" | custom-call | tf_op jit(solution)/shard_map/triangular_solve/custom-call.4 | solution.py:59
  159.2 6.7 %all-to-all-done.4 = f32[8,64,128]{2,1,0:T(8,128)S(1)} async-done(((f32[8,64,128]{2,1,0:T(8,128)}), f32[8,64,128]{2,1,0:T(8,128)S(1)}, u32[]{:S(2)}, u32[]{:S(2)}) %all-to-all-start.4) | async-done | bytes 262176 | tf_op jit(solution)/shard_map/all_to_all | solution.py:20
  165.9 7.3 %fusion.24 = f32[64,2048]{1,0:T(8,128)S(1)} fusion(f32[2048,1024]{1,0:T(8,128)} %param.11, f32[8,64,128]{2,1,0:T(8,128)S(1)} %all-to-all-done.4), kind=kOutput, calls=%fused_computation.66 | convolution fusion | flops 805306368 | bytes 9175040 | tf_op jit(solution)/shard_map/dot_general | solution.py:13
  173.2 7.3 %fusion.26 = f32[64,2048]{1,0:T(8,128)S(1)} fusion(f32[2048,1024]{1,0:T(8,128)} %param.10, f32[8,64,128]{2,1,0:T(8,128)S(1)} %all-to-all-done.4), kind=kOutput, calls=%fused_computation.68 | convolution fusion | flops 805306368 | bytes 9175040 | tf_op jit(solution)/shard_map/dot_general | solution.py:13
  186.8 16.5 %all-to-all-done.5 = f32[16,128,128]{2,1,0:T(8,128)S(1)} async-done(((f32[16,128,128]{2,1,0:T(8,128)}), f32[16,128,128]{2,1,0:T(8,128)S(1)}, u32[]{:S(2)}, u32[]{:S(2)}) %all-to-all-start.5) | async-done | bytes 1048608 | tf_op jit(solution)/shard_map/all_to_all | solution.py:119
  204.3 9.8 %all-to-all-start.6 = ((f32[8,24,128]{2,1,0:T(8,128)}), f32[8,24,128]{2,1,0:T(8,128)S(1)}, u32[]{:S(2)}, u32[]{:S(2)}) async-start(f32[8,24,128]{2,1,0:T(8,128)} %fusion.80), calls=%async_computation.7 | async-start | bytes 196608 | tf_op jit(solution)/shard_map/all_to_all | solution.py:25
  214.1 5.8 %all-to-all-done.6 = f32[8,24,128]{2,1,0:T(8,128)S(1)} async-done(((f32[8,24,128]{2,1,0:T(8,128)}), f32[8,24,128]{2,1,0:T(8,128)S(1)}, u32[]{:S(2)}, u32[]{:S(2)}) %all-to-all-start.6) | async-done | bytes 98336 | tf_op jit(solution)/shard_map/all_to_all | solution.py:25
  220.6 4.8 %all-to-all-start.7 = ((f32[16,24,128]{2,1,0:T(8,128)}), f32[16,24,128]{2,1,0:T(8,128)S(1)}, u32[]{:S(2)}, u32[]{:S(2)}) async-start(f32[16,24,128]{2,1,0:T(8,128)} %broadcast_in_dim.25), calls=%async_computation.8 | async-start | bytes 393216 | tf_op jit(solution)/shard_map/all_to_all | solution.py:20
  225.5 8.3 %all-to-all-done.7 = f32[16,24,128]{2,1,0:T(8,128)S(1)} async-done(((f32[16,24,128]{2,1,0:T(8,128)}), f32[16,24,128]{2,1,0:T(8,128)S(1)}, u32[]{:S(2)}, u32[]{:S(2)}) %all-to-all-start.7) | async-done | bytes 196640 | tf_op jit(solution)/shard_map/all_to_all | solution.py:20
  238.2 5.5 %all-to-all-done.8 = f32[8,24,128]{2,1,0:T(8,128)S(1)} async-done(((f32[8,24,128]{2,1,0:T(8,128)}), f32[8,24,128]{2,1,0:T(8,128)S(1)}, u32[]{:S(2)}, u32[]{:S(2)}) %all-to-all-start.8) | async-done | bytes 98336 | tf_op jit(solution)/shard_map/all_to_all | solution.py:20
  244.8 11.7 %cholesky.174 = f32[128,128]{1,0:T(8,128)S(1)} custom-call(f32[128,128]{1,0:T(8,128)S(1)} %cholesky.211), custom_call_target="Cholesky" | custom-call | tf_op jit(solution)/shard_map/jit(cholesky)/cholesky | solution.py:47
  256.6 9.8 %custom-call.23 = f32[1,128,128]{1,2,0:T(8,128)S(1)} custom-call(f32[1,128,128]{2,1,0:T(8,128)S(1)} %get-tuple-element.124), custom_call_target="InvertDiagBlocksLowerTriangular" | custom-call | tf_op jit(solution)/shard_map/jit(cholesky)/cholesky | solution.py:47
  266.8 5.8 %cholesky.194 = f32[64,64]{1,0:T(8,128)S(1)} custom-call(f32[64,64]{1,0:T(8,128)S(1)} %convolution_subtract_fusion.5), custom_call_target="Cholesky" | custom-call | tf_op jit(solution)/shard_map/jit(cholesky)/cholesky | solution.py:47
  275.6 19.9 %custom-call.26 = f32[2,128,128]{1,2,0:T(8,128)S(1)} custom-call(f32[2,128,128]{2,1,0:T(8,128)S(1)} %pad_maximum_fusion.7), custom_call_target="InvertDiagBlocksLowerTriangular" | custom-call | tf_op jit(solution)/shard_map/triangular_solve/custom-call.4 | solution.py:59
  313.5 25.6 %all_to_all.51 = f32[16,192,128]{2,1,0:T(8,128)S(1)} all-to-all(f32[16,192,128]{2,1,0:T(8,128)S(1)} %broadcast_in_dim.27), channel_id=1, replica_groups=mesh['row'=8,'col'=16] {'col'}, dimensions={0} | all-to-all | bytes 3145728 | tf_op jit(solution)/shard_map/all_to_all | solution.py:20
  (215 shorter events, 79.3 us)
Async XLA Ops:
  8.7 19.6 %copy-start.1 = (f32[2048,64]{0,1:T(8,128)S(1)}, f32[2048,64]{0,1:T(8,128)}, u32[]{:S(2)}) copy-start(f32[2048,64]{0,1:T(8,128)} %param.14) | copy-start | bytes 1572868
  8.7 19.6 %copy-start.2 = (f32[2048,64]{0,1:T(8,128)S(1)}, f32[2048,64]{0,1:T(8,128)}, u32[]{:S(2)}) copy-start(f32[2048,64]{0,1:T(8,128)} %param.13) | copy-start | bytes 1572868
  8.7 19.6 %copy-start.3 = (f32[2048,64]{0,1:T(8,128)S(1)}, f32[2048,64]{0,1:T(8,128)}, u32[]{:S(2)}) copy-start(f32[2048,64]{0,1:T(8,128)} %param.12) | copy-start | bytes 1572868
  8.8 0.8 collective-permute-start
  10.5 31.1 %all-to-all-start = ((f32[8,192,128]{2,1,0:T(8,128)}), f32[8,192,128]{2,1,0:T(8,128)}, u32[]{:S(2)}, u32[]{:S(2)}) async-start(f32[8,192,128]{2,1,0:T(8,128)} %broadcast_in_dim.20), calls=%async_computation | async-start | bytes 1572864 | tf_op jit(solution)/shard_map/all_to_all | solution.py:20
  28.4 5.8 %copy-start = (f32[2048,1024]{1,0:T(8,128)S(1)}, f32[2048,1024]{1,0:T(8,128)}, u32[]{:S(2)}) copy-start(f32[2048,1024]{1,0:T(8,128)} %param.10) | copy-start | bytes 25165828
  54.6 17.6 %all-to-all-start.2 = ((f32[16,48,128]{2,1,0:T(8,128)}), f32[16,48,128]{2,1,0:T(8,128)S(1)}, u32[]{:S(2)}, u32[]{:S(2)}) async-start(f32[16,48,128]{2,1,0:T(8,128)} %broadcast_in_dim.21), calls=%async_computation.2 | async-start | bytes 786432 | tf_op jit(solution)/shard_map/all_to_all | solution.py:20
  62.4 90.5 %reduce-scatter.2.cloned.1.call-start = ((), (), s32[]{:S(2)}) async-start(), calls=%async_computation.11 | async-start | bytes 1769472 | tf_op jit(solution)/shard_map/reduce_scatter | solution.py:89
  72.9 11.1 %all-to-all-start.3 = ((f32[8,48,128]{2,1,0:T(8,128)}), f32[8,48,128]{2,1,0:T(8,128)S(1)}, u32[]{:S(2)}, u32[]{:S(2)}) async-start(f32[8,48,128]{2,1,0:T(8,128)} %broadcast_in_dim.22), calls=%async_computation.3 | async-start | bytes 393216 | tf_op jit(solution)/shard_map/all_to_all | solution.py:20
  154.9 11.0 %all-to-all-start.4 = ((f32[8,64,128]{2,1,0:T(8,128)}), f32[8,64,128]{2,1,0:T(8,128)S(1)}, u32[]{:S(2)}, u32[]{:S(2)}) async-start(f32[8,64,128]{2,1,0:T(8,128)} %broadcast_in_dim.24), calls=%async_computation.5 | async-start | bytes 524288 | tf_op jit(solution)/shard_map/all_to_all | solution.py:20
  181.7 4.1 %copy-start.4 = (f32[1,384,128]{2,1,0:T(8,128)S(1)}, f32[1,384,128]{2,1,0:T(8,128)}, u32[]{:S(2)}) copy-start(f32[1,384,128]{2,1,0:T(8,128)} %reduce-scatter.2.cloned.1.call-done) | copy-start | bytes 589828
  181.7 21.6 %all-to-all-start.5 = ((f32[16,128,128]{2,1,0:T(8,128)}), f32[16,128,128]{2,1,0:T(8,128)S(1)}, u32[]{:S(2)}, u32[]{:S(2)}) async-start(f32[16,128,128]{2,1,0:T(8,128)} %bitcast_bitcast_fusion.1), calls=%async_computation.6 | async-start | bytes 2097152 | tf_op jit(solution)/shard_map/all_to_all | solution.py:119
  185.8 0.7 collective-permute-start.1
  204.3 15.6 %all-to-all-start.6 = ((f32[8,24,128]{2,1,0:T(8,128)}), f32[8,24,128]{2,1,0:T(8,128)S(1)}, u32[]{:S(2)}, u32[]{:S(2)}) async-start(f32[8,24,128]{2,1,0:T(8,128)} %fusion.80), calls=%async_computation.7 | async-start | bytes 196608 | tf_op jit(solution)/shard_map/all_to_all | solution.py:25
  220.6 13.2 %all-to-all-start.7 = ((f32[16,24,128]{2,1,0:T(8,128)}), f32[16,24,128]{2,1,0:T(8,128)S(1)}, u32[]{:S(2)}, u32[]{:S(2)}) async-start(f32[16,24,128]{2,1,0:T(8,128)} %broadcast_in_dim.25), calls=%async_computation.8 | async-start | bytes 393216 | tf_op jit(solution)/shard_map/all_to_all | solution.py:20
  234.4 9.3 %all-to-all-start.8 = ((f32[8,24,128]{2,1,0:T(8,128)}), f32[8,24,128]{2,1,0:T(8,128)S(1)}, u32[]{:S(2)}, u32[]{:S(2)}) async-start(f32[8,24,128]{2,1,0:T(8,128)} %broadcast_in_dim.26), calls=%async_computation.9 | async-start | bytes 196608 | tf_op jit(solution)/shard_map/all_to_all | solution.py:20
Sparse Core Ops, SparseCore 0:
  65.6 33.5 reduce-scatter.1

commit v2 on v1

v2 whole, which is shorter than its diff:
```python
import functools
import math

import jax
import jax.numpy as jnp
from jax import lax
from jax.experimental import pallas as pl
from jax.experimental.pallas import tpu as pltpu
from jax.sharding import PartitionSpec as P

NS_STEPS = 8
BOTH = ("row", "col")


def mm(left, right, dims=((1,), (0,)), precision=lax.Precision.HIGHEST):
    return lax.dot_general(
        left, right, (dims, ((), ())), precision=precision, preferred_element_type=jnp.float32
    )


def share(x, axis):
    copies = jnp.broadcast_to(x[None], (lax.axis_size(axis),) + x.shape)
    return lax.all_to_all(copies, axis, 0, 0)


def sum_everywhere(x):
    parts = x.reshape(lax.axis_size("row"), -1, x.shape[-1])
    own = lax.all_to_all(parts, "row", 0, 0).sum(0)
    own = share(own, "col").sum(0)
    return share(own, "row").reshape(x.shape)


def sides(gram, k):
    return [gram[i * k : (i + 1) * k, j * k : (j + 1) * k] for i in range(3) for j in range(i + 1)]


def dot(left, right, dims=((1,), (0,))):
    return lax.dot_general(
        left, right, (dims, ((), ())),
        precision=lax.Precision.HIGHEST, preferred_element_type=jnp.float32,
    )


NT = ((1,), (1,))
TN = ((0,), (0,))


def split(x):
    high = x.astype(jnp.bfloat16)
    return high, (x - high.astype(jnp.float32)).astype(jnp.bfloat16)


def dot3(left, right):
    def one(a, b):
        return jnp.dot(a, b, preferred_element_type=jnp.float32)

    return one(left[0], right[1]) + one(left[1], right[0]) + one(left[0], right[0])


def inverse_factor(block):
    k = block.shape[0]
    height = 8
    diag = lax.broadcasted_iota(jnp.int32, (k, k), 0) == lax.broadcasted_iota(jnp.int32, (k, k), 1)
    wide = jnp.concatenate([block, diag.astype(jnp.float32)], 1)
    strips = [wide[i : i + height] for i in range(0, k, height)]
    below = lax.broadcasted_iota(jnp.int32, (height, 1), 0)
    for j in range(k):
        at, line = divmod(j, height)
        row = strips[at][line : line + 1]
        row = row * (1.0 / row[:, j : j + 1])
        for i in range(at, k // height):
            col = strips[i][:, j : j + 1]
            if i == at:
                col = jnp.where(below > line, col, 0.0)
            strips[i] = strips[i] - col * row
    wide = jnp.concatenate(strips, 0)
    pivots = jnp.sum(jnp.where(diag, wide[:, :k], 0.0), 1, keepdims=True)
    return wide[:, k:] * (1.0 / jnp.sqrt(pivots))


def ritz_step(k, order, blocks_b, whole_a, inv_ref):
    b00, b10, b11, b20, b21, b22 = blocks_b
    t0 = inverse_factor(b00)
    l10 = dot(b10, t0, NT)
    l20 = dot(b20, t0, NT)
    t1 = inverse_factor(b11 - dot(l10, l10, NT))
    l21 = dot(b21 - dot(l20, l10, NT), t1, NT)
    t2 = inverse_factor(b22 - dot(l20, l20, NT) - dot(l21, l21, NT))
    t10 = -dot(t1, dot(l10, t0))
    t20 = -dot(t2, dot(l20, t0) + dot(l21, t10))
    t21 = -dot(t2, dot(l21, t1))
    inv_ref[...] = jnp.zeros_like(inv_ref)
    inv_ref[:k, :k] = t0
    inv_ref[k : 2 * k, :k] = t10
    inv_ref[k : 2 * k, k : 2 * k] = t1
    inv_ref[2 * k :, : 2 * k] = jnp.concatenate([t20, t21], 1)
    inv_ref[2 * k :, 2 * k :] = t2
    inverse = inv_ref[...]
    middle = dot(dot(inverse, whole_a), inverse, NT)
    middle = 0.5 * (middle + middle.T)
    size = 3 * k
    diag = lax.broadcasted_iota(jnp.int32, (size, size), 0) == lax.broadcasted_iota(
        jnp.int32, (size, size), 1
    )

    def total(x):
        return jnp.sum(jnp.sum(x, 0, keepdims=True), 1, keepdims=True)

    shift = total(jnp.where(diag, middle, 0.0)) * (1.0 / size)
    sign = middle - jnp.where(diag, shift, 0.0)
    sign = sign * (1.0 / jnp.sqrt(total(sign * sign) + 1e-06))
    for turn in range(NS_STEPS):
        parts = split(sign)
        sign = 1.5 * sign - 0.5 * dot3(parts, split(dot3(parts, parts)))
    filtered = 0.5 * (jnp.where(diag, 1.0, 0.0) - sign)[:, :k]
    coords = dot(inverse, filtered, TN) * math.sqrt(order)
    reduced = dot(filtered, dot(middle, filtered), TN)
    return coords, reduced


def put_whole(ref, blocks, k):
    b00, b10, b11, b20, b21, b22 = blocks
    ref[:k, : 2 * k] = jnp.concatenate([b00, b10.T], 1)
    ref[:k, 2 * k :] = b20.T
    ref[k : 2 * k, : 2 * k] = jnp.concatenate([b10, b11], 1)
    ref[k : 2 * k, 2 * k :] = b21.T
    ref[2 * k :, : 2 * k] = jnp.concatenate([b20, b21], 1)
    ref[2 * k :, 2 * k :] = b22
    return ref[...]


def first_kernel(k, order, packed_ref, turn_ref, basis_ref, old_ref, inv_ref, a_ref, b_ref):
    blocks = [packed_ref[i * k : (i + 1) * k] for i in range(6)]
    blocks_a = [x[:, :k] for x in blocks]
    blocks_b = [x[:, k:] for x in blocks]
    whole_a = put_whole(a_ref, blocks_a, k)
    whole_b = put_whole(b_ref, blocks_b, k)
    coords, reduced = ritz_step(k, order, blocks_b, whole_a, inv_ref)
    turn_ref[: 3 * k] = coords
    turn_ref[3 * k :] = -dot(coords, reduced)
    basis_ref[:k] = jnp.concatenate([coords[:k], jnp.zeros((k, k), jnp.float32)], 1)
    basis_ref[k:] = jnp.concatenate([coords[k:], coords[k:]], 1)
    basis = basis_ref[...]
    old_ref[: 2 * k] = dot(basis, dot(whole_a, basis), TN)
    old_ref[2 * k :] = dot(basis, dot(whole_b, basis), TN)


def second_kernel(
    k,
    order,
    old_ref,
    fresh_ref,
    basis_ref,
    own_ref,
    resid_ref,
    prod_ref,
    more_ref,
    out_ref,
    inv_ref,
    a_ref,
):
    def blocks(old, new):
        mid = new[k : 2 * k]
        return [
            old[:k, :k],
            new[:k].T,
            0.5 * (mid + mid.T),
            old[k:, :k],
            new[2 * k :],
            old[k:, k:],
        ]

    whole_a = put_whole(a_ref, blocks(old_ref[: 2 * k], fresh_ref[:, :k]), k)
    blocks_b = blocks(old_ref[2 * k :], fresh_ref[:, k:])
    coords, reduced = ritz_step(k, order, blocks_b, whole_a, inv_ref)
    basis = basis_ref[...]
    from_r = coords[k : 2 * k]
    move_p = dot(basis[:, k:], coords[2 * k :])
    move_x = dot(basis, jnp.concatenate([coords[:k], coords[2 * k :]], 0))
    vectors = jnp.concatenate([own_ref[...], resid_ref[...]], 0)
    out_ref[:k] = dot(jnp.concatenate([move_x, from_r], 0), vectors, TN)
    out_ref[2 * k :] = dot(jnp.concatenate([move_p, from_r], 0), vectors, TN)
    out_ref[k : 2 * k] = (
        dot(move_x, prod_ref[: 3 * k], TN)
        - dot(dot(move_x, reduced), prod_ref[3 * k :], TN)
        + dot(from_r, more_ref[:k], TN)
        - dot(dot(from_r, reduced), more_ref[k:], TN)
    )


def f32(*shape):
    return jax.ShapeDtypeStruct(shape, jnp.float32)


def call(kernel, name, out_shape, scratch, *args):
    return pl.pallas_call(
        kernel,
        out_shape=out_shape,
        scratch_shapes=[pltpu.VMEM(shape, jnp.float32) for shape in scratch],
        compiler_params=pltpu.CompilerParams(vmem_limit_bytes=32 * 2**20),
        name=name,
    )(*args)


def symmetric(x):
    return 0.5 * (x + x.T)


def local(a_matrix, b_matrix, x_block, r_block, p_block):
    rows, cols = lax.axis_size("row"), lax.axis_size("col")
    count = rows * cols
    k = x_block.shape[1]
    order = x_block.shape[0] * rows
    piece = order // count
    high = lax.Precision.HIGH
    to_col = [(b, (b % rows) * cols + b // rows) for b in range(count)]
    to_row = [(d, s) for s, d in to_col]

    panel = jnp.concatenate([x_block.T, r_block.T, p_block.T], 0)
    start = lax.axis_index("col") * piece
    own_row = lax.dynamic_slice_in_dim(panel, start, piece, 1)
    own_col = lax.ppermute(own_row, BOTH, to_col)

    prods = jnp.concatenate(
        [mm(panel, a_matrix, precision=high), mm(panel, b_matrix, precision=high)], 0
    )
    prods_by_piece = prods.reshape(6 * k, rows, piece).transpose(1, 0, 2)
    prod_col = lax.psum_scatter(prods_by_piece, "row", scatter_dimension=0)
    prod_row = lax.ppermute(prod_col, BOTH, to_row)
    matched = share(own_col, "row").transpose(1, 0, 2).reshape(3 * k, -1)
    grams = mm(prods, matched, ((1,), (1,)), high)
    packed = jnp.concatenate(
        [
            jnp.concatenate([ga, gb], 1)
            for ga, gb in zip(
                sides(symmetric(grams[: 3 * k]), k), sides(symmetric(grams[3 * k :]), k)
            )
        ],
        0,
    )
    packed = sum_everywhere(packed)
    turn, basis, old = call(
        functools.partial(first_kernel, k, order),
        "ritz_first",
        (f32(6 * k, k), f32(3 * k, 2 * k), f32(4 * k, 2 * k)),
        [(3 * k, 3 * k)] * 3,
        packed,
    )

    resid_col = mm(turn, prod_col, TN)
    resid_row = mm(turn, prod_row, TN)
    resid = share(resid_col, "row").transpose(1, 0, 2).reshape(k, -1)
    parts = jnp.concatenate(
        [mm(resid, a_matrix, NT, high), mm(resid, b_matrix, NT, high)], 0
    )
    parts = parts.reshape(2 * k, cols, piece).transpose(1, 0, 2)
    more_row = lax.all_to_all(parts, "col", 0, 0).sum(0)

    kept = mm(basis, own_row, TN)
    tests = jnp.concatenate([kept[:k], resid_row, kept[k:]], 0)
    fresh = sum_everywhere(mm(tests, more_row, NT))
    outs = call(
        functools.partial(second_kernel, k, order),
        "ritz_second",
        f32(3 * k, piece),
        [(3 * k, 3 * k)] * 2,
        old,
        fresh,
        basis,
        own_row,
        resid_row,
        prod_row,
        more_row,
    )
    outs = share(outs, "col").transpose(1, 0, 2).reshape(3 * k, -1)
    return (outs[:k].T, outs[k : 2 * k].T, outs[2 * k :].T)


def solution(mesh):
    return jax.shard_map(
        local,
        mesh=mesh,
        in_specs=(P("row", "col"), P("row", "col"), P("row", None), P("row", None), P("row", None)),
        out_specs=(P("row", None), P("row", None), P("row", None)),
        check_vma=False,
    )
```

time: 356 us -> 258 us (0.72); the launches traced: 349 us -> 257 us
  other arithmetic: 105 us -> 4.25 us
  blocking collectives: 34.8 us -> 131 us
  starting transfers between devices: 56.3 us -> 5.16 us
  Pallas kernels: 0 us -> 50.7 us
  waiting for transfers between devices: 62.5 us -> 16.2 us
  matrix products: 58.2 us -> 27.5 us
  between operations: 20.9 us -> 14.4 us
  local copies, waits for them, and re-layouts: 11 us -> 7.21 us
    another operation x26 -> x0, other arithmetic: 97.7 us -> none  [the longest x14 57.4 us: ritz_step(): lower = jnp.linalg.cholesky(gram_b)]
    all_to_all x1 -> x7, blocking collectives: 25.6 us -> 106 us  [share(): return lax.all_to_all(copies, axis, 0, 0)]
    all_to_all x7 -> x0, starting transfers between devices: 51 us -> none  [the longest x6 41.2 us: share(): return lax.all_to_all(copies, axis, 0, 0)]
    pallas_call x0 -> x2, Pallas kernels: none -> 50.7 us  [call(): pl.pallas_call(kernel, out_shape=out_shape, scratch_shapes=[pltpu.VMEM(sh...]
    all_to_all x7 -> x0, waiting for transfers between devices: 45.9 us -> none  [the longest x6 40.1 us: share(): return lax.all_to_all(copies, axis, 0, 0)]
    dot_general x59 -> x9, matrix products: 52.2 us -> 27.5 us  [mm(): lax.dot_general(left, right, (dims, ((), ())), precision=precision, prefe...]
    all_to_all x1 -> x2, blocking collectives: 9.23 us -> 25.4 us  [sum_everywhere(): own = lax.all_to_all(parts, 'row', 0, 0).sum(0)]
    another operation x22 -> x0, matrix products: 6.01 us -> none  [the longest x6 2.2 us: ritz_step(): lax.linalg.triangular_solve(lower, gram_a, left_side=True, lower=True)]
  transfers between devices with their start and end apart: 11 -> 4, of which waited for: 8 -> 1; matrix products, arithmetic and copies ran while one was open for 23% -> 7% of each run, Pallas kernels for 0% -> 10%
where the time goes in v2:
time: 258 us; the launch traced here: 257 us
  blocking collectives  131 us (51%)
  Pallas kernels  50.7 us (20%)
  matrix products  27.5 us (11%)
  waiting for transfers between devices  16.2 us (6%)
  between operations  14.4 us (6%)
  local copies, waits for them, and re-layouts  7.21 us (3%)
  starting transfers between devices  5.16 us (2%)
  other arithmetic  4.25 us (2%)
    all_to_all x7, blocking collectives, share(): return lax.all_to_all(copies, axis, 0, 0)  106 us
    pallas_call x2, Pallas kernels, call(): pl.pallas_call(kernel, out_shape=out_shape, scratch_shapes=[pltpu.VMEM(sh...  50.7 us
    dot_general x9, matrix products, mm(): lax.dot_general(left, right, (dims, ((), ())), precision=precision, prefe...  27.5 us
    all_to_all x2, blocking collectives, sum_everywhere(): own = lax.all_to_all(parts, 'row', 0, 0).sum(0)  25.4 us
    all_to_all x1, waiting for transfers between devices, local(): more_row = lax.all_to_all(parts, 'col', 0, 0).sum(0)  16.2 us
  transfers between devices with their start and end apart: 4, of which 1 were waited for; matrix products, arithmetic and copies ran while one was open for 7% of the time, Pallas kernels for 10%

profile of v2, /device:TPU:0, one launch (start us, length us, event | category | flops | bytes accessed | tf_op | source)
XLA Modules:
  0.0 257.0 jit_solution(9198046454932599407)
XLA Ops:
  7.2 1.6 pad_maximum_fusion
  9.6 5.8 %fusion.15 = f32[192,1024]{1,0:T(8,128)S(1)} fusion(f32[2048,1024]{1,0:T(8,128)} %param.6, f32[64,2048]{1,0:T(8,128)S(1)} %bitcast.92, f32[64,2048]{1,0:T(8,128)S(1)} %bitcast.95, f32[64,2048]{1,0:T(8,128)S(1)} %bitcast.98), kind=kOutput, calls=%fused_computation.35 | convolution fusion | flops 2416705536 | bytes 10747904 | tf_op jit(solution)/shard_map/dot_general | solution.py:16
  15.4 3.6 %fusion.16 = f32[192,1024]{1,0:T(8,128)S(1)} fusion(f32[2048,1024]{1,0:T(8,128)S(1)} %copy-done, f32[64,2048]{1,0:T(8,128)S(1)} %bitcast.93, f32[64,2048]{1,0:T(8,128)S(1)} %bitcast.96, f32[64,2048]{1,0:T(8,128)S(1)} %bitcast.99), kind=kOutput, calls=%fused_computation.36 | convolution fusion | flops 2416705536 | bytes 10747904 | tf_op jit(solution)/shard_map/dot_general | solution.py:16
  19.0 1.3 pad_maximum_fusion.1
  20.3 1.9 copy.43
  22.2 1.6 copy.44
  23.9 26.8 %all_to_all.50 = f32[8,192,128]{2,1,0:T(8,128)S(1)} all-to-all(f32[8,192,128]{2,1,0:T(8,128)S(1)} %broadcast_in_dim.14), channel_id=1, replica_groups=mesh['row'=8,'col'=16] {'row'}, dimensions={0} | all-to-all | bytes 1572864 | tf_op jit(solution)/shard_map/all_to_all | solution.py:23
  50.7 0.9 fusion
  52.6 9.8 %all_to_all.51 = f32[8,48,128]{2,1,0:T(8,128)S(1)} all-to-all(f32[8,48,128]{2,1,0:T(8,128)S(1)} %bitcast.100), channel_id=1, replica_groups=mesh['row'=8,'col'=16] {'row'}, dimensions={0} | all-to-all | bytes 393216 | tf_op jit(solution)/shard_map/all_to_all | solution.py:28
  62.4 13.4 %all_to_all.52 = f32[16,48,128]{2,1,0:T(8,128)S(1)} all-to-all(f32[16,48,128]{2,1,0:T(8,128)S(1)} %broadcast_in_dim.15), channel_id=1, replica_groups=mesh['row'=8,'col'=16] {'col'}, dimensions={0} | all-to-all | bytes 786432 | tf_op jit(solution)/shard_map/all_to_all | solution.py:23
  75.9 9.2 %all_to_all.53 = f32[8,48,128]{2,1,0:T(8,128)S(1)} all-to-all(f32[8,48,128]{2,1,0:T(8,128)S(1)} %broadcast_in_dim.16), channel_id=1, replica_groups=mesh['row'=8,'col'=16] {'row'}, dimensions={0} | all-to-all | bytes 393216 | tf_op jit(solution)/shard_map/all_to_all | solution.py:23
  85.1 25.5 %ritz_first.1 = (f32[384,64]{1,0:T(8,128)S(1)}, f32[192,128]{1,0:T(8,128)S(1)}, f32[256,128]{1,0:T(8,128)S(1)}) custom-call(f32[384,128]{1,0:T(8,128)S(1)} %bitcast.86), custom_call_target="tpu_custom_call" | custom-call | tf_op jit(solution)/shard_map/ritz_first/pallas_call | solution.py:196
  110.6 1.4 fusion.13
  112.1 9.9 %all_to_all.54 = f32[8,64,128]{2,1,0:T(8,128)S(1)} all-to-all(f32[8,64,128]{2,1,0:T(8,128)S(1)} %broadcast_in_dim.17), channel_id=1, replica_groups=mesh['row'=8,'col'=16] {'row'}, dimensions={0} | all-to-all | bytes 524288 | tf_op jit(solution)/shard_map/all_to_all | solution.py:23
  122.0 7.3 %fusion.3 = f32[64,2048]{1,0:T(8,128)S(1)} fusion(f32[2048,1024]{1,0:T(8,128)} %param.6, f32[8,64,128]{2,1,0:T(8,128)S(1)} %all_to_all.54), kind=kOutput, calls=%fused_computation.13 | convolution fusion | flops 805306368 | bytes 9175040 | tf_op jit(solution)/shard_map/dot_general | solution.py:16
  129.3 7.3 %fusion.5 = f32[64,2048]{1,0:T(8,128)S(1)} fusion(f32[2048,1024]{1,0:T(8,128)} %param.5, f32[8,64,128]{2,1,0:T(8,128)S(1)} %all_to_all.54), kind=kOutput, calls=%fused_computation.15 | convolution fusion | flops 805306368 | bytes 9175040 | tf_op jit(solution)/shard_map/dot_general | solution.py:16
  136.6 1.1 bitcast_bitcast_fusion
  137.7 3.8 %all-to-all-start.5 = ((f32[16,128,128]{2,1,0:T(8,128)}), f32[16,128,128]{2,1,0:T(8,128)S(1)}, u32[]{:S(2)}, u32[]{:S(2)}) async-start(f32[16,128,128]{2,1,0:T(8,128)} %bitcast_bitcast_fusion), calls=%async_computation.6 | async-start | bytes 2097152 | tf_op jit(solution)/shard_map/all_to_all | solution.py:257
  143.2 16.2 %all-to-all-done.5 = f32[16,128,128]{2,1,0:T(8,128)S(1)} async-done(((f32[16,128,128]{2,1,0:T(8,128)}), f32[16,128,128]{2,1,0:T(8,128)S(1)}, u32[]{:S(2)}, u32[]{:S(2)}) %all-to-all-start.5) | async-done | bytes 1048608 | tf_op jit(solution)/shard_map/all_to_all | solution.py:257
  159.7 15.6 %all_to_all.55 = f32[8,24,128]{2,1,0:T(8,128)S(1)} all-to-all(f32[8,24,128]{2,1,0:T(8,128)S(1)} %fusion.11), channel_id=1, replica_groups=mesh['row'=8,'col'=16] {'row'}, dimensions={0} | all-to-all | bytes 196608 | tf_op jit(solution)/shard_map/all_to_all | solution.py:28
  175.3 13.0 %all_to_all.56 = f32[16,24,128]{2,1,0:T(8,128)S(1)} all-to-all(f32[16,24,128]{2,1,0:T(8,128)S(1)} %broadcast_in_dim.18), channel_id=1, replica_groups=mesh['row'=8,'col'=16] {'col'}, dimensions={0} | all-to-all | bytes 393216 | tf_op jit(solution)/shard_map/all_to_all | solution.py:23
  188.3 8.2 %all_to_all.57 = f32[8,24,128]{2,1,0:T(8,128)S(1)} all-to-all(f32[8,24,128]{2,1,0:T(8,128)S(1)} %broadcast_in_dim.19), channel_id=1, replica_groups=mesh['row'=8,'col'=16] {'row'}, dimensions={0} | all-to-all | bytes 196608 | tf_op jit(solution)/shard_map/all_to_all | solution.py:23
  196.5 25.2 %ritz_second.1 = f32[192,128]{1,0:T(8,128)S(1)} custom-call(f32[256,128]{1,0:T(8,128)S(1)} %get-tuple-element.6.old_ref, f32[192,128]{1,0:T(8,128)S(1)} %bitcast.87, f32[192,128]{1,0:T(8,128)S(1)} %get-tuple-element.7.basis_ref, f32[192,128]{1,0:T(8,128)S(1)} %constant_dynamic-slice_fusion.own_ref, f32[64,128]{1,0:T(8,128)S(1)} %fusion.22.resid_ref, ...), custom_call_target="tpu_custom_call" | custom-call | tf_op jit(solution)/shard_map/ritz_second/pallas_call | solution.py:196
  221.9 25.6 %all_to_all.58 = f32[16,192,128]{2,1,0:T(8,128)S(1)} all-to-all(f32[16,192,128]{2,1,0:T(8,128)S(1)} %broadcast_in_dim.20), channel_id=1, replica_groups=mesh['row'=8,'col'=16] {'col'}, dimensions={0} | all-to-all | bytes 3145728 | tf_op jit(solution)/shard_map/all_to_all | solution.py:23
  (52 shorter events, 6.6 us)
Async XLA Ops:
  7.2 103.4 %reduce-scatter.2.cloned.1.call-start = ((), (), s32[]{:S(2)}) async-start(), calls=%async_computation.11 | async-start | bytes 1769472 | tf_op jit(solution)/shard_map/reduce_scatter | solution.py:228
  7.2 2.3 copy-start.1
  7.2 2.3 copy-start.2
  7.2 2.3 copy-start.3
  8.9 15.0 %collective-permute-start = (f32[192,128]{1,0:T(8,128)S(1)}, f32[192,128]{1,0:T(8,128)S(1)}, u32[]{:S(2)}, u32[]{:S(2)}) collective-permute-start(f32[192,128]{1,0:T(8,128)S(1)} %constant_dynamic-slice_fusion.own_ref), channel_id=1, source_target_pairs={{0,0},{1,16},{2,32},{3,48},{4,64},{5,80},{6,96},{7,112},{8,1},{9,1... | collective-permute-start | bytes 294920 | tf_op jit(solution)/shard_map/ppermute | solution.py:222
  9.6 5.8 %copy-start = (f32[2048,1024]{1,0:T(8,128)S(1)}, f32[2048,1024]{1,0:T(8,128)}, u32[]{:S(2)}) copy-start(f32[2048,1024]{1,0:T(8,128)} %param.5) | copy-start | bytes 25165828
  137.7 4.2 %copy-start.4 = (f32[1,384,128]{2,1,0:T(8,128)S(1)}, f32[1,384,128]{2,1,0:T(8,128)}, u32[]{:S(2)}) copy-start(f32[1,384,128]{2,1,0:T(8,128)} %reduce-scatter.2.cloned.1.call-done) | copy-start | bytes 589828
  137.7 21.6 %all-to-all-start.5 = ((f32[16,128,128]{2,1,0:T(8,128)}), f32[16,128,128]{2,1,0:T(8,128)S(1)}, u32[]{:S(2)}, u32[]{:S(2)}) async-start(f32[16,128,128]{2,1,0:T(8,128)} %bitcast_bitcast_fusion), calls=%async_computation.6 | async-start | bytes 2097152 | tf_op jit(solution)/shard_map/all_to_all | solution.py:257
  142.0 0.7 collective-permute-start.1
Sparse Core Ops, SparseCore 0:
  24.0 43.6 reduce-scatter.1

commit v3 on v2

--- a/solution.py
+++ b/solution.py
@@ -30,10 +30,6 @@
     return share(own, "row").reshape(x.shape)
 
 
-def sides(gram, k):
-    return [gram[i * k : (i + 1) * k, j * k : (j + 1) * k] for i in range(3) for j in range(i + 1)]
-
-
 def dot(left, right, dims=((1,), (0,))):
     return lax.dot_general(
         left, right, (dims, ((), ())),
@@ -62,20 +58,49 @@
     height = 8
     diag = lax.broadcasted_iota(jnp.int32, (k, k), 0) == lax.broadcasted_iota(jnp.int32, (k, k), 1)
     wide = jnp.concatenate([block, diag.astype(jnp.float32)], 1)
+    full = (height, 2 * k)
     strips = [wide[i : i + height] for i in range(0, k, height)]
-    below = lax.broadcasted_iota(jnp.int32, (height, 1), 0)
-    for j in range(k):
-        at, line = divmod(j, height)
-        row = strips[at][line : line + 1]
-        row = row * (1.0 / row[:, j : j + 1])
-        for i in range(at, k // height):
-            col = strips[i][:, j : j + 1]
-            if i == at:
-                col = jnp.where(below > line, col, 0.0)
-            strips[i] = strips[i] - col * row
-    wide = jnp.concatenate(strips, 0)
-    pivots = jnp.sum(jnp.where(diag, wide[:, :k], 0.0), 1, keepdims=True)
-    return wide[:, k:] * (1.0 / jnp.sqrt(pivots))
+    line = lax.broadcasted_iota(jnp.int32, full, 0)
+    done = []
+    for at in range(k // height):
+        first = at * height
+        rows = [jnp.broadcast_to(strips[at][i : i + 1], full) for i in range(height)]
+        elem = [
+            [jnp.broadcast_to(rows[m][:, first + i : first + i + 1], full) for i in range(m + 1)]
+            for m in range(height)
+        ]
+        later = range(at + 1, k // height)
+        cols = {
+            t: [
+                jnp.broadcast_to(strips[t][:, first + i : first + i + 1], full)
+                for i in range(height)
+            ]
+            for t in later
+        }
+        low = [[None] * height for _ in range(height)]
+        inv = [None] * height
+        for i in range(height):
+            inv[i] = 1.0 / elem[i][i]
+            for m in range(i + 1, height):
+                low[m][i] = elem[m][i] * inv[i]
+                for n in range(i + 1, m + 1):
+                    elem[m][n] = elem[m][n] - low[m][i] * elem[n][i]
+                rows[m] = rows[m] - low[m][i] * rows[i]
+        out = rows[0] * (1.0 / jnp.sqrt(elem[0][0]))
+        for m in range(1, height):
+            out = jnp.where(line == m, rows[m] * (1.0 / jnp.sqrt(elem[m][m])), out)
+        done.append(out)
+        if not later:
+            break
+        solved = [None] * height
+        for m in reversed(range(height)):
+            solved[m] = rows[m] * inv[m]
+            for i in range(m + 1, height):
+                solved[m] = solved[m] - low[i][m] * solved[i]
+        for t in later:
+            for m in range(height):
+                strips[t] = strips[t] - cols[t][m] * solved[m]
+    return jnp.concatenate(done, 0)[:, k:]
 
 
 def ritz_step(k, order, blocks_b, whole_a, inv_ref):
@@ -180,11 +205,12 @@
     vectors = jnp.concatenate([own_ref[...], resid_ref[...]], 0)
     out_ref[:k] = dot(jnp.concatenate([move_x, from_r], 0), vectors, TN)
     out_ref[2 * k :] = dot(jnp.concatenate([move_p, from_r], 0), vectors, TN)
+    more = more_ref[...].T
     out_ref[k : 2 * k] = (
         dot(move_x, prod_ref[: 3 * k], TN)
         - dot(dot(move_x, reduced), prod_ref[3 * k :], TN)
-        + dot(from_r, more_ref[:k], TN)
-        - dot(dot(from_r, reduced), more_ref[k:], TN)
+        + dot(from_r, more[:k], TN)
+        - dot(dot(from_r, reduced), more[k:], TN)
     )
 
 
@@ -202,8 +228,113 @@
     )(*args)
 
 
-def symmetric(x):
-    return 0.5 * (x + x.T)
+def three(left, right, dims):
+    def one(a, b):
+        return lax.dot_general(a, b, (dims, ((), ())), preferred_element_type=jnp.float32)
+
+    return one(left[0], right[1]) + one(left[1], right[0]) + one(left[0], right[0])
+
+
+def products_kernel(x_ref, r_ref, p_ref, a_ref, b_ref, out_ref, panel_ref):
+    k = x_ref.shape[0]
+    wide = 3 * k
+
+    @pl.when(pl.program_id(0) == 0)
+    def _():
+        for i, ref in enumerate((x_ref, r_ref, p_ref)):
+            high, low = split(ref[...])
+            panel_ref[i * k : (i + 1) * k] = high
+            panel_ref[wide + i * k : wide + (i + 1) * k] = low
+
+    def one(a, b):
+        return jnp.dot(a, b, preferred_element_type=jnp.float32)
+
+    for at, ref in ((0, a_ref), (wide, b_ref)):
+        high, low = split(ref[...])
+        both = one(panel_ref[...], high)
+        prod = both[:wide] + both[wide:] + one(panel_ref[:wide], low)
+        for i in range(out_ref.shape[0]):
+            lanes = out_ref.shape[2]
+            out_ref[i, at : at + wide] = prod[:, i * lanes : (i + 1) * lanes]
+
+
+def gram_kernel(prods_ref, panel_ref, out_ref):
+    pieces, wide, lanes = panel_ref.shape
+    k = wide // 3
+    gram = jnp.zeros((2 * wide, wide), jnp.float32)
+    for i in range(0, pieces, 2):
+        left = jnp.concatenate([prods_ref[i], prods_ref[i + 1]], 1)
+        right = jnp.concatenate([panel_ref[i], panel_ref[i + 1]], 1)
+        gram = gram + three(split(left), split(right), NT)
+    at = 0
+    for i in range(3):
+        for j in range(i + 1):
+            pair = []
+            for base in (0, wide):
+                block = gram[base + i * k : base + (i + 1) * k, j * k : (j + 1) * k]
+                other = gram[base + j * k : base + (j + 1) * k, i * k : (i + 1) * k]
+                pair.append(0.5 * (block + other.T))
+            out_ref[at : at + k] = jnp.concatenate(pair, 1)
+            at += k
+
+
+def residual_kernel(resid_ref, a_ref, b_ref, out_ref, first_ref, second_ref):
+    pieces, k, lanes = resid_ref.shape
+
+    @pl.when(pl.program_id(0) == 0)
+    def _():
+        for i in range(pieces):
+            block = resid_ref[i].T
+            high = block.astype(jnp.bfloat16).astype(jnp.float32)
+            low = block - high
+            rows = pl.ds(i * lanes, lanes)
+            first_ref[rows, :] = jnp.concatenate([high, low], 1).astype(jnp.bfloat16)
+            second_ref[rows, :] = jnp.concatenate([low, high], 1).astype(jnp.bfloat16)
+
+    sums = []
+    for ref, parts_ref in ((a_ref, first_ref), (b_ref, second_ref)):
+        high, low = split(ref[...])
+        part = jnp.dot(high, parts_ref[...], preferred_element_type=jnp.float32) + jnp.dot(
+            low, parts_ref[...], preferred_element_type=jnp.float32
+        )
+        sums.append(part + pltpu.roll(part, k, 1))
+    lane = lax.broadcasted_iota(jnp.int32, sums[0].shape, 1)
+    out_ref[...] = jnp.where(lane < k, sums[0], sums[1])
+
+
+def products(x, r, p, a, b, pieces):
+    k, rows = x.shape
+    lanes = a.shape[1] // pieces
+    each = 2
+    block = pl.BlockSpec((k, rows), lambda i: (0, 0))
+    tile = pl.BlockSpec((rows, each * lanes), lambda i: (0, i))
+    return pl.pallas_call(
+        products_kernel,
+        grid=(pieces // each,),
+        in_specs=[block, block, block, tile, tile],
+        out_specs=pl.BlockSpec((each, 6 * k, lanes), lambda i: (i, 0, 0)),
+        out_shape=f32(pieces, 6 * k, lanes),
+        scratch_shapes=[pltpu.VMEM((6 * k, rows), jnp.bfloat16)],
+        compiler_params=pltpu.CompilerParams(vmem_limit_bytes=48 * 2**20),
+        name="products",
+    )(x, r, p, a, b)
+
+
+def residual_products(resid, a, b):
+    pieces, k, lanes = resid.shape
+    rows, cols = a.shape
+    height = 512
+    tile = pl.BlockSpec((height, cols), lambda i: (i, 0))
+    return pl.pallas_call(
+        residual_kernel,
+        grid=(rows // height,),
+        in_specs=[pl.BlockSpec(resid.shape, lambda i: (0, 0, 0)), tile, tile],
+        out_specs=pl.BlockSpec((height, 2 * k), lambda i: (i, 0)),
+        out_shape=f32(rows, 2 * k),
+        scratch_shapes=[pltpu.VMEM((cols, 2 * k), jnp.bfloat16)] * 2,
+        compiler_params=pltpu.CompilerParams(vmem_limit_bytes=48 * 2**20),
+        name="residual_products",
+    )(resid, a, b)
 
 
 def local(a_matrix, b_matrix, x_block, r_block, p_block):
@@ -212,33 +343,22 @@
     k = x_block.shape[1]
     order = x_block.shape[0] * rows
     piece = order // count
-    high = lax.Precision.HIGH
     to_col = [(b, (b % rows) * cols + b // rows) for b in range(count)]
     to_row = [(d, s) for s, d in to_col]
 
-    panel = jnp.concatenate([x_block.T, r_block.T, p_block.T], 0)
+    panel = [x_block.T, r_block.T, p_block.T]
     start = lax.axis_index("col") * piece
-    own_row = lax.dynamic_slice_in_dim(panel, start, piece, 1)
+    own_row = jnp.concatenate(
+        [lax.dynamic_slice_in_dim(x, start, piece, 1) for x in panel], 0
+    )
     own_col = lax.ppermute(own_row, BOTH, to_col)
 
-    prods = jnp.concatenate(
-        [mm(panel, a_matrix, precision=high), mm(panel, b_matrix, precision=high)], 0
-    )
-    prods_by_piece = prods.reshape(6 * k, rows, piece).transpose(1, 0, 2)
-    prod_col = lax.psum_scatter(prods_by_piece, "row", scatter_dimension=0)
+    prods = products(*panel, a_matrix, b_matrix, rows)
+    prod_col = lax.psum_scatter(prods, "row", scatter_dimension=0)
     prod_row = lax.ppermute(prod_col, BOTH, to_row)
-    matched = share(own_col, "row").transpose(1, 0, 2).reshape(3 * k, -1)
-    grams = mm(prods, matched, ((1,), (1,)), high)
-    packed = jnp.concatenate(
-        [
-            jnp.concatenate([ga, gb], 1)
-            for ga, gb in zip(
-                sides(symmetric(grams[: 3 * k]), k), sides(symmetric(grams[3 * k :]), k)
-            )
-        ],
-        0,
-    )
-    packed = sum_everywhere(packed)
+    matched = share(own_col, "row")
+    packed = sum_everywhere(call(gram_kernel, "gram", f32(6 * k, 2 * k), [], prods, matched))
+    packed, prod_row = lax.optimization_barrier((packed, prod_row))
     turn, basis, old = call(
         functools.partial(first_kernel, k, order),
         "ritz_first",
@@ -249,16 +369,13 @@
 
     resid_col = mm(turn, prod_col, TN)
     resid_row = mm(turn, prod_row, TN)
-    resid = share(resid_col, "row").transpose(1, 0, 2).reshape(k, -1)
-    parts = jnp.concatenate(
-        [mm(resid, a_matrix, NT, high), mm(resid, b_matrix, NT, high)], 0
-    )
-    parts = parts.reshape(2 * k, cols, piece).transpose(1, 0, 2)
+    parts = residual_products(share(resid_col, "row"), a_matrix, b_matrix)
+    parts = parts.reshape(cols, piece, 2 * k)
     more_row = lax.all_to_all(parts, "col", 0, 0).sum(0)
 
     kept = mm(basis, own_row, TN)
     tests = jnp.concatenate([kept[:k], resid_row, kept[k:]], 0)
-    fresh = sum_everywhere(mm(tests, more_row, NT))
+    fresh = sum_everywhere(mm(tests, more_row))
     outs = call(
         functools.partial(second_kernel, k, order),
         "ritz_second",

time: 258 us -> 243 us (0.942)
  matrix products: 27.5 us -> 2.54 us
  blocking collectives: 131 us -> 116 us
  starting transfers between devices: 5.16 us -> 19.5 us
  waiting for transfers between devices: 16.2 us -> 24.8 us
  Pallas kernels: 50.7 us -> 57.3 us
  other arithmetic: 4.25 us -> 0.15 us
    dot_general x9 -> x4, matrix products: 27.5 us -> 2.54 us  [mm(): lax.dot_general(left, right, (dims, ((), ())), precision=precision, prefe...]
    pallas_call x0 -> x2, Pallas kernels: none -> 20 us  [the longest x1 10.1 us: products(): pl.pallas_call(products_kernel, grid=(pieces // each,), in_specs=[block,...]
    pallas_call x2 -> x3, Pallas kernels: 50.7 us -> 37.3 us  [call(): pl.pallas_call(kernel, out_shape=out_shape, scratch_shapes=[pltpu.VMEM(sh...]
    all_to_all x0 -> x1, waiting for transfers between devices: none -> 8.5 us  [share(): return lax.all_to_all(copies, axis, 0, 0)]
    all_to_all x0 -> x1, starting transfers between devices: none -> 7.97 us  [share(): return lax.all_to_all(copies, axis, 0, 0)]
    all_to_all x2, blocking collectives: 25.4 us -> 17.4 us  [sum_everywhere(): own = lax.all_to_all(parts, 'row', 0, 0).sum(0)]
    all_to_all x7 -> x6, blocking collectives: 106 us -> 98.2 us  [share(): return lax.all_to_all(copies, axis, 0, 0)]
    all_to_all x1, starting transfers between devices: 3.78 us -> 9.21 us  [local(): more_row = lax.all_to_all(parts, 'col', 0, 0).sum(0)]
  transfers between devices with their start and end apart: 4 -> 5, of which waited for: 1 -> 2; matrix products, arithmetic and copies ran while one was open for 7% -> 1% of each run, Pallas kernels for 10% -> 1%
where the time goes in v3:
time: 243 us; the launch traced here: 242 us
  blocking collectives  116 us (48%)
  Pallas kernels  57.3 us (24%)
  waiting for transfers between devices  24.8 us (10%)
  starting transfers between devices  19.5 us (8%)
  between operations  14.2 us (6%)
  local copies, waits for them, and re-layouts  8.38 us (3%)
  matrix products  2.54 us (1%)
    all_to_all x6, blocking collectives, share(): return lax.all_to_all(copies, axis, 0, 0)  98.2 us
    pallas_call x3, Pallas kernels, call(): pl.pallas_call(kernel, out_shape=out_shape, scratch_shapes=[pltpu.VMEM(sh...  37.3 us
    all_to_all x2, blocking collectives, sum_everywhere(): own = lax.all_to_all(parts, 'row', 0, 0).sum(0)  17.4 us
    all_to_all x1, waiting for transfers between devices, local(): more_row = lax.all_to_all(parts, 'col', 0, 0).sum(0)  16.3 us
    pallas_call x1, Pallas kernels, products(): pl.pallas_call(products_kernel, grid=(pieces // each,), in_specs=[block,...  10.1 us
    pallas_call x1, Pallas kernels, residual_products(): pl.pallas_call(residual_kernel, grid=(rows // height,), in_specs=[pl.Bloc...  9.87 us
    all_to_all x1, starting transfers between devices, local(): more_row = lax.all_to_all(parts, 'col', 0, 0).sum(0)  9.21 us
    all_to_all x1, waiting for transfers between devices, share(): return lax.all_to_all(copies, axis, 0, 0)  8.5 us
  transfers between devices with their start and end apart: 5, of which 2 were waited for; matrix products, arithmetic and copies ran while one was open for 1% of the time, Pallas kernels for 1%

profile of v3, /device:TPU:0, one launch (start us, length us, event | category | flops | bytes accessed | tf_op | source)
XLA Modules:
  0.0 242.5 jit_solution(2009154457713652275)
XLA Ops:
  7.2 1.0 copy-done
  8.3 1.0 copy-done.1
  9.3 1.0 copy-done.2
  10.3 10.1 %products.1.prods_ref = f32[8,384,128]{2,1,0:T(8,128)} custom-call(f32[64,2048]{1,0:T(8,128)S(1)} %bitcast.52, f32[64,2048]{1,0:T(8,128)S(1)} %bitcast.53, f32[64,2048]{1,0:T(8,128)S(1)} %bitcast.54, f32[2048,1024]{1,0:T(8,128)} %a_ref.3, f32[2048,1024]{1,0:T(8,128)} %b_ref.3), custom_call_target="tpu_custom_call" | custom-call | tf_op jit(solution)/shard_map/products/pallas_call | solution.py:311
  22.8 33.4 %all_to_all.50.panel_ref = f32[8,192,128]{2,1,0:T(8,128)S(1)} all-to-all(f32[8,192,128]{2,1,0:T(8,128)S(1)} %broadcast_in_dim.14), channel_id=1, replica_groups=mesh['row'=8,'col'=16] {'row'}, dimensions={0} | all-to-all | bytes 1572864 | tf_op jit(solution)/shard_map/all_to_all | solution.py:23
  56.2 2.7 %gram.1 = f32[384,128]{1,0:T(8,128)S(1)} custom-call(f32[8,384,128]{2,1,0:T(8,128)} %products.1.prods_ref, f32[8,192,128]{2,1,0:T(8,128)S(1)} %all_to_all.50.panel_ref), custom_call_target="tpu_custom_call" | custom-call | tf_op jit(solution)/shard_map/gram/pallas_call | solution.py:222
  59.0 9.2 %all_to_all.51 = f32[8,48,128]{2,1,0:T(8,128)S(1)} all-to-all(f32[8,48,128]{2,1,0:T(8,128)S(1)} %bitcast.50), channel_id=1, replica_groups=mesh['row'=8,'col'=16] {'row'}, dimensions={0} | all-to-all | bytes 393216 | tf_op jit(solution)/shard_map/all_to_all | solution.py:28
  69.0 8.0 %all-to-all-start.2 = ((f32[16,48,128]{2,1,0:T(8,128)}), f32[16,48,128]{2,1,0:T(8,128)S(1)}, u32[]{:S(2)}, u32[]{:S(2)}) async-start(f32[16,48,128]{2,1,0:T(8,128)} %broadcast_in_dim.15), calls=%async_computation.2 | async-start | bytes 786432 | tf_op jit(solution)/shard_map/all_to_all | solution.py:23
  77.0 1.6 collective-permute-start.1
  78.6 8.5 %all-to-all-done.2 = f32[16,48,128]{2,1,0:T(8,128)S(1)} async-done(((f32[16,48,128]{2,1,0:T(8,128)}), f32[16,48,128]{2,1,0:T(8,128)S(1)}, u32[]{:S(2)}, u32[]{:S(2)}) %all-to-all-start.2) | async-done | bytes 393248 | tf_op jit(solution)/shard_map/all_to_all | solution.py:23
  87.1 9.2 %all_to_all.52 = f32[8,48,128]{2,1,0:T(8,128)S(1)} all-to-all(f32[8,48,128]{2,1,0:T(8,128)S(1)} %broadcast_in_dim.16), channel_id=1, replica_groups=mesh['row'=8,'col'=16] {'row'}, dimensions={0} | all-to-all | bytes 393216 | tf_op jit(solution)/shard_map/all_to_all | solution.py:23
  96.4 17.3 %ritz_first.1 = (f32[384,64]{1,0:T(8,128)S(1)}, f32[192,128]{1,0:T(8,128)S(1)}, f32[256,128]{1,0:T(8,128)S(1)}) custom-call(f32[384,128]{1,0:T(8,128)S(1)} %bitcast.51), custom_call_target="tpu_custom_call" | custom-call | tf_op jit(solution)/shard_map/ritz_first/pallas_call | solution.py:222
  113.7 1.4 fusion.2
  115.1 10.6 %all_to_all.53.resid_ref = f32[8,64,128]{2,1,0:T(8,128)S(1)} all-to-all(f32[8,64,128]{2,1,0:T(8,128)S(1)} %broadcast_in_dim.17), channel_id=1, replica_groups=mesh['row'=8,'col'=16] {'row'}, dimensions={0} | all-to-all | bytes 524288 | tf_op jit(solution)/shard_map/all_to_all | solution.py:23
  125.7 9.9 %residual_products.1 = f32[2048,128]{1,0:T(8,128)} custom-call(f32[8,64,128]{2,1,0:T(8,128)S(1)} %all_to_all.53.resid_ref, f32[2048,1024]{1,0:T(8,128)} %a_ref.3, f32[2048,1024]{1,0:T(8,128)} %b_ref.3), custom_call_target="tpu_custom_call" | custom-call | tf_op jit(solution)/shard_map/residual_products/pallas_call | solution.py:328
  135.6 9.2 %all-to-all-start.5 = ((f32[16,128,128]{2,1,0:T(8,128)}), f32[16,128,128]{2,1,0:T(8,128)S(1)}, u32[]{:S(2)}, u32[]{:S(2)}) async-start(f32[16,128,128]{2,1,0:T(8,128)} %bitcast.10), calls=%async_computation.6 | async-start | bytes 2097152 | tf_op jit(solution)/shard_map/all_to_all | solution.py:374
  145.7 16.3 %all-to-all-done.5 = f32[16,128,128]{2,1,0:T(8,128)S(1)} async-done(((f32[16,128,128]{2,1,0:T(8,128)}), f32[16,128,128]{2,1,0:T(8,128)S(1)}, u32[]{:S(2)}, u32[]{:S(2)}) %all-to-all-start.5) | async-done | bytes 1048608 | tf_op jit(solution)/shard_map/all_to_all | solution.py:374
  162.3 8.2 %all_to_all.54 = f32[8,24,128]{2,1,0:T(8,128)S(1)} all-to-all(f32[8,24,128]{2,1,0:T(8,128)S(1)} %fusion), channel_id=1, replica_groups=mesh['row'=8,'col'=16] {'row'}, dimensions={0} | all-to-all | bytes 196608 | tf_op jit(solution)/shard_map/all_to_all | solution.py:28
  170.5 11.2 %all_to_all.55 = f32[16,24,128]{2,1,0:T(8,128)S(1)} all-to-all(f32[16,24,128]{2,1,0:T(8,128)S(1)} %broadcast_in_dim.18), channel_id=1, replica_groups=mesh['row'=8,'col'=16] {'col'}, dimensions={0} | all-to-all | bytes 393216 | tf_op jit(solution)/shard_map/all_to_all | solution.py:23
  181.7 8.2 %all_to_all.56 = f32[8,24,128]{2,1,0:T(8,128)S(1)} all-to-all(f32[8,24,128]{2,1,0:T(8,128)S(1)} %broadcast_in_dim.19), channel_id=1, replica_groups=mesh['row'=8,'col'=16] {'row'}, dimensions={0} | all-to-all | bytes 196608 | tf_op jit(solution)/shard_map/all_to_all | solution.py:23
  189.9 17.3 %ritz_second.1 = f32[192,128]{1,0:T(8,128)S(1)} custom-call(f32[256,128]{1,0:T(8,128)S(1)} %get-tuple-element.9.old_ref, f32[192,128]{1,0:T(8,128)S(1)} %bitcast.55, f32[192,128]{1,0:T(8,128)S(1)} %get-tuple-element.10.basis_ref, f32[192,128]{1,0:T(8,128)S(1)} %pad_maximum_fusion.own_ref, f32[64,128]{1,0:T(8,128)S(1)} %fusion.6.resid_ref, ...), custom_call_target="tpu_custom_call" | custom-call | tf_op jit(solution)/shard_map/ritz_second/pallas_call | solution.py:222
  207.4 25.6 %all_to_all.57 = f32[16,192,128]{2,1,0:T(8,128)S(1)} all-to-all(f32[16,192,128]{2,1,0:T(8,128)S(1)} %broadcast_in_dim.20), channel_id=1, replica_groups=mesh['row'=8,'col'=16] {'col'}, dimensions={0} | all-to-all | bytes 3145728 | tf_op jit(solution)/shard_map/all_to_all | solution.py:23
  233.1 0.8 copy.20
  234.0 0.8 copy.21
  (31 shorter events, 5.6 us)
Async XLA Ops:
  7.2 69.8 %reduce-scatter.2.cloned.1.call-start = ((), (), s32[]{:S(2)}) async-start(), calls=%async_computation.11 | async-start | bytes 1769472 | tf_op jit(solution)/shard_map/reduce_scatter | solution.py:357
  7.2 1.0 copy-start
  8.3 1.0 copy-start.1
  9.3 1.0 copy-start.2
  22.0 0.7 collective-permute-start
  69.0 18.1 %all-to-all-start.2 = ((f32[16,48,128]{2,1,0:T(8,128)}), f32[16,48,128]{2,1,0:T(8,128)S(1)}, u32[]{:S(2)}, u32[]{:S(2)}) async-start(f32[16,48,128]{2,1,0:T(8,128)} %broadcast_in_dim.15), calls=%async_computation.2 | async-start | bytes 786432 | tf_op jit(solution)/shard_map/all_to_all | solution.py:23
  77.0 19.4 %collective-permute-start.1 = (f32[384,128]{1,0:T(8,128)}, f32[384,128]{1,0:T(8,128)S(1)}, u32[]{:S(2)}, u32[]{:S(2)}) collective-permute-start(f32[384,128]{1,0:T(8,128)} %bitcast.61), channel_id=1, source_target_pairs={{0,0},{16,1},{32,2},{48,3},{64,4},{80,5},{96,6},{112,7},{1,8},{17,... | collective-permute-start | bytes 589832 | tf_op jit(solution)/shard_map/ppermute | solution.py:358
  135.6 26.4 %all-to-all-start.5 = ((f32[16,128,128]{2,1,0:T(8,128)}), f32[16,128,128]{2,1,0:T(8,128)S(1)}, u32[]{:S(2)}, u32[]{:S(2)}) async-start(f32[16,128,128]{2,1,0:T(8,128)} %bitcast.10), calls=%async_computation.6 | async-start | bytes 2097152 | tf_op jit(solution)/shard_map/all_to_all | solution.py:374
Sparse Core Ops, SparseCore 0:
  20.6 40.8 reduce-scatter.1

commit v4 on v3

--- a/solution.py
+++ b/solution.py
@@ -176,11 +176,11 @@
     old_ref,
     fresh_ref,
     basis_ref,
-    own_ref,
-    resid_ref,
+    turn_ref,
     prod_ref,
     more_ref,
-    out_ref,
+    r_ref,
+    mix_ref,
     inv_ref,
     a_ref,
 ):
@@ -202,11 +202,11 @@
     from_r = coords[k : 2 * k]
     move_p = dot(basis[:, k:], coords[2 * k :])
     move_x = dot(basis, jnp.concatenate([coords[:k], coords[2 * k :]], 0))
-    vectors = jnp.concatenate([own_ref[...], resid_ref[...]], 0)
-    out_ref[:k] = dot(jnp.concatenate([move_x, from_r], 0), vectors, TN)
-    out_ref[2 * k :] = dot(jnp.concatenate([move_p, from_r], 0), vectors, TN)
     more = more_ref[...].T
-    out_ref[k : 2 * k] = (
+    shared = dot(turn_ref[...], from_r)
+    mix_ref[: 3 * k] = jnp.concatenate([move_x, move_p], 1)
+    mix_ref[3 * k :] = jnp.concatenate([shared, shared], 1)
+    r_ref[...] = (
         dot(move_x, prod_ref[: 3 * k], TN)
         - dot(dot(move_x, reduced), prod_ref[3 * k :], TN)
         + dot(from_r, more[:k], TN)
@@ -218,12 +218,17 @@
     return jax.ShapeDtypeStruct(shape, jnp.float32)
 
 
-def call(kernel, name, out_shape, scratch, *args):
+def cost(flops, size):
+    return pl.CostEstimate(flops=int(flops), bytes_accessed=int(size), transcendentals=0)
+
+
+def call(kernel, name, out_shape, scratch, flops, *args):
     return pl.pallas_call(
         kernel,
         out_shape=out_shape,
         scratch_shapes=[pltpu.VMEM(shape, jnp.float32) for shape in scratch],
         compiler_params=pltpu.CompilerParams(vmem_limit_bytes=32 * 2**20),
+        cost_estimate=cost(flops, 2**20),
         name=name,
     )(*args)
 
@@ -258,14 +263,14 @@
             out_ref[i, at : at + wide] = prod[:, i * lanes : (i + 1) * lanes]
 
 
-def gram_kernel(prods_ref, panel_ref, out_ref):
-    pieces, wide, lanes = panel_ref.shape
+def gram_kernel(parts_ref, panel_ref, prods_ref, out_ref):
+    wide = panel_ref.shape[0]
     k = wide // 3
-    gram = jnp.zeros((2 * wide, wide), jnp.float32)
-    for i in range(0, pieces, 2):
-        left = jnp.concatenate([prods_ref[i], prods_ref[i + 1]], 1)
-        right = jnp.concatenate([panel_ref[i], panel_ref[i + 1]], 1)
-        gram = gram + three(split(left), split(right), NT)
+    prods = parts_ref[0]
+    for i in range(1, parts_ref.shape[0]):
+        prods = prods + parts_ref[i]
+    prods_ref[...] = prods
+    gram = three(split(prods), split(panel_ref[...]), NT)
     at = 0
     for i in range(3):
         for j in range(i + 1):
@@ -278,13 +283,37 @@
             at += k
 
 
-def residual_kernel(resid_ref, a_ref, b_ref, out_ref, first_ref, second_ref):
-    pieces, k, lanes = resid_ref.shape
+def fresh_kernel(parts_ref, turn_ref, prods_ref, basis_ref, own_ref, more_ref, resid_ref, out_ref):
+    k = turn_ref.shape[1]
+    more = parts_ref[0]
+    for i in range(1, parts_ref.shape[0]):
+        more = more + parts_ref[i]
+    more_ref[...] = more
+    resid = dot(turn_ref[...], prods_ref[...], TN)
+    resid_ref[...] = resid
+    kept = dot(basis_ref[...], own_ref[...], TN)
+    tests = jnp.concatenate([kept[:k], resid, kept[k:]], 0)
+    out_ref[...] = three(split(tests), split(more), ((1,), (0,)))
+
+
+def outputs_kernel(mix_ref, x_ref, r_ref, p_ref, prods_ref, x_out, p_out):
+    k = x_ref.shape[0]
+    prods = jnp.concatenate([prods_ref[i] for i in range(prods_ref.shape[0])], 1)
+    vectors = jnp.concatenate([x_ref[...], r_ref[...], p_ref[...], prods], 0)
+    out = three(split(mix_ref[...]), split(vectors), TN)
+    x_out[...] = out[:k]
+    p_out[...] = out[k:]
+
+
+def residual_kernel(turn_ref, prods_ref, a_ref, b_ref, out_ref, first_ref, second_ref):
+    pieces, _, lanes = prods_ref.shape
+    k = turn_ref.shape[1]
 
     @pl.when(pl.program_id(0) == 0)
     def _():
+        turn = split(turn_ref[...])
         for i in range(pieces):
-            block = resid_ref[i].T
+            block = three(split(prods_ref[i]), turn, TN)
             high = block.astype(jnp.bfloat16).astype(jnp.float32)
             low = block - high
             rows = pl.ds(i * lanes, lanes)
@@ -315,26 +344,56 @@
         out_specs=pl.BlockSpec((each, 6 * k, lanes), lambda i: (i, 0, 0)),
         out_shape=f32(pieces, 6 * k, lanes),
         scratch_shapes=[pltpu.VMEM((6 * k, rows), jnp.bfloat16)],
-        compiler_params=pltpu.CompilerParams(vmem_limit_bytes=48 * 2**20),
+        compiler_params=pltpu.CompilerParams(vmem_limit_bytes=60 * 2**20),
+        cost_estimate=cost(1e10, 8 * rows * a.shape[1]),
         name="products",
     )(x, r, p, a, b)
 
 
-def residual_products(resid, a, b):
-    pieces, k, lanes = resid.shape
+def residual_products(turn, prods, a, b):
+    k = turn.shape[1]
     rows, cols = a.shape
     height = 512
     tile = pl.BlockSpec((height, cols), lambda i: (i, 0))
     return pl.pallas_call(
         residual_kernel,
         grid=(rows // height,),
-        in_specs=[pl.BlockSpec(resid.shape, lambda i: (0, 0, 0)), tile, tile],
+        in_specs=[
+            pl.BlockSpec(turn.shape, lambda i: (0, 0)),
+            pl.BlockSpec(prods.shape, lambda i: (0, 0, 0)),
+            tile,
+            tile,
+        ],
         out_specs=pl.BlockSpec((height, 2 * k), lambda i: (i, 0)),
         out_shape=f32(rows, 2 * k),
         scratch_shapes=[pltpu.VMEM((cols, 2 * k), jnp.bfloat16)] * 2,
-        compiler_params=pltpu.CompilerParams(vmem_limit_bytes=48 * 2**20),
+        compiler_params=pltpu.CompilerParams(vmem_limit_bytes=60 * 2**20),
+        cost_estimate=cost(1e10, 8 * rows * cols),
         name="residual_products",
-    )(resid, a, b)
+    )(turn, prods, a, b)
+
+
+def outputs(mix, x, r, p, prods):
+    k, rows = x.shape
+    pieces, wide, lanes = prods.shape
+    each = 4
+    part = pl.BlockSpec((k, each * lanes), lambda i: (0, i))
+    return pl.pallas_call(
+        outputs_kernel,
+        grid=(pieces // each,),
+        in_specs=[
+            pl.BlockSpec(mix.shape, lambda i: (0, 0)),
+            part,
+            part,
+            part,
+            pl.BlockSpec((each, wide, lanes), lambda i: (i, 0, 0)),
+        ],
+        out_specs=(part, part),
+        out_shape=(f32(k, rows), f32(k, rows)),
+        compiler_params=pltpu.CompilerParams(vmem_limit_bytes=60 * 2**20),
+        cost_estimate=cost(3e9, 12 * rows * wide),
+        name="outputs",
+    )(mix, x, r, p, prods)
 
 
 def local(a_matrix, b_matrix, x_block, r_block, p_block):
@@ -354,43 +413,56 @@
     own_col = lax.ppermute(own_row, BOTH, to_col)
 
     prods = products(*panel, a_matrix, b_matrix, rows)
-    prod_col = lax.psum_scatter(prods, "row", scatter_dimension=0)
+    prods = lax.all_to_all(prods, "row", 0, 0)
+    prod_col, packed = call(
+        gram_kernel, "gram", (f32(6 * k, piece), f32(6 * k, 2 * k)), [], 2e9, prods, own_col
+    )
     prod_row = lax.ppermute(prod_col, BOTH, to_row)
-    matched = share(own_col, "row")
-    packed = sum_everywhere(call(gram_kernel, "gram", f32(6 * k, 2 * k), [], prods, matched))
-    packed, prod_row = lax.optimization_barrier((packed, prod_row))
+    prods_col = lax.all_gather(prod_col, "row")
+    prods_row = lax.all_gather(prod_row, "col")
+    packed = sum_everywhere(packed)
     turn, basis, old = call(
         functools.partial(first_kernel, k, order),
         "ritz_first",
         (f32(6 * k, k), f32(3 * k, 2 * k), f32(4 * k, 2 * k)),
         [(3 * k, 3 * k)] * 3,
+        1.7e10,
         packed,
     )
 
-    resid_col = mm(turn, prod_col, TN)
-    resid_row = mm(turn, prod_row, TN)
-    parts = residual_products(share(resid_col, "row"), a_matrix, b_matrix)
-    parts = parts.reshape(cols, piece, 2 * k)
-    more_row = lax.all_to_all(parts, "col", 0, 0).sum(0)
-
-    kept = mm(basis, own_row, TN)
-    tests = jnp.concatenate([kept[:k], resid_row, kept[k:]], 0)
-    fresh = sum_everywhere(mm(tests, more_row))
-    outs = call(
+    parts = residual_products(turn, prods_col, a_matrix, b_matrix)
+    parts = lax.all_to_all(parts.reshape(cols, piece, 2 * k), "col", 0, 0)
+    more_row, resid_row, fresh = call(
+        fresh_kernel,
+        "fresh",
+        (f32(piece, 2 * k), f32(k, piece), f32(3 * k, 2 * k)),
+        [],
+        1e9,
+        parts,
+        turn,
+        prod_row,
+        basis,
+        own_row,
+    )
+    fresh = sum_everywhere(fresh)
+    r_own, mix = call(
         functools.partial(second_kernel, k, order),
         "ritz_second",
-        f32(3 * k, piece),
+        (f32(k, piece), f32(9 * k, 2 * k)),
         [(3 * k, 3 * k)] * 2,
+        1.7e10,
         old,
         fresh,
         basis,
-        own_row,
-        resid_row,
+        turn,
         prod_row,
         more_row,
     )
-    outs = share(outs, "col").transpose(1, 0, 2).reshape(3 * k, -1)
-    return (outs[:k].T, outs[k : 2 * k].T, outs[2 * k :].T)
+    r_next = share(r_own, "col")
+    x_next, p_next = outputs(mix, *panel, prods_row)
+    r_next, x_next, p_next = lax.optimization_barrier((r_next, x_next, p_next))
+    r_next = r_next.transpose(1, 0, 2).reshape(k, -1)
+    return (x_next.T, r_next.T, p_next.T)
 
 
 def solution(mesh):

time: 243 us -> 222 us (0.914)
  blocking collectives: 116 us -> 72.8 us
  waiting for transfers between devices: 24.8 us -> 40.7 us
  Pallas kernels: 57.3 us -> 63.3 us
  starting transfers between devices: 19.5 us -> 22.9 us
  matrix products: 2.54 us -> 0 us
    all_to_all x6 -> x2, blocking collectives: 98.2 us -> 19.4 us  [share(): return lax.all_to_all(copies, axis, 0, 0)]
    all_to_all x0 -> x1, blocking collectives: none -> 31.6 us  [local(): parts = lax.all_to_all(parts.reshape(cols, piece, 2 * k), 'col', 0, 0)]
    all_to_all x1 -> x3, waiting for transfers between devices: 8.5 us -> 20.7 us  [share(): return lax.all_to_all(copies, axis, 0, 0)]
    all_to_all x1 -> x3, starting transfers between devices: 7.97 us -> 15 us  [share(): return lax.all_to_all(copies, axis, 0, 0)]
    pallas_call x0 -> x1, Pallas kernels: none -> 5.25 us  [outputs(): pl.pallas_call(outputs_kernel, grid=(pieces // each,), in_specs=[pl.Block...]
    all_to_all x2, blocking collectives: 17.4 us -> 21.8 us  [sum_everywhere(): own = lax.all_to_all(parts, 'row', 0, 0).sum(0)]
    all_to_all x1, starting transfers between devices: 9.21 us -> 5.39 us  [local(): prods = lax.all_to_all(prods, 'row', 0, 0)]
    all_to_all x1, waiting for transfers between devices: 16.3 us -> 20 us  [local(): prods = lax.all_to_all(prods, 'row', 0, 0)]
  transfers between devices with their start and end apart: 5 -> 8, of which waited for: 2 -> 4; matrix products, arithmetic and copies ran while one was open for 1% -> 2% of each run, Pallas kernels for 1% -> 24%
where the time goes in v4:
time: 222 us; the launch traced here: 221 us
  blocking collectives  72.8 us (33%)
  Pallas kernels  63.3 us (29%)
  waiting for transfers between devices  40.7 us (18%)
  starting transfers between devices  22.9 us (10%)
  between operations  14.2 us (6%)
  local copies, waits for them, and re-layouts  6.79 us (3%)
    pallas_call x4, Pallas kernels, call(): pl.pallas_call(kernel, out_shape=out_shape, scratch_shapes=[pltpu.VMEM(sh...  36.5 us
    all_to_all x1, blocking collectives, local(): parts = lax.all_to_all(parts.reshape(cols, piece, 2 * k), 'col', 0, 0)  31.6 us
    all_to_all x2, blocking collectives, sum_everywhere(): own = lax.all_to_all(parts, 'row', 0, 0).sum(0)  21.8 us
    all_to_all x3, waiting for transfers between devices, share(): return lax.all_to_all(copies, axis, 0, 0)  20.7 us
    all_to_all x1, waiting for transfers between devices, local(): prods = lax.all_to_all(prods, 'row', 0, 0)  20 us
    all_to_all x2, blocking collectives, share(): return lax.all_to_all(copies, axis, 0, 0)  19.4 us
    all_to_all x3, starting transfers between devices, share(): return lax.all_to_all(copies, axis, 0, 0)  15 us
    pallas_call x1, Pallas kernels, residual_products(): pl.pallas_call(residual_kernel, grid=(rows // height,), in_specs=[pl.Bloc...  11 us
  transfers between devices with their start and end apart: 8, of which 4 were waited for; matrix products, arithmetic and copies ran while one was open for 2% of the time, Pallas kernels for 24%

profile of v4, /device:TPU:0, one launch (start us, length us, event | category | flops | bytes accessed | tf_op | source)
XLA Modules:
  0.0 220.8 jit_solution(345903422121501647)
XLA Ops:
  7.2 10.6 %products.1 = f32[8,384,128]{2,1,0:T(8,128)} custom-call(f32[64,2048]{1,0:T(8,128)} %bitcast.31, f32[64,2048]{1,0:T(8,128)} %bitcast.33, f32[64,2048]{1,0:T(8,128)} %bitcast.35, f32[2048,1024]{1,0:T(8,128)} %a_ref.3, f32[2048,1024]{1,0:T(8,128)} %b_ref.3), custom_call_target="tpu_custom_call" | custom-call | flops 10000000000 | bytes 16777216 | tf_op jit(solution)/shard_map/products/pallas_call | solution.py:340
  17.7 5.4 %all-to-all-start = ((f32[8,384,128]{2,1,0:T(8,128)}), f32[8,384,128]{2,1,0:T(8,128)S(1)}, u32[]{:S(2)}, u32[]{:S(2)}) async-start(f32[8,384,128]{2,1,0:T(8,128)} %products.1), calls=%async_computation | async-start | bytes 3145728 | tf_op jit(solution)/shard_map/all_to_all | solution.py:416
  23.9 0.8 dynamic-slice_bitcast_fusion
  25.4 20.0 %all-to-all-done.parts_ref = f32[8,384,128]{2,1,0:T(8,128)S(1)} async-done(((f32[8,384,128]{2,1,0:T(8,128)}), f32[8,384,128]{2,1,0:T(8,128)S(1)}, u32[]{:S(2)}, u32[]{:S(2)}) %all-to-all-start) | async-done | bytes 1572896 | tf_op jit(solution)/shard_map/all_to_all | solution.py:416
  45.4 0.9 gram.1
  46.3 11.8 %all_to_all.45 = f32[8,48,128]{2,1,0:T(8,128)S(1)} all-to-all(f32[8,48,128]{2,1,0:T(8,128)S(1)} %bitcast.27), channel_id=1, replica_groups=mesh['row'=8,'col'=16] {'row'}, dimensions={0} | all-to-all | bytes 393216 | tf_op jit(solution)/shard_map/all_to_all | solution.py:28
  58.9 8.0 %all-to-all-start.2 = ((f32[16,48,128]{2,1,0:T(8,128)}), f32[16,48,128]{2,1,0:T(8,128)S(1)}, u32[]{:S(2)}, u32[]{:S(2)}) async-start(f32[16,48,128]{2,1,0:T(8,128)} %broadcast_in_dim.10), calls=%async_computation.2 | async-start | bytes 786432 | tf_op jit(solution)/shard_map/all_to_all | solution.py:23
  66.9 1.6 collective-permute-start.1
  68.5 8.5 %all-to-all-done.2 = f32[16,48,128]{2,1,0:T(8,128)S(1)} async-done(((f32[16,48,128]{2,1,0:T(8,128)}), f32[16,48,128]{2,1,0:T(8,128)S(1)}, u32[]{:S(2)}, u32[]{:S(2)}) %all-to-all-start.2) | async-done | bytes 393248 | tf_op jit(solution)/shard_map/all_to_all | solution.py:23
  77.7 3.4 %all-to-all-start.3 = ((f32[8,48,128]{2,1,0:T(8,128)}), f32[8,48,128]{2,1,0:T(8,128)S(1)}, u32[]{:S(2)}, u32[]{:S(2)}) async-start(f32[8,48,128]{2,1,0:T(8,128)} %broadcast_in_dim.11), calls=%async_computation.3 | async-start | bytes 393216 | tf_op jit(solution)/shard_map/all_to_all | solution.py:23
  82.1 5.8 %all-to-all-done.3 = f32[8,48,128]{2,1,0:T(8,128)S(1)} async-done(((f32[8,48,128]{2,1,0:T(8,128)}), f32[8,48,128]{2,1,0:T(8,128)S(1)}, u32[]{:S(2)}, u32[]{:S(2)}) %all-to-all-start.3) | async-done | bytes 196640 | tf_op jit(solution)/shard_map/all_to_all | solution.py:23
  87.9 17.3 %ritz_first.1 = (f32[384,64]{1,0:T(8,128)S(1)}, f32[192,128]{1,0:T(8,128)S(1)}, f32[256,128]{1,0:T(8,128)S(1)}) custom-call(f32[384,128]{1,0:T(8,128)S(1)} %bitcast.26), custom_call_target="tpu_custom_call" | custom-call | flops 16999999488 | bytes 1048576 | tf_op jit(solution)/shard_map/ritz_first/pallas_call | solution.py:226
  105.9 11.0 %residual_products.1 = f32[2048,128]{1,0:T(8,128)} custom-call(f32[384,64]{1,0:T(8,128)} %copy-done.2, f32[8,384,128]{2,1,0:T(8,128)} %bitcast.38, f32[2048,1024]{1,0:T(8,128)} %a_ref.3, f32[2048,1024]{1,0:T(8,128)} %b_ref.3), custom_call_target="tpu_custom_call" | custom-call | flops 10000000000 | bytes 16777216 | tf_op jit(solution)/shard_map/residual_products/pallas_call | solution.py:358
  116.9 31.6 %all_to_all.46.parts_ref = f32[16,128,128]{2,1,0:T(8,128)S(1)} all-to-all(f32[16,128,128]{2,1,0:T(8,128)} %bitcast.30), channel_id=1, replica_groups=mesh['row'=8,'col'=16] {'col'}, dimensions={0} | all-to-all | bytes 2097152 | tf_op jit(solution)/shard_map/all_to_all | solution.py:434
  148.5 1.0 fresh.1
  149.5 10.0 %all_to_all.47 = f32[8,24,128]{2,1,0:T(8,128)S(1)} all-to-all(f32[8,24,128]{2,1,0:T(8,128)S(1)} %bitcast.29), channel_id=1, replica_groups=mesh['row'=8,'col'=16] {'row'}, dimensions={0} | all-to-all | bytes 196608 | tf_op jit(solution)/shard_map/all_to_all | solution.py:28
  159.5 11.0 %all_to_all.48 = f32[16,24,128]{2,1,0:T(8,128)S(1)} all-to-all(f32[16,24,128]{2,1,0:T(8,128)S(1)} %broadcast_in_dim.12), channel_id=1, replica_groups=mesh['row'=8,'col'=16] {'col'}, dimensions={0} | all-to-all | bytes 393216 | tf_op jit(solution)/shard_map/all_to_all | solution.py:23
  170.5 8.4 %all_to_all.49 = f32[8,24,128]{2,1,0:T(8,128)S(1)} all-to-all(f32[8,24,128]{2,1,0:T(8,128)S(1)} %broadcast_in_dim.13), channel_id=1, replica_groups=mesh['row'=8,'col'=16] {'row'}, dimensions={0} | all-to-all | bytes 196608 | tf_op jit(solution)/shard_map/all_to_all | solution.py:23
  178.9 17.4 %ritz_second.1 = (f32[64,128]{1,0:T(8,128)S(1)}, f32[576,128]{1,0:T(8,128)S(1)}) custom-call(f32[256,128]{1,0:T(8,128)S(1)} %get-tuple-element.18.old_ref, f32[192,128]{1,0:T(8,128)S(1)} %bitcast.28, f32[192,128]{1,0:T(8,128)S(1)} %get-tuple-element.21.basis_ref, f32[384,64]{1,0:T(8,128)S(1)} %copy-done.3, f32[384,128]{1,0:T(8,128)S(1)} %copy-done.1, ...), custom_call_target="tpu_custom_call" | custom-call | flops 16999999488 | bytes 1048576 | tf_op jit(solution)/shard_map/ritz_second/pallas_call | solution.py:226
  197.0 0.8 broadcast_in_dim.14
  197.9 3.6 %all-to-all-start.8 = ((f32[16,64,128]{2,1,0:T(8,128)}), f32[16,64,128]{2,1,0:T(8,128)S(1)}, u32[]{:S(2)}, u32[]{:S(2)}) async-start(f32[16,64,128]{2,1,0:T(8,128)} %broadcast_in_dim.14), calls=%async_computation.8 | async-start | bytes 1048576 | tf_op jit(solution)/shard_map/all_to_all | solution.py:23
  201.5 5.3 %outputs.1 = (f32[64,2048]{1,0:T(8,128)}, f32[64,2048]{1,0:T(8,128)}) custom-call(f32[576,128]{1,0:T(8,128)} %copy-done.4, f32[64,2048]{1,0:T(8,128)} %bitcast.32, f32[64,2048]{1,0:T(8,128)} %bitcast.34, f32[64,2048]{1,0:T(8,128)} %bitcast.36, f32[16,384,128]{2,1,0:T(8,128)} %bitcast.37), custom_call_target="tpu_custom_call" | custom-call | flops 3000000000 | bytes 9437184 | tf_op jit(solution)/shard_map/outputs/pallas_call | solution.py:381
  206.7 6.4 %all-to-all-done.8 = f32[16,64,128]{2,1,0:T(8,128)S(1)} async-done(((f32[16,64,128]{2,1,0:T(8,128)}), f32[16,64,128]{2,1,0:T(8,128)S(1)}, u32[]{:S(2)}, u32[]{:S(2)}) %all-to-all-start.8) | async-done | bytes 524320 | tf_op jit(solution)/shard_map/all_to_all | solution.py:23
  213.1 0.8 bitcast_bitcast_fusion
  (29 shorter events, 5.4 us)
Async XLA Ops:
  17.7 27.7 %all-to-all-start = ((f32[8,384,128]{2,1,0:T(8,128)}), f32[8,384,128]{2,1,0:T(8,128)S(1)}, u32[]{:S(2)}, u32[]{:S(2)}) async-start(f32[8,384,128]{2,1,0:T(8,128)} %products.1), calls=%async_computation | async-start | bytes 3145728 | tf_op jit(solution)/shard_map/all_to_all | solution.py:416
  23.1 82.8 %all-gather.5.cloned.1.call-start = ((), (), s32[]{:S(2)}) async-start(), calls=%async_computation.9 | async-start | bytes 1769472 | tf_op jit(solution)/shard_map/all_gather | solution.py:421
  24.7 0.7 collective-permute-start
  58.9 18.1 %all-to-all-start.2 = ((f32[16,48,128]{2,1,0:T(8,128)}), f32[16,48,128]{2,1,0:T(8,128)S(1)}, u32[]{:S(2)}, u32[]{:S(2)}) async-start(f32[16,48,128]{2,1,0:T(8,128)} %broadcast_in_dim.10), calls=%async_computation.2 | async-start | bytes 786432 | tf_op jit(solution)/shard_map/all_to_all | solution.py:23
  66.9 14.5 %collective-permute-start.1 = (f32[384,128]{1,0:T(8,128)}, f32[384,128]{1,0:T(8,128)S(1)}, u32[]{:S(2)}, u32[]{:S(2)}) collective-permute-start(f32[384,128]{1,0:T(8,128)} %get-tuple-element.20), channel_id=1, source_target_pairs={{0,0},{16,1},{32,2},{48,3},{64,4},{80,5},{96,6},{112,7},{1,8},{17,... | collective-permute-start | bytes 589832 | tf_op jit(solution)/shard_map/ppermute | solution.py:420
  77.7 10.2 %all-to-all-start.3 = ((f32[8,48,128]{2,1,0:T(8,128)}), f32[8,48,128]{2,1,0:T(8,128)S(1)}, u32[]{:S(2)}, u32[]{:S(2)}) async-start(f32[8,48,128]{2,1,0:T(8,128)} %broadcast_in_dim.11), calls=%async_computation.3 | async-start | bytes 393216 | tf_op jit(solution)/shard_map/all_to_all | solution.py:23
  81.1 120.4 %all-gather.7.cloned.1.call-start = ((), (), s32[]{:S(2)}) async-start(), calls=%async_computation.10 | async-start | bytes 3342336 | tf_op jit(solution)/shard_map/all_gather | solution.py:422
  81.4 0.7 copy-start
  105.2 0.7 copy-start.2
  105.9 42.6 %copy-start.1 = (f32[384,128]{1,0:T(8,128)S(1)}, f32[384,128]{1,0:T(8,128)}, u32[]{:S(2)}) copy-start(f32[384,128]{1,0:T(8,128)} %copy-done) | copy-start | bytes 589828
  105.9 42.6 %copy-start.3 = (f32[384,64]{1,0:T(8,128)S(1)}, f32[384,64]{1,0:T(8,128)}, u32[]{:S(2)}) copy-start(f32[384,64]{1,0:T(8,128)} %copy-done.2) | copy-start | bytes 294916
  196.3 0.7 copy-start.4
  197.9 15.2 %all-to-all-start.8 = ((f32[16,64,128]{2,1,0:T(8,128)}), f32[16,64,128]{2,1,0:T(8,128)S(1)}, u32[]{:S(2)}, u32[]{:S(2)}) async-start(f32[16,64,128]{2,1,0:T(8,128)} %broadcast_in_dim.14), calls=%async_computation.8 | async-start | bytes 1048576 | tf_op jit(solution)/shard_map/all_to_all | solution.py:23
Sparse Core Ops, SparseCore 0:
  46.4 26.9 all-gather.4
  84.7 62.5 all-gather.6

commit v5 on v4

--- a/solution.py
+++ b/solution.py
@@ -78,25 +78,37 @@
             for t in later
         }
         low = [[None] * height for _ in range(height)]
-        inv = [None] * height
-        for i in range(height):
-            inv[i] = 1.0 / elem[i][i]
-            for m in range(i + 1, height):
-                low[m][i] = elem[m][i] * inv[i]
-                for n in range(i + 1, m + 1):
-                    elem[m][n] = elem[m][n] - low[m][i] * elem[n][i]
-                rows[m] = rows[m] - low[m][i] * rows[i]
-        out = rows[0] * (1.0 / jnp.sqrt(elem[0][0]))
-        for m in range(1, height):
-            out = jnp.where(line == m, rows[m] * (1.0 / jnp.sqrt(elem[m][m])), out)
+        inv = {}
+        out = None
+        for i in range(0, height, 2):
+            a, b, c = elem[i][i], elem[i + 1][i], elem[i + 1][i + 1]
+            det = a * c - b * b
+            inv[i] = 1.0 / det
+            for m in range(i + 2, height):
+                u, v = elem[m][i], elem[m][i + 1]
+                low[m][i] = (u * c - v * b) * inv[i]
+                low[m][i + 1] = (v * a - u * b) * inv[i]
+                for n in range(i + 2, m + 1):
+                    elem[m][n] = elem[m][n] - (
+                        low[m][i] * elem[n][i] + low[m][i + 1] * elem[n][i + 1]
+                    )
+                rows[m] = rows[m] - (low[m][i] * rows[i] + low[m][i + 1] * rows[i + 1])
+            scale = 1.0 / a
+            upper = rows[i] * (1.0 / jnp.sqrt(a))
+            lower = (rows[i + 1] - (b * scale) * rows[i]) * (1.0 / jnp.sqrt(det * scale))
+            out = upper if out is None else jnp.where(line == i, upper, out)
+            out = jnp.where(line == i + 1, lower, out)
         done.append(out)
         if not later:
             break
         solved = [None] * height
-        for m in reversed(range(height)):
-            solved[m] = rows[m] * inv[m]
-            for i in range(m + 1, height):
-                solved[m] = solved[m] - low[i][m] * solved[i]
+        for i in reversed(range(0, height, 2)):
+            a, b, c = elem[i][i], elem[i + 1][i], elem[i + 1][i + 1]
+            solved[i] = (c * rows[i] - b * rows[i + 1]) * inv[i]
+            solved[i + 1] = (a * rows[i + 1] - b * rows[i]) * inv[i]
+            for m in range(i + 2, height):
+                solved[i] = solved[i] - low[m][i] * solved[m]
+                solved[i + 1] = solved[i + 1] - low[m][i + 1] * solved[m]
         for t in later:
             for m in range(height):
                 strips[t] = strips[t] - cols[t][m] * solved[m]
@@ -176,7 +188,6 @@
     old_ref,
     fresh_ref,
     basis_ref,
-    turn_ref,
     prod_ref,
     more_ref,
     r_ref,
@@ -203,9 +214,8 @@
     move_p = dot(basis[:, k:], coords[2 * k :])
     move_x = dot(basis, jnp.concatenate([coords[:k], coords[2 * k :]], 0))
     more = more_ref[...].T
-    shared = dot(turn_ref[...], from_r)
     mix_ref[: 3 * k] = jnp.concatenate([move_x, move_p], 1)
-    mix_ref[3 * k :] = jnp.concatenate([shared, shared], 1)
+    mix_ref[3 * k :] = jnp.concatenate([from_r, from_r], 1)
     r_ref[...] = (
         dot(move_x, prod_ref[: 3 * k], TN)
         - dot(dot(move_x, reduced), prod_ref[3 * k :], TN)
@@ -290,16 +300,17 @@
         more = more + parts_ref[i]
     more_ref[...] = more
     resid = dot(turn_ref[...], prods_ref[...], TN)
-    resid_ref[...] = resid
+    resid_ref[:k] = resid
+    resid_ref[k:] = jnp.zeros_like(resid)
     kept = dot(basis_ref[...], own_ref[...], TN)
     tests = jnp.concatenate([kept[:k], resid, kept[k:]], 0)
     out_ref[...] = three(split(tests), split(more), ((1,), (0,)))
 
 
-def outputs_kernel(mix_ref, x_ref, r_ref, p_ref, prods_ref, x_out, p_out):
+def outputs_kernel(mix_ref, x_ref, r_ref, p_ref, resid_ref, x_out, p_out):
     k = x_ref.shape[0]
-    prods = jnp.concatenate([prods_ref[i] for i in range(prods_ref.shape[0])], 1)
-    vectors = jnp.concatenate([x_ref[...], r_ref[...], p_ref[...], prods], 0)
+    resid = jnp.concatenate([resid_ref[i] for i in range(resid_ref.shape[0])], 1)
+    vectors = jnp.concatenate([x_ref[...], r_ref[...], p_ref[...], resid], 0)
     out = three(split(mix_ref[...]), split(vectors), TN)
     x_out[...] = out[:k]
     p_out[...] = out[k:]
@@ -373,10 +384,10 @@
     )(turn, prods, a, b)
 
 
-def outputs(mix, x, r, p, prods):
+def outputs(mix, x, r, p, resid):
     k, rows = x.shape
-    pieces, wide, lanes = prods.shape
-    each = 4
+    pieces, _, lanes = resid.shape
+    each = 8
     part = pl.BlockSpec((k, each * lanes), lambda i: (0, i))
     return pl.pallas_call(
         outputs_kernel,
@@ -386,14 +397,14 @@
             part,
             part,
             part,
-            pl.BlockSpec((each, wide, lanes), lambda i: (i, 0, 0)),
+            pl.BlockSpec((each, k, lanes), lambda i: (i, 0, 0)),
         ],
         out_specs=(part, part),
         out_shape=(f32(k, rows), f32(k, rows)),
         compiler_params=pltpu.CompilerParams(vmem_limit_bytes=60 * 2**20),
-        cost_estimate=cost(3e9, 12 * rows * wide),
+        cost_estimate=cost(3e9, 40 * rows * k),
         name="outputs",
-    )(mix, x, r, p, prods)
+    )(mix, x, r, p, resid)
 
 
 def local(a_matrix, b_matrix, x_block, r_block, p_block):
@@ -419,7 +430,6 @@
     )
     prod_row = lax.ppermute(prod_col, BOTH, to_row)
     prods_col = lax.all_gather(prod_col, "row")
-    prods_row = lax.all_gather(prod_row, "col")
     packed = sum_everywhere(packed)
     turn, basis, old = call(
         functools.partial(first_kernel, k, order),
@@ -429,13 +439,14 @@
         1.7e10,
         packed,
     )
+    turn, prod_row = lax.optimization_barrier((turn, prod_row))
 
     parts = residual_products(turn, prods_col, a_matrix, b_matrix)
     parts = lax.all_to_all(parts.reshape(cols, piece, 2 * k), "col", 0, 0)
     more_row, resid_row, fresh = call(
         fresh_kernel,
         "fresh",
-        (f32(piece, 2 * k), f32(k, piece), f32(3 * k, 2 * k)),
+        (f32(piece, 2 * k), f32(2 * k, piece), f32(3 * k, 2 * k)),
         [],
         1e9,
         parts,
@@ -444,22 +455,22 @@
         basis,
         own_row,
     )
+    resid = lax.all_gather(resid_row, "col")
     fresh = sum_everywhere(fresh)
     r_own, mix = call(
         functools.partial(second_kernel, k, order),
         "ritz_second",
-        (f32(k, piece), f32(9 * k, 2 * k)),
+        (f32(k, piece), f32(4 * k, 2 * k)),
         [(3 * k, 3 * k)] * 2,
         1.7e10,
         old,
         fresh,
         basis,
-        turn,
         prod_row,
         more_row,
     )
     r_next = share(r_own, "col")
-    x_next, p_next = outputs(mix, *panel, prods_row)
+    x_next, p_next = outputs(mix, *panel, resid)
     r_next, x_next, p_next = lax.optimization_barrier((r_next, x_next, p_next))
     r_next = r_next.transpose(1, 0, 2).reshape(k, -1)
     return (x_next.T, r_next.T, p_next.T)

time: 222 us -> 211 us (0.950)
  Pallas kernels: 63.3 us -> 57.5 us
  blocking collectives: 72.8 us -> 67.8 us
  waiting for transfers between devices: 40.7 us -> 45.5 us
  starting transfers between devices: 22.9 us -> 18.2 us
    all_gather x1, waiting for transfers between devices: 0.02 us -> 12 us  [local(): resid = lax.all_gather(resid_row, 'col')]
    all_to_all x1, blocking collectives: 31.6 us -> 22 us  [local(): parts = lax.all_to_all(parts.reshape(cols, piece, 2 * k), 'col', 0, 0)]
    all_to_all x3, waiting for transfers between devices: 20.7 us -> 12.7 us  [share(): return lax.all_to_all(copies, axis, 0, 0)]
    all_to_all x2, blocking collectives: 19.4 us -> 25.8 us  [share(): return lax.all_to_all(copies, axis, 0, 0)]
    all_to_all x3, starting transfers between devices: 15 us -> 10.5 us  [share(): return lax.all_to_all(copies, axis, 0, 0)]
    pallas_call x4, Pallas kernels: 36.5 us -> 33.2 us  [call(): pl.pallas_call(kernel, out_shape=out_shape, scratch_shapes=[pltpu.VMEM(sh...]
    pallas_call x1, Pallas kernels: 5.25 us -> 2.86 us  [outputs(): pl.pallas_call(outputs_kernel, grid=(pieces // each,), in_specs=[pl.Block...]
  transfers between devices with their start and end apart: 8 -> 8, of which waited for: 4 -> 4; matrix products, arithmetic and copies ran while one was open for 2% -> 2% of each run, Pallas kernels for 24% -> 16%
where the time goes in v5:
time: 211 us; the launch traced here: 209 us
  blocking collectives  67.8 us (32%)
  Pallas kernels  57.5 us (27%)
  waiting for transfers between devices  45.5 us (22%)
  starting transfers between devices  18.2 us (9%)
  between operations  14.2 us (7%)
  local copies, waits for them, and re-layouts  5.34 us (3%)
    pallas_call x4, Pallas kernels, call(): pl.pallas_call(kernel, out_shape=out_shape, scratch_shapes=[pltpu.VMEM(sh...  33.2 us
    all_to_all x2, blocking collectives, share(): return lax.all_to_all(copies, axis, 0, 0)  25.8 us
    all_to_all x1, blocking collectives, local(): parts = lax.all_to_all(parts.reshape(cols, piece, 2 * k), 'col', 0, 0)  22 us
    all_to_all x1, waiting for transfers between devices, local(): prods = lax.all_to_all(prods, 'row', 0, 0)  20 us
    all_to_all x2, blocking collectives, sum_everywhere(): own = lax.all_to_all(parts, 'row', 0, 0).sum(0)  20 us
    all_to_all x3, waiting for transfers between devices, share(): return lax.all_to_all(copies, axis, 0, 0)  12.7 us
    all_gather x1, waiting for transfers between devices, local(): resid = lax.all_gather(resid_row, 'col')  12 us
    pallas_call x1, Pallas kernels, residual_products(): pl.pallas_call(residual_kernel, grid=(rows // height,), in_specs=[pl.Bloc...  10.9 us
  transfers between devices with their start and end apart: 8, of which 4 were waited for; matrix products, arithmetic and copies ran while one was open for 2% of the time, Pallas kernels for 16%

profile of v5, /device:TPU:0, one launch (start us, length us, event | category | flops | bytes accessed | tf_op | source)
XLA Modules:
  0.0 208.6 jit_solution(6707800067785855416)
XLA Ops:
  7.2 10.6 %products.1 = f32[8,384,128]{2,1,0:T(8,128)} custom-call(f32[64,2048]{1,0:T(8,128)} %bitcast.31, f32[64,2048]{1,0:T(8,128)} %bitcast.33, f32[64,2048]{1,0:T(8,128)} %bitcast.35, f32[2048,1024]{1,0:T(8,128)} %a_ref.3, f32[2048,1024]{1,0:T(8,128)} %b_ref.3), custom_call_target="tpu_custom_call" | custom-call | flops 10000000000 | bytes 16777216 | tf_op jit(solution)/shard_map/products/pallas_call | solution.py:351
  17.7 5.4 %all-to-all-start = ((f32[8,384,128]{2,1,0:T(8,128)}), f32[8,384,128]{2,1,0:T(8,128)S(1)}, u32[]{:S(2)}, u32[]{:S(2)}) async-start(f32[8,384,128]{2,1,0:T(8,128)} %products.1), calls=%async_computation | async-start | bytes 3145728 | tf_op jit(solution)/shard_map/all_to_all | solution.py:427
  23.9 0.8 dynamic-slice_bitcast_fusion
  25.4 20.0 %all-to-all-done.parts_ref = f32[8,384,128]{2,1,0:T(8,128)S(1)} async-done(((f32[8,384,128]{2,1,0:T(8,128)}), f32[8,384,128]{2,1,0:T(8,128)S(1)}, u32[]{:S(2)}, u32[]{:S(2)}) %all-to-all-start) | async-done | bytes 1572896 | tf_op jit(solution)/shard_map/all_to_all | solution.py:427
  45.4 0.9 gram.1
  46.3 11.8 %all_to_all.45 = f32[8,48,128]{2,1,0:T(8,128)S(1)} all-to-all(f32[8,48,128]{2,1,0:T(8,128)S(1)} %bitcast.27), channel_id=1, replica_groups=mesh['row'=8,'col'=16] {'row'}, dimensions={0} | all-to-all | bytes 393216 | tf_op jit(solution)/shard_map/all_to_all | solution.py:28
  58.1 17.6 %all_to_all.46 = f32[16,48,128]{2,1,0:T(8,128)S(1)} all-to-all(f32[16,48,128]{2,1,0:T(8,128)S(1)} %broadcast_in_dim.10), channel_id=1, replica_groups=mesh['row'=8,'col'=16] {'col'}, dimensions={0} | all-to-all | bytes 786432 | tf_op jit(solution)/shard_map/all_to_all | solution.py:23
  76.5 3.4 %all-to-all-start.3 = ((f32[8,48,128]{2,1,0:T(8,128)}), f32[8,48,128]{2,1,0:T(8,128)S(1)}, u32[]{:S(2)}, u32[]{:S(2)}) async-start(f32[8,48,128]{2,1,0:T(8,128)} %broadcast_in_dim.11), calls=%async_computation.3 | async-start | bytes 393216 | tf_op jit(solution)/shard_map/all_to_all | solution.py:23
  79.9 1.6 collective-permute-start.1
  81.5 5.2 %all-to-all-done.3 = f32[8,48,128]{2,1,0:T(8,128)S(1)} async-done(((f32[8,48,128]{2,1,0:T(8,128)}), f32[8,48,128]{2,1,0:T(8,128)S(1)}, u32[]{:S(2)}, u32[]{:S(2)}) %all-to-all-start.3) | async-done | bytes 196640 | tf_op jit(solution)/shard_map/all_to_all | solution.py:23
  86.6 15.7 %ritz_first.1 = (f32[384,64]{1,0:T(8,128)S(1)}, f32[192,128]{1,0:T(8,128)S(1)}, f32[256,128]{1,0:T(8,128)S(1)}) custom-call(f32[384,128]{1,0:T(8,128)S(1)} %bitcast.26), custom_call_target="tpu_custom_call" | custom-call | flops 16999999488 | bytes 1048576 | tf_op jit(solution)/shard_map/ritz_first/pallas_call | solution.py:236
  103.0 10.9 %residual_products.1 = f32[2048,128]{1,0:T(8,128)} custom-call(f32[384,64]{1,0:T(8,128)} %copy-done, f32[8,384,128]{2,1,0:T(8,128)} %bitcast.37, f32[2048,1024]{1,0:T(8,128)} %a_ref.3, f32[2048,1024]{1,0:T(8,128)} %b_ref.3), custom_call_target="tpu_custom_call" | custom-call | flops 10000000000 | bytes 16777216 | tf_op jit(solution)/shard_map/residual_products/pallas_call | solution.py:369
  113.9 22.0 %all_to_all.47.parts_ref = f32[16,128,128]{2,1,0:T(8,128)S(1)} all-to-all(f32[16,128,128]{2,1,0:T(8,128)} %bitcast.30), channel_id=1, replica_groups=mesh['row'=8,'col'=16] {'col'}, dimensions={0} | all-to-all | bytes 2097152 | tf_op jit(solution)/shard_map/all_to_all | solution.py:445
  135.9 1.1 fresh.1
  137.0 8.2 %all_to_all.48 = f32[8,24,128]{2,1,0:T(8,128)S(1)} all-to-all(f32[8,24,128]{2,1,0:T(8,128)S(1)} %bitcast.29), channel_id=1, replica_groups=mesh['row'=8,'col'=16] {'row'}, dimensions={0} | all-to-all | bytes 196608 | tf_op jit(solution)/shard_map/all_to_all | solution.py:28
  145.9 3.5 %all-to-all-start.6 = ((f32[16,24,128]{2,1,0:T(8,128)}), f32[16,24,128]{2,1,0:T(8,128)S(1)}, u32[]{:S(2)}, u32[]{:S(2)}) async-start(f32[16,24,128]{2,1,0:T(8,128)} %broadcast_in_dim.12), calls=%async_computation.6 | async-start | bytes 393216 | tf_op jit(solution)/shard_map/all_to_all | solution.py:23
  150.2 7.6 %all-to-all-done.6 = f32[16,24,128]{2,1,0:T(8,128)S(1)} async-done(((f32[16,24,128]{2,1,0:T(8,128)}), f32[16,24,128]{2,1,0:T(8,128)S(1)}, u32[]{:S(2)}, u32[]{:S(2)}) %all-to-all-start.6) | async-done | bytes 196640 | tf_op jit(solution)/shard_map/all_to_all | solution.py:23
  157.7 8.2 %all_to_all.49 = f32[8,24,128]{2,1,0:T(8,128)S(1)} all-to-all(f32[8,24,128]{2,1,0:T(8,128)S(1)} %broadcast_in_dim.13), channel_id=1, replica_groups=mesh['row'=8,'col'=16] {'row'}, dimensions={0} | all-to-all | bytes 196608 | tf_op jit(solution)/shard_map/all_to_all | solution.py:23
  165.9 15.6 %ritz_second.1 = (f32[64,128]{1,0:T(8,128)S(1)}, f32[256,128]{1,0:T(8,128)S(1)}) custom-call(f32[256,128]{1,0:T(8,128)S(1)} %get-tuple-element.21.old_ref, f32[192,128]{1,0:T(8,128)S(1)} %bitcast.28, f32[192,128]{1,0:T(8,128)S(1)} %get-tuple-element.26.basis_ref, f32[384,128]{1,0:T(8,128)S(1)} %collective-permute-done.1.prods_ref.prod_ref, ...), custom_call_target="tpu_custom_call" | custom-call | flops 16999999488 | bytes 1048576 | tf_op jit(solution)/shard_map/ritz_second/pallas_call | solution.py:236
  181.6 0.8 broadcast_in_dim.14
  182.4 3.6 %all-to-all-start.8 = ((f32[16,64,128]{2,1,0:T(8,128)}), f32[16,64,128]{2,1,0:T(8,128)S(1)}, u32[]{:S(2)}, u32[]{:S(2)}) async-start(f32[16,64,128]{2,1,0:T(8,128)} %broadcast_in_dim.14), calls=%async_computation.8 | async-start | bytes 1048576 | tf_op jit(solution)/shard_map/all_to_all | solution.py:23
  186.0 12.0 %all-gather.7.cloned.1.call-done = f32[2048,128]{1,0:T(8,128)} async-done(((f32[128,128]{1,0:T(8,128)}), f32[2048,128]{1,0:T(8,128)}) %all-gather.7.cloned.1.call-update) | async-done | bytes 1048592 | tf_op jit(solution)/shard_map/all_gather | solution.py:458
  198.0 2.9 %outputs.1 = (f32[64,2048]{1,0:T(8,128)}, f32[64,2048]{1,0:T(8,128)}) custom-call(f32[256,128]{1,0:T(8,128)} %copy-done.2, f32[64,2048]{1,0:T(8,128)} %bitcast.32, f32[64,2048]{1,0:T(8,128)} %bitcast.34, f32[64,2048]{1,0:T(8,128)} %bitcast.36, f32[16,128,128]{2,1,0:T(8,128)} %bitcast.38), custom_call_target="tpu_custom_call" | custom-call | flops 3000000000 | bytes 5242880 | tf_op jit(solution)/shard_map/outputs/pallas_call | solution.py:392
  200.9 0.8 bitcast_bitcast_fusion
  (25 shorter events, 4.4 us)
Async XLA Ops:
  17.7 27.7 %all-to-all-start = ((f32[8,384,128]{2,1,0:T(8,128)}), f32[8,384,128]{2,1,0:T(8,128)S(1)}, u32[]{:S(2)}, u32[]{:S(2)}) async-start(f32[8,384,128]{2,1,0:T(8,128)} %products.1), calls=%async_computation | async-start | bytes 3145728 | tf_op jit(solution)/shard_map/all_to_all | solution.py:427
  23.1 79.9 %all-gather.5.cloned.1.call-start = ((), (), s32[]{:S(2)}) async-start(), calls=%async_computation.9 | async-start | bytes 1769472 | tf_op jit(solution)/shard_map/all_gather | solution.py:432
  24.7 0.7 collective-permute-start
  76.5 10.2 %all-to-all-start.3 = ((f32[8,48,128]{2,1,0:T(8,128)}), f32[8,48,128]{2,1,0:T(8,128)S(1)}, u32[]{:S(2)}, u32[]{:S(2)}) async-start(f32[8,48,128]{2,1,0:T(8,128)} %broadcast_in_dim.11), calls=%async_computation.3 | async-start | bytes 393216 | tf_op jit(solution)/shard_map/all_to_all | solution.py:23
  79.9 23.1 %collective-permute-start.1 = (f32[384,128]{1,0:T(8,128)}, f32[384,128]{1,0:T(8,128)S(1)}, u32[]{:S(2)}, u32[]{:S(2)}) collective-permute-start(f32[384,128]{1,0:T(8,128)} %get-tuple-element.23), channel_id=1, source_target_pairs={{0,0},{16,1},{32,2},{48,3},{64,4},{80,5},{96,6},{112,7},{1,8},{17,... | collective-permute-start | bytes 589832 | tf_op jit(solution)/shard_map/ppermute | solution.py:431
  102.3 0.7 copy-start
  113.9 22.0 %copy-start.1 = (f32[384,64]{1,0:T(8,128)S(1)}, f32[384,64]{1,0:T(8,128)}, u32[]{:S(2)}) copy-start(f32[384,64]{1,0:T(8,128)} %copy-done) | copy-start | bytes 294916
  145.9 11.8 %all-to-all-start.6 = ((f32[16,24,128]{2,1,0:T(8,128)}), f32[16,24,128]{2,1,0:T(8,128)S(1)}, u32[]{:S(2)}, u32[]{:S(2)}) async-start(f32[16,24,128]{2,1,0:T(8,128)} %broadcast_in_dim.12), calls=%async_computation.6 | async-start | bytes 393216 | tf_op jit(solution)/shard_map/all_to_all | solution.py:23
  149.4 48.6 %all-gather.7.cloned.1.call-start = ((), (), s32[]{:S(2)}) async-start(), calls=%async_computation.10 | async-start | bytes 1114112 | tf_op jit(solution)/shard_map/all_gather | solution.py:458
  181.5 16.5 %copy-start.2 = (f32[256,128]{1,0:T(8,128)}, f32[256,128]{1,0:T(8,128)S(1)}, u32[]{:S(2)}) copy-start(f32[256,128]{1,0:T(8,128)S(1)} %get-tuple-element.30.mix_ref) | copy-start | bytes 393220
  182.4 18.5 %all-to-all-start.8 = ((f32[16,64,128]{2,1,0:T(8,128)}), f32[16,64,128]{2,1,0:T(8,128)S(1)}, u32[]{:S(2)}, u32[]{:S(2)}) async-start(f32[16,64,128]{2,1,0:T(8,128)} %broadcast_in_dim.14), calls=%async_computation.8 | async-start | bytes 1048576 | tf_op jit(solution)/shard_map/all_to_all | solution.py:23
Sparse Core Ops, SparseCore 0:
  46.4 26.9 all-gather.4
  153.0 45.0 all-gather.6

commit v6 on v5

--- a/solution.py
+++ b/solution.py
@@ -166,20 +166,23 @@
     return ref[...]
 
 
-def first_kernel(k, order, packed_ref, turn_ref, basis_ref, old_ref, inv_ref, a_ref, b_ref):
+def first_kernel(k, order, packed_ref, turn_ref, basis_ref, inv_ref, a_ref):
     blocks = [packed_ref[i * k : (i + 1) * k] for i in range(6)]
-    blocks_a = [x[:, :k] for x in blocks]
-    blocks_b = [x[:, k:] for x in blocks]
-    whole_a = put_whole(a_ref, blocks_a, k)
-    whole_b = put_whole(b_ref, blocks_b, k)
-    coords, reduced = ritz_step(k, order, blocks_b, whole_a, inv_ref)
+    whole_a = put_whole(a_ref, [x[:, :k] for x in blocks], k)
+    coords, reduced = ritz_step(k, order, [x[:, k:] for x in blocks], whole_a, inv_ref)
     turn_ref[: 3 * k] = coords
     turn_ref[3 * k :] = -dot(coords, reduced)
     basis_ref[:k] = jnp.concatenate([coords[:k], jnp.zeros((k, k), jnp.float32)], 1)
     basis_ref[k:] = jnp.concatenate([coords[k:], coords[k:]], 1)
+
+
+def kept_kernel(packed_ref, basis_ref, old_ref, whole_ref):
+    k = basis_ref.shape[1] // 2
+    blocks = [packed_ref[i * k : (i + 1) * k] for i in range(6)]
     basis = basis_ref[...]
-    old_ref[: 2 * k] = dot(basis, dot(whole_a, basis), TN)
-    old_ref[2 * k :] = dot(basis, dot(whole_b, basis), TN)
+    for i in range(2):
+        whole = put_whole(whole_ref, [x[:, i * k : (i + 1) * k] for x in blocks], k)
+        old_ref[i * 2 * k : (i + 1) * 2 * k] = dot(basis, dot(whole, basis), TN)
 
 
 def second_kernel(
@@ -216,12 +219,14 @@
     more = more_ref[...].T
     mix_ref[: 3 * k] = jnp.concatenate([move_x, move_p], 1)
     mix_ref[3 * k :] = jnp.concatenate([from_r, from_r], 1)
-    r_ref[...] = (
+    resid = (
         dot(move_x, prod_ref[: 3 * k], TN)
         - dot(dot(move_x, reduced), prod_ref[3 * k :], TN)
         + dot(from_r, more[:k], TN)
         - dot(dot(from_r, reduced), more[k:], TN)
     )
+    for i in range(r_ref.shape[0]):
+        r_ref[i] = resid
 
 
 def f32(*shape):
@@ -293,18 +298,23 @@
             at += k
 
 
-def fresh_kernel(parts_ref, turn_ref, prods_ref, basis_ref, own_ref, more_ref, resid_ref, out_ref):
+def tests_kernel(turn_ref, prods_ref, basis_ref, own_ref, out_ref, resid_ref):
     k = turn_ref.shape[1]
+    resid = dot(turn_ref[...], prods_ref[...], TN)
+    resid_ref[:k] = resid
+    resid_ref[k:] = jnp.zeros_like(resid)
+    kept = dot(basis_ref[...], own_ref[...], TN)
+    out_ref[:k] = kept[:k]
+    out_ref[k : 2 * k] = resid
+    out_ref[2 * k :] = kept[k:]
+
+
+def fresh_kernel(parts_ref, tests_ref, more_ref, out_ref):
     more = parts_ref[0]
     for i in range(1, parts_ref.shape[0]):
         more = more + parts_ref[i]
     more_ref[...] = more
-    resid = dot(turn_ref[...], prods_ref[...], TN)
-    resid_ref[:k] = resid
-    resid_ref[k:] = jnp.zeros_like(resid)
-    kept = dot(basis_ref[...], own_ref[...], TN)
-    tests = jnp.concatenate([kept[:k], resid, kept[k:]], 0)
-    out_ref[...] = three(split(tests), split(more), ((1,), (0,)))
+    out_ref[...] = three(split(tests_ref[...]), split(more), ((1,), (0,)))
 
 
 def outputs_kernel(mix_ref, x_ref, r_ref, p_ref, resid_ref, x_out, p_out):
@@ -431,11 +441,11 @@
     prod_row = lax.ppermute(prod_col, BOTH, to_row)
     prods_col = lax.all_gather(prod_col, "row")
     packed = sum_everywhere(packed)
-    turn, basis, old = call(
+    turn, basis = call(
         functools.partial(first_kernel, k, order),
         "ritz_first",
-        (f32(6 * k, k), f32(3 * k, 2 * k), f32(4 * k, 2 * k)),
-        [(3 * k, 3 * k)] * 3,
+        (f32(6 * k, k), f32(3 * k, 2 * k)),
+        [(3 * k, 3 * k)] * 2,
         1.7e10,
         packed,
     )
@@ -443,33 +453,37 @@
 
     parts = residual_products(turn, prods_col, a_matrix, b_matrix)
     parts = lax.all_to_all(parts.reshape(cols, piece, 2 * k), "col", 0, 0)
-    more_row, resid_row, fresh = call(
-        fresh_kernel,
-        "fresh",
-        (f32(piece, 2 * k), f32(2 * k, piece), f32(3 * k, 2 * k)),
+    old = call(kept_kernel, "kept", f32(4 * k, 2 * k), [(3 * k, 3 * k)], 3e9, packed, basis)
+    tests, resid_row = call(
+        tests_kernel,
+        "tests",
+        (f32(3 * k, piece), f32(2 * k, piece)),
         [],
         1e9,
-        parts,
         turn,
         prod_row,
         basis,
         own_row,
     )
+    more_row, fresh = call(
+        fresh_kernel, "fresh", (f32(piece, 2 * k), f32(3 * k, 2 * k)), [], 1e9, parts, tests
+    )
+    fresh, resid_row = lax.optimization_barrier((fresh, resid_row))
     resid = lax.all_gather(resid_row, "col")
     fresh = sum_everywhere(fresh)
     r_own, mix = call(
         functools.partial(second_kernel, k, order),
         "ritz_second",
-        (f32(k, piece), f32(4 * k, 2 * k)),
+        (f32(cols, k, piece), f32(4 * k, 2 * k)),
         [(3 * k, 3 * k)] * 2,
-        1.7e10,
+        1e7,
         old,
         fresh,
         basis,
         prod_row,
         more_row,
     )
-    r_next = share(r_own, "col")
+    r_next = lax.all_to_all(r_own, "col", 0, 0)
     x_next, p_next = outputs(mix, *panel, resid)
     r_next, x_next, p_next = lax.optimization_barrier((r_next, x_next, p_next))
     r_next = r_next.transpose(1, 0, 2).reshape(k, -1)

time: 211 us -> 205 us (0.972)
  blocking collectives: 67.8 us -> 48.6 us
  waiting for transfers between devices: 45.5 us -> 53.8 us
  starting transfers between devices: 18.2 us -> 23.7 us
    all_to_all x0 -> x2, waiting for transfers between devices: none -> 24.6 us  [the longest x1 15.8 us: local(): parts = lax.all_to_all(parts.reshape(cols, piece, 2 * k), 'col', 0, 0)]
    all_to_all x1 -> x0, blocking collectives: 22 us -> none  [local(): parts = lax.all_to_all(parts.reshape(cols, piece, 2 * k), 'col', 0, 0)]
    all_gather x1, waiting for transfers between devices: 12 us -> 0.02 us  [local(): resid = lax.all_gather(resid_row, 'col')]
    all_to_all x0 -> x2, starting transfers between devices: none -> 9 us  [the longest x1 5.43 us: local(): parts = lax.all_to_all(parts.reshape(cols, piece, 2 * k), 'col', 0, 0)]
    all_to_all x3 -> x2, waiting for transfers between devices: 12.7 us -> 9.17 us  [share(): return lax.all_to_all(copies, axis, 0, 0)]
    all_to_all x3 -> x2, starting transfers between devices: 10.5 us -> 6.97 us  [share(): return lax.all_to_all(copies, axis, 0, 0)]
    all_to_all x2, blocking collectives: 25.8 us -> 28.7 us  [share(): return lax.all_to_all(copies, axis, 0, 0)]
    pallas_call x4 -> x6, Pallas kernels: 33.2 us -> 34.8 us  [call(): pl.pallas_call(kernel, out_shape=out_shape, scratch_shapes=[pltpu.VMEM(sh...]
  transfers between devices with their start and end apart: 8 -> 9, of which waited for: 4 -> 5; matrix products, arithmetic and copies ran while one was open for 2% -> 1% of each run, Pallas kernels for 16% -> 18%
where the time goes in v6:
time: 205 us
  Pallas kernels  59.1 us (29%)
  waiting for transfers between devices  53.8 us (26%)
  blocking collectives  48.6 us (24%)
  starting transfers between devices  23.7 us (12%)
  between operations  14.2 us (7%)
  local copies, waits for them, and re-layouts  5.09 us (2%)
    pallas_call x6, Pallas kernels, call(): pl.pallas_call(kernel, out_shape=out_shape, scratch_shapes=[pltpu.VMEM(sh...  34.8 us
    all_to_all x2, blocking collectives, share(): return lax.all_to_all(copies, axis, 0, 0)  28.7 us
    all_to_all x1, waiting for transfers between devices, local(): prods = lax.all_to_all(prods, 'row', 0, 0)  20 us
    all_to_all x2, blocking collectives, sum_everywhere(): own = lax.all_to_all(parts, 'row', 0, 0).sum(0)  20 us
    all_to_all x1, waiting for transfers between devices, local(): parts = lax.all_to_all(parts.reshape(cols, piece, 2 * k), 'col', 0, 0)  15.8 us
    pallas_call x1, Pallas kernels, residual_products(): pl.pallas_call(residual_kernel, grid=(rows // height,), in_specs=[pl.Bloc...  10.9 us
    pallas_call x1, Pallas kernels, products(): pl.pallas_call(products_kernel, grid=(pieces // each,), in_specs=[block,...  10.6 us
    all_to_all x2, waiting for transfers between devices, share(): return lax.all_to_all(copies, axis, 0, 0)  9.17 us
  transfers between devices with their start and end apart: 9, of which 5 were waited for; matrix products, arithmetic and copies ran while one was open for 1% of the time, Pallas kernels for 18%

profile of v6, /device:TPU:0, one launch (start us, length us, event | category | flops | bytes accessed | tf_op | source)
XLA Modules:
  0.0 204.6 jit_solution(9015901988858276698)
XLA Ops:
  7.2 10.6 %products.1 = f32[8,384,128]{2,1,0:T(8,128)} custom-call(f32[64,2048]{1,0:T(8,128)} %bitcast.32, f32[64,2048]{1,0:T(8,128)} %bitcast.34, f32[64,2048]{1,0:T(8,128)} %bitcast.36, f32[2048,1024]{1,0:T(8,128)} %a_ref.3, f32[2048,1024]{1,0:T(8,128)} %b_ref.3), custom_call_target="tpu_custom_call" | custom-call | flops 10000000000 | bytes 16777216 | tf_op jit(solution)/shard_map/products/pallas_call | solution.py:361
  17.7 5.4 %all-to-all-start = ((f32[8,384,128]{2,1,0:T(8,128)}), f32[8,384,128]{2,1,0:T(8,128)S(1)}, u32[]{:S(2)}, u32[]{:S(2)}) async-start(f32[8,384,128]{2,1,0:T(8,128)} %products.1), calls=%async_computation | async-start | bytes 3145728 | tf_op jit(solution)/shard_map/all_to_all | solution.py:437
  25.4 20.0 %all-to-all-done.parts_ref = f32[8,384,128]{2,1,0:T(8,128)S(1)} async-done(((f32[8,384,128]{2,1,0:T(8,128)}), f32[8,384,128]{2,1,0:T(8,128)S(1)}, u32[]{:S(2)}, u32[]{:S(2)}) %all-to-all-start) | async-done | bytes 1572896 | tf_op jit(solution)/shard_map/all_to_all | solution.py:437
  45.4 0.9 gram.1
  46.3 11.8 %all_to_all.45 = f32[8,48,128]{2,1,0:T(8,128)S(1)} all-to-all(f32[8,48,128]{2,1,0:T(8,128)S(1)} %bitcast.29), channel_id=1, replica_groups=mesh['row'=8,'col'=16] {'row'}, dimensions={0} | all-to-all | bytes 393216 | tf_op jit(solution)/shard_map/all_to_all | solution.py:28
  58.1 17.6 %all_to_all.46 = f32[16,48,128]{2,1,0:T(8,128)S(1)} all-to-all(f32[16,48,128]{2,1,0:T(8,128)S(1)} %broadcast_in_dim.8), channel_id=1, replica_groups=mesh['row'=8,'col'=16] {'col'}, dimensions={0} | all-to-all | bytes 786432 | tf_op jit(solution)/shard_map/all_to_all | solution.py:23
  76.5 3.4 %all-to-all-start.3 = ((f32[8,48,128]{2,1,0:T(8,128)}), f32[8,48,128]{2,1,0:T(8,128)S(1)}, u32[]{:S(2)}, u32[]{:S(2)}) async-start(f32[8,48,128]{2,1,0:T(8,128)} %broadcast_in_dim.9), calls=%async_computation.3 | async-start | bytes 393216 | tf_op jit(solution)/shard_map/all_to_all | solution.py:23
  79.9 1.6 collective-permute-start.1
  81.5 5.2 %all-to-all-done.3 = f32[8,48,128]{2,1,0:T(8,128)S(1)} async-done(((f32[8,48,128]{2,1,0:T(8,128)}), f32[8,48,128]{2,1,0:T(8,128)S(1)}, u32[]{:S(2)}, u32[]{:S(2)}) %all-to-all-start.3) | async-done | bytes 196640 | tf_op jit(solution)/shard_map/all_to_all | solution.py:23
  86.6 14.7 %ritz_first.1 = (f32[384,64]{1,0:T(8,128)S(1)}, f32[192,128]{1,0:T(8,128)S(1)}) custom-call(f32[384,128]{1,0:T(8,128)S(1)} %bitcast.27), custom_call_target="tpu_custom_call" | custom-call | flops 16999999488 | bytes 1048576 | tf_op jit(solution)/shard_map/ritz_first/pallas_call | solution.py:241
  102.0 10.9 %residual_products.1 = f32[2048,128]{1,0:T(8,128)} custom-call(f32[384,64]{1,0:T(8,128)} %copy-done.1, f32[8,384,128]{2,1,0:T(8,128)} %bitcast.38, f32[2048,1024]{1,0:T(8,128)} %a_ref.3, f32[2048,1024]{1,0:T(8,128)} %b_ref.3), custom_call_target="tpu_custom_call" | custom-call | flops 10000000000 | bytes 16777216 | tf_op jit(solution)/shard_map/residual_products/pallas_call | solution.py:379
  112.9 5.4 %all-to-all-start.4 = ((f32[16,128,128]{2,1,0:T(8,128)}), f32[16,128,128]{2,1,0:T(8,128)S(1)}, u32[]{:S(2)}, u32[]{:S(2)}) async-start(f32[16,128,128]{2,1,0:T(8,128)} %bitcast.31), calls=%async_computation.4 | async-start | bytes 2097152 | tf_op jit(solution)/shard_map/all_to_all | solution.py:455
  118.4 1.0 tests.1
  119.4 15.8 %all-to-all-done.4.parts_ref = f32[16,128,128]{2,1,0:T(8,128)S(1)} async-done(((f32[16,128,128]{2,1,0:T(8,128)}), f32[16,128,128]{2,1,0:T(8,128)S(1)}, u32[]{:S(2)}, u32[]{:S(2)}) %all-to-all-start.4) | async-done | bytes 1048608 | tf_op jit(solution)/shard_map/all_to_all | solution.py:455
  135.5 8.2 %all_to_all.47 = f32[8,24,128]{2,1,0:T(8,128)S(1)} all-to-all(f32[8,24,128]{2,1,0:T(8,128)S(1)} %bitcast.30), channel_id=1, replica_groups=mesh['row'=8,'col'=16] {'row'}, dimensions={0} | all-to-all | bytes 196608 | tf_op jit(solution)/shard_map/all_to_all | solution.py:28
  143.7 11.1 %all_to_all.48 = f32[16,24,128]{2,1,0:T(8,128)S(1)} all-to-all(f32[16,24,128]{2,1,0:T(8,128)S(1)} %broadcast_in_dim.10), channel_id=1, replica_groups=mesh['row'=8,'col'=16] {'col'}, dimensions={0} | all-to-all | bytes 393216 | tf_op jit(solution)/shard_map/all_to_all | solution.py:23
  155.4 3.6 %all-to-all-start.7 = ((f32[8,24,128]{2,1,0:T(8,128)}), f32[8,24,128]{2,1,0:T(8,128)S(1)}, u32[]{:S(2)}, u32[]{:S(2)}) async-start(f32[8,24,128]{2,1,0:T(8,128)} %broadcast_in_dim.11), calls=%async_computation.7 | async-start | bytes 196608 | tf_op jit(solution)/shard_map/all_to_all | solution.py:23
  159.0 1.5 kept.1.old_ref
  160.5 4.0 %all-to-all-done.7 = f32[8,24,128]{2,1,0:T(8,128)S(1)} async-done(((f32[8,24,128]{2,1,0:T(8,128)}), f32[8,24,128]{2,1,0:T(8,128)S(1)}, u32[]{:S(2)}, u32[]{:S(2)}) %all-to-all-start.7) | async-done | bytes 98336 | tf_op jit(solution)/shard_map/all_to_all | solution.py:23
  164.5 16.5 %ritz_second.1 = (f32[16,64,128]{2,1,0:T(8,128)}, f32[256,128]{1,0:T(8,128)S(1)}) custom-call(f32[256,128]{1,0:T(8,128)S(1)} %kept.1.old_ref, f32[192,128]{1,0:T(8,128)S(1)} %bitcast.26, f32[192,128]{1,0:T(8,128)S(1)} %get-tuple-element.23.basis_ref, f32[384,128]{1,0:T(8,128)S(1)} %collective-permute-done.1.prods_ref.prod_ref, ...), custom_call_target="tpu_custom_call" | custom-call | flops 10000000 | bytes 1048576 | tf_op jit(solution)/shard_map/ritz_second/pallas_call | solution.py:241
  181.7 3.6 %all-to-all-start.8 = ((f32[16,64,128]{2,1,0:T(8,128)}), f32[16,64,128]{2,1,0:T(8,128)S(1)}, u32[]{:S(2)}, u32[]{:S(2)}) async-start(f32[16,64,128]{2,1,0:T(8,128)} %get-tuple-element.33), calls=%async_computation.8 | async-start | bytes 1048576 | tf_op jit(solution)/shard_map/all_to_all | solution.py:486
  185.3 2.9 %outputs.1 = (f32[64,2048]{1,0:T(8,128)}, f32[64,2048]{1,0:T(8,128)}) custom-call(f32[256,128]{1,0:T(8,128)} %copy-done, f32[64,2048]{1,0:T(8,128)} %bitcast.33, f32[64,2048]{1,0:T(8,128)} %bitcast.35, f32[64,2048]{1,0:T(8,128)} %bitcast.37, f32[16,128,128]{2,1,0:T(8,128)} %bitcast.39), custom_call_target="tpu_custom_call" | custom-call | flops 3000000000 | bytes 5242880 | tf_op jit(solution)/shard_map/outputs/pallas_call | solution.py:402
  188.1 8.8 %all-to-all-done.8 = f32[16,64,128]{2,1,0:T(8,128)S(1)} async-done(((f32[16,64,128]{2,1,0:T(8,128)}), f32[16,64,128]{2,1,0:T(8,128)S(1)}, u32[]{:S(2)}, u32[]{:S(2)}) %all-to-all-start.8) | async-done | bytes 524320 | tf_op jit(solution)/shard_map/all_to_all | solution.py:486
  196.9 0.8 bitcast_bitcast_fusion
  (27 shorter events, 5.4 us)
Async XLA Ops:
  17.7 27.7 %all-to-all-start = ((f32[8,384,128]{2,1,0:T(8,128)}), f32[8,384,128]{2,1,0:T(8,128)S(1)}, u32[]{:S(2)}, u32[]{:S(2)}) async-start(f32[8,384,128]{2,1,0:T(8,128)} %products.1), calls=%async_computation | async-start | bytes 3145728 | tf_op jit(solution)/shard_map/all_to_all | solution.py:437
  23.1 78.9 %all-gather.5.cloned.1.call-start = ((), (), s32[]{:S(2)}) async-start(), calls=%async_computation.9 | async-start | bytes 1769472 | tf_op jit(solution)/shard_map/all_gather | solution.py:442
  24.7 0.7 collective-permute-start
  76.5 10.2 %all-to-all-start.3 = ((f32[8,48,128]{2,1,0:T(8,128)}), f32[8,48,128]{2,1,0:T(8,128)S(1)}, u32[]{:S(2)}, u32[]{:S(2)}) async-start(f32[8,48,128]{2,1,0:T(8,128)} %broadcast_in_dim.9), calls=%async_computation.3 | async-start | bytes 393216 | tf_op jit(solution)/shard_map/all_to_all | solution.py:23
  79.9 22.1 %collective-permute-start.1 = (f32[384,128]{1,0:T(8,128)}, f32[384,128]{1,0:T(8,128)S(1)}, u32[]{:S(2)}, u32[]{:S(2)}) collective-permute-start(f32[384,128]{1,0:T(8,128)} %get-tuple-element.25), channel_id=1, source_target_pairs={{0,0},{16,1},{32,2},{48,3},{64,4},{80,5},{96,6},{112,7},{1,8},{17,... | collective-permute-start | bytes 589832 | tf_op jit(solution)/shard_map/ppermute | solution.py:441
  101.3 0.7 copy-start.1
  112.9 5.5 %copy-start.2 = (f32[384,64]{1,0:T(8,128)S(1)}, f32[384,64]{1,0:T(8,128)}, u32[]{:S(2)}) copy-start(f32[384,64]{1,0:T(8,128)} %copy-done.1) | copy-start | bytes 294916
  112.9 22.3 %all-to-all-start.4 = ((f32[16,128,128]{2,1,0:T(8,128)}), f32[16,128,128]{2,1,0:T(8,128)S(1)}, u32[]{:S(2)}, u32[]{:S(2)}) async-start(f32[16,128,128]{2,1,0:T(8,128)} %bitcast.31), calls=%async_computation.4 | async-start | bytes 2097152 | tf_op jit(solution)/shard_map/all_to_all | solution.py:455
  118.4 66.9 %all-gather.7.cloned.1.call-start = ((), (), s32[]{:S(2)}) async-start(), calls=%async_computation.10 | async-start | bytes 1114112 | tf_op jit(solution)/shard_map/all_gather | solution.py:472
  155.4 9.1 %all-to-all-start.7 = ((f32[8,24,128]{2,1,0:T(8,128)}), f32[8,24,128]{2,1,0:T(8,128)S(1)}, u32[]{:S(2)}, u32[]{:S(2)}) async-start(f32[8,24,128]{2,1,0:T(8,128)} %broadcast_in_dim.11), calls=%async_computation.7 | async-start | bytes 196608 | tf_op jit(solution)/shard_map/all_to_all | solution.py:23
  181.0 0.7 copy-start
  181.7 15.3 %all-to-all-start.8 = ((f32[16,64,128]{2,1,0:T(8,128)}), f32[16,64,128]{2,1,0:T(8,128)S(1)}, u32[]{:S(2)}, u32[]{:S(2)}) async-start(f32[16,64,128]{2,1,0:T(8,128)} %get-tuple-element.33), calls=%async_computation.8 | async-start | bytes 1048576 | tf_op jit(solution)/shard_map/all_to_all | solution.py:486
Sparse Core Ops, SparseCore 0:
  46.4 26.9 all-gather.4
  135.6 37.7 all-gather.6

commit v7 on v6

--- a/solution.py
+++ b/solution.py
@@ -166,14 +166,62 @@
     return ref[...]
 
 
-def first_kernel(k, order, packed_ref, turn_ref, basis_ref, inv_ref, a_ref):
+def first_kernel(
+    k,
+    order,
+    packed_ref,
+    prods_ref,
+    a_hbm,
+    b_hbm,
+    turn_ref,
+    basis_ref,
+    out_ref,
+    inv_ref,
+    whole_ref,
+    a_ref,
+    b_ref,
+    high_ref,
+    low_ref,
+    sems,
+):
+    copies = [
+        pltpu.make_async_copy(a_hbm, a_ref, sems.at[0]),
+        pltpu.make_async_copy(b_hbm, b_ref, sems.at[1]),
+    ]
+    for copy in copies:
+        copy.start()
     blocks = [packed_ref[i * k : (i + 1) * k] for i in range(6)]
-    whole_a = put_whole(a_ref, [x[:, :k] for x in blocks], k)
+    whole_a = put_whole(whole_ref, [x[:, :k] for x in blocks], k)
     coords, reduced = ritz_step(k, order, [x[:, k:] for x in blocks], whole_a, inv_ref)
     turn_ref[: 3 * k] = coords
     turn_ref[3 * k :] = -dot(coords, reduced)
     basis_ref[:k] = jnp.concatenate([coords[:k], jnp.zeros((k, k), jnp.float32)], 1)
     basis_ref[k:] = jnp.concatenate([coords[k:], coords[k:]], 1)
+
+    pieces, _, lanes = prods_ref.shape
+    turn = split(turn_ref[...])
+    for i in range(pieces):
+        block = three(turn, split(prods_ref[i]), TN).T
+        high = block.astype(jnp.bfloat16).astype(jnp.float32)
+        low = block - high
+        high_ref[i * lanes : (i + 1) * lanes] = jnp.concatenate([high, low], 1).astype(jnp.bfloat16)
+        low_ref[i * lanes : (i + 1) * lanes] = jnp.concatenate([low, high], 1).astype(jnp.bfloat16)
+    for copy in copies:
+        copy.wait()
+    height = 256
+    lane = lax.broadcasted_iota(jnp.int32, (height, 2 * k), 1)
+
+    @pl.loop(0, out_ref.shape[0] // height, unroll=8)
+    def _(step):
+        rows = pl.ds(pl.multiple_of(step * height, height), height)
+        sums = []
+        for ref, parts_ref in ((a_ref, high_ref), (b_ref, low_ref)):
+            high, low = split(ref[rows, :])
+            part = jnp.dot(high, parts_ref[...], preferred_element_type=jnp.float32) + jnp.dot(
+                low, parts_ref[...], preferred_element_type=jnp.float32
+            )
+            sums.append(part + pltpu.roll(part, k, 1))
+        out_ref[rows, :] = jnp.where(lane < k, sums[0], sums[1])
 
 
 def kept_kernel(packed_ref, basis_ref, old_ref, whole_ref):
@@ -326,32 +374,6 @@
     p_out[...] = out[k:]
 
 
-def residual_kernel(turn_ref, prods_ref, a_ref, b_ref, out_ref, first_ref, second_ref):
-    pieces, _, lanes = prods_ref.shape
-    k = turn_ref.shape[1]
-
-    @pl.when(pl.program_id(0) == 0)
-    def _():
-        turn = split(turn_ref[...])
-        for i in range(pieces):
-            block = three(split(prods_ref[i]), turn, TN)
-            high = block.astype(jnp.bfloat16).astype(jnp.float32)
-            low = block - high
-            rows = pl.ds(i * lanes, lanes)
-            first_ref[rows, :] = jnp.concatenate([high, low], 1).astype(jnp.bfloat16)
-            second_ref[rows, :] = jnp.concatenate([low, high], 1).astype(jnp.bfloat16)
-
-    sums = []
-    for ref, parts_ref in ((a_ref, first_ref), (b_ref, second_ref)):
-        high, low = split(ref[...])
-        part = jnp.dot(high, parts_ref[...], preferred_element_type=jnp.float32) + jnp.dot(
-            low, parts_ref[...], preferred_element_type=jnp.float32
-        )
-        sums.append(part + pltpu.roll(part, k, 1))
-    lane = lax.broadcasted_iota(jnp.int32, sums[0].shape, 1)
-    out_ref[...] = jnp.where(lane < k, sums[0], sums[1])
-
-
 def products(x, r, p, a, b, pieces):
     k, rows = x.shape
     lanes = a.shape[1] // pieces
@@ -371,27 +393,23 @@
     )(x, r, p, a, b)
 
 
-def residual_products(turn, prods, a, b):
-    k = turn.shape[1]
+def first_step(k, order, packed, prods, a, b):
     rows, cols = a.shape
-    height = 512
-    tile = pl.BlockSpec((height, cols), lambda i: (i, 0))
+    inside = pl.BlockSpec(memory_space=pltpu.VMEM)
+    outside = pl.BlockSpec(memory_space=pl.ANY)
     return pl.pallas_call(
-        residual_kernel,
-        grid=(rows // height,),
-        in_specs=[
-            pl.BlockSpec(turn.shape, lambda i: (0, 0)),
-            pl.BlockSpec(prods.shape, lambda i: (0, 0, 0)),
-            tile,
-            tile,
-        ],
-        out_specs=pl.BlockSpec((height, 2 * k), lambda i: (i, 0)),
-        out_shape=f32(rows, 2 * k),
-        scratch_shapes=[pltpu.VMEM((cols, 2 * k), jnp.bfloat16)] * 2,
-        compiler_params=pltpu.CompilerParams(vmem_limit_bytes=60 * 2**20),
-        cost_estimate=cost(1e10, 8 * rows * cols),
-        name="residual_products",
-    )(turn, prods, a, b)
+        functools.partial(first_kernel, k, order),
+        in_specs=[inside, inside, outside, outside],
+        out_specs=(inside, inside, inside),
+        out_shape=(f32(6 * k, k), f32(3 * k, 2 * k), f32(rows, 2 * k)),
+        scratch_shapes=[pltpu.VMEM((3 * k, 3 * k), jnp.float32)] * 2
+        + [pltpu.VMEM((rows, cols), jnp.float32)] * 2
+        + [pltpu.VMEM((cols, 2 * k), jnp.bfloat16)] * 2
+        + [pltpu.SemaphoreType.DMA((2,))],
+        compiler_params=pltpu.CompilerParams(vmem_limit_bytes=56 * 2**20),
+        cost_estimate=cost(1.7e10, 8 * rows * cols),
+        name="first_step",
+    )(packed, prods, a, b)
 
 
 def outputs(mix, x, r, p, resid):
@@ -441,17 +459,8 @@
     prod_row = lax.ppermute(prod_col, BOTH, to_row)
     prods_col = lax.all_gather(prod_col, "row")
     packed = sum_everywhere(packed)
-    turn, basis = call(
-        functools.partial(first_kernel, k, order),
-        "ritz_first",
-        (f32(6 * k, k), f32(3 * k, 2 * k)),
-        [(3 * k, 3 * k)] * 2,
-        1.7e10,
-        packed,
-    )
-    turn, prod_row = lax.optimization_barrier((turn, prod_row))
-
-    parts = residual_products(turn, prods_col, a_matrix, b_matrix)
+    turn, basis, parts = first_step(k, order, packed, prods_col, a_matrix, b_matrix)
+    turn, prod_row, parts = lax.optimization_barrier((turn, prod_row, parts))
     parts = lax.all_to_all(parts.reshape(cols, piece, 2 * k), "col", 0, 0)
     old = call(kept_kernel, "kept", f32(4 * k, 2 * k), [(3 * k, 3 * k)], 3e9, packed, basis)
     tests, resid_row = call(

time: 205 us -> 203 us (level)
  Pallas kernels: 59.1 us -> 56.7 us
    pallas_call x6 -> x5, Pallas kernels: 34.8 us -> 20 us  [call(): pl.pallas_call(kernel, out_shape=out_shape, scratch_shapes=[pltpu.VMEM(sh...]
    pallas_call x1, Pallas kernels: 10.9 us -> 23.2 us  [first_step(): pl.pallas_call(functools.partial(first_kernel, k, order), in_specs=[insid...]
  transfers between devices with their start and end apart: 9 -> 9, of which waited for: 5 -> 5; matrix products, arithmetic and copies ran while one was open for 1% -> 1% of each run, Pallas kernels for 18% -> 22%
where the time goes in v7:
time: 203 us; the launch traced here: 202 us
  Pallas kernels  56.7 us (28%)
  waiting for transfers between devices  54 us (27%)
  blocking collectives  48.6 us (24%)
  starting transfers between devices  23.5 us (12%)
  between operations  14.2 us (7%)
  local copies, waits for them, and re-layouts  5.11 us (3%)
    all_to_all x2, blocking collectives, share(): return lax.all_to_all(copies, axis, 0, 0)  28.7 us
    pallas_call x1, Pallas kernels, first_step(): pl.pallas_call(functools.partial(first_kernel, k, order), in_specs=[insid...  23.2 us
    pallas_call x5, Pallas kernels, call(): pl.pallas_call(kernel, out_shape=out_shape, scratch_shapes=[pltpu.VMEM(sh...  20 us
    all_to_all x1, waiting for transfers between devices, local(): prods = lax.all_to_all(prods, 'row', 0, 0)  20 us
    all_to_all x2, blocking collectives, sum_everywhere(): own = lax.all_to_all(parts, 'row', 0, 0).sum(0)  20 us
    all_to_all x1, waiting for transfers between devices, local(): parts = lax.all_to_all(parts.reshape(cols, piece, 2 * k), 'col', 0, 0)  15.8 us
    pallas_call x1, Pallas kernels, products(): pl.pallas_call(products_kernel, grid=(pieces // each,), in_specs=[block,...  10.5 us
    all_to_all x2, waiting for transfers between devices, share(): return lax.all_to_all(copies, axis, 0, 0)  9.38 us
  transfers between devices with their start and end apart: 9, of which 5 were waited for; matrix products, arithmetic and copies ran while one was open for 1% of the time, Pallas kernels for 22%

profile of v7, /device:TPU:0, one launch (start us, length us, event | category | flops | bytes accessed | tf_op | source)
XLA Modules:
  0.0 202.2 jit_solution(12382390378781274495)
XLA Ops:
  7.2 10.5 %products.1 = f32[8,384,128]{2,1,0:T(8,128)} custom-call(f32[64,2048]{1,0:T(8,128)} %bitcast.32, f32[64,2048]{1,0:T(8,128)} %bitcast.34, f32[64,2048]{1,0:T(8,128)} %bitcast.36, f32[2048,1024]{1,0:T(8,128)} %a_hbm.1, f32[2048,1024]{1,0:T(8,128)} %b_hbm.1), custom_call_target="tpu_custom_call" | custom-call | flops 10000000000 | bytes 16777216 | tf_op jit(solution)/shard_map/products/pallas_call | solution.py:383
  17.7 5.4 %all-to-all-start = ((f32[8,384,128]{2,1,0:T(8,128)}), f32[8,384,128]{2,1,0:T(8,128)S(1)}, u32[]{:S(2)}, u32[]{:S(2)}) async-start(f32[8,384,128]{2,1,0:T(8,128)} %products.1), calls=%async_computation | async-start | bytes 3145728 | tf_op jit(solution)/shard_map/all_to_all | solution.py:455
  23.9 0.8 dynamic-slice_bitcast_fusion
  25.4 20.0 %all-to-all-done.parts_ref = f32[8,384,128]{2,1,0:T(8,128)S(1)} async-done(((f32[8,384,128]{2,1,0:T(8,128)}), f32[8,384,128]{2,1,0:T(8,128)S(1)}, u32[]{:S(2)}, u32[]{:S(2)}) %all-to-all-start) | async-done | bytes 1572896 | tf_op jit(solution)/shard_map/all_to_all | solution.py:455
  45.4 0.9 gram.1
  46.3 11.8 %all_to_all.45 = f32[8,48,128]{2,1,0:T(8,128)S(1)} all-to-all(f32[8,48,128]{2,1,0:T(8,128)S(1)} %bitcast.29), channel_id=1, replica_groups=mesh['row'=8,'col'=16] {'row'}, dimensions={0} | all-to-all | bytes 393216 | tf_op jit(solution)/shard_map/all_to_all | solution.py:28
  58.1 17.6 %all_to_all.46 = f32[16,48,128]{2,1,0:T(8,128)S(1)} all-to-all(f32[16,48,128]{2,1,0:T(8,128)S(1)} %broadcast_in_dim.8), channel_id=1, replica_groups=mesh['row'=8,'col'=16] {'col'}, dimensions={0} | all-to-all | bytes 786432 | tf_op jit(solution)/shard_map/all_to_all | solution.py:23
  76.5 3.4 %all-to-all-start.3 = ((f32[8,48,128]{2,1,0:T(8,128)}), f32[8,48,128]{2,1,0:T(8,128)S(1)}, u32[]{:S(2)}, u32[]{:S(2)}) async-start(f32[8,48,128]{2,1,0:T(8,128)} %broadcast_in_dim.9), calls=%async_computation.3 | async-start | bytes 393216 | tf_op jit(solution)/shard_map/all_to_all | solution.py:23
  79.9 1.6 collective-permute-start.1
  81.4 5.2 %all-to-all-done.3 = f32[8,48,128]{2,1,0:T(8,128)S(1)} async-done(((f32[8,48,128]{2,1,0:T(8,128)}), f32[8,48,128]{2,1,0:T(8,128)S(1)}, u32[]{:S(2)}, u32[]{:S(2)}) %all-to-all-start.3) | async-done | bytes 196640 | tf_op jit(solution)/shard_map/all_to_all | solution.py:23
  87.3 23.2 %first_step.1 = (f32[384,64]{1,0:T(8,128)}, f32[192,128]{1,0:T(8,128)}, f32[2048,128]{1,0:T(8,128)}) custom-call(f32[384,128]{1,0:T(8,128)} %bitcast.27, f32[8,384,128]{2,1,0:T(8,128)} %bitcast.38, f32[2048,1024]{1,0:T(8,128)} %a_hbm.1, f32[2048,1024]{1,0:T(8,128)} %b_hbm.1), custom_call_target="tpu_custom_call" | custom-call | flops 16999999488 | bytes 16777216 | tf_op jit(solution)/shard_map/first_step/pallas_call | solution.py:400
  110.6 5.4 %all-to-all-start.4 = ((f32[16,128,128]{2,1,0:T(8,128)}), f32[16,128,128]{2,1,0:T(8,128)S(1)}, u32[]{:S(2)}, u32[]{:S(2)}) async-start(f32[16,128,128]{2,1,0:T(8,128)} %bitcast.31), calls=%async_computation.4 | async-start | bytes 2097152 | tf_op jit(solution)/shard_map/all_to_all | solution.py:464
  116.1 1.0 tests.1
  117.1 15.8 %all-to-all-done.4.parts_ref = f32[16,128,128]{2,1,0:T(8,128)S(1)} async-done(((f32[16,128,128]{2,1,0:T(8,128)}), f32[16,128,128]{2,1,0:T(8,128)S(1)}, u32[]{:S(2)}, u32[]{:S(2)}) %all-to-all-start.4) | async-done | bytes 1048608 | tf_op jit(solution)/shard_map/all_to_all | solution.py:464
  133.1 8.2 %all_to_all.47 = f32[8,24,128]{2,1,0:T(8,128)S(1)} all-to-all(f32[8,24,128]{2,1,0:T(8,128)S(1)} %bitcast.30), channel_id=1, replica_groups=mesh['row'=8,'col'=16] {'row'}, dimensions={0} | all-to-all | bytes 196608 | tf_op jit(solution)/shard_map/all_to_all | solution.py:28
  141.4 11.1 %all_to_all.48 = f32[16,24,128]{2,1,0:T(8,128)S(1)} all-to-all(f32[16,24,128]{2,1,0:T(8,128)S(1)} %broadcast_in_dim.10), channel_id=1, replica_groups=mesh['row'=8,'col'=16] {'col'}, dimensions={0} | all-to-all | bytes 393216 | tf_op jit(solution)/shard_map/all_to_all | solution.py:23
  153.1 3.4 %all-to-all-start.7 = ((f32[8,24,128]{2,1,0:T(8,128)}), f32[8,24,128]{2,1,0:T(8,128)S(1)}, u32[]{:S(2)}, u32[]{:S(2)}) async-start(f32[8,24,128]{2,1,0:T(8,128)} %broadcast_in_dim.11), calls=%async_computation.7 | async-start | bytes 196608 | tf_op jit(solution)/shard_map/all_to_all | solution.py:23
  156.5 1.5 kept.1.old_ref
  158.0 4.2 %all-to-all-done.7 = f32[8,24,128]{2,1,0:T(8,128)S(1)} async-done(((f32[8,24,128]{2,1,0:T(8,128)}), f32[8,24,128]{2,1,0:T(8,128)S(1)}, u32[]{:S(2)}, u32[]{:S(2)}) %all-to-all-start.7) | async-done | bytes 98336 | tf_op jit(solution)/shard_map/all_to_all | solution.py:23
  162.2 16.5 %ritz_second.1 = (f32[16,64,128]{2,1,0:T(8,128)}, f32[256,128]{1,0:T(8,128)S(1)}) custom-call(f32[256,128]{1,0:T(8,128)S(1)} %kept.1.old_ref, f32[192,128]{1,0:T(8,128)S(1)} %bitcast.26, f32[192,128]{1,0:T(8,128)S(1)} %copy-done.2, f32[384,128]{1,0:T(8,128)S(1)} %collective-permute-done.1.prods_ref.prod_ref, f32[128,128]{1,0:T(8,128)S(1)} %get-tuple-element.36.more_ref), custom_call_target="tpu_custom_call" | custom-call | flops 10000000 | bytes 1048576 | tf_op jit(solution)/shard_map/ritz_second/pallas_call | solution.py:289
  179.3 3.6 %all-to-all-start.8 = ((f32[16,64,128]{2,1,0:T(8,128)}), f32[16,64,128]{2,1,0:T(8,128)S(1)}, u32[]{:S(2)}, u32[]{:S(2)}) async-start(f32[16,64,128]{2,1,0:T(8,128)} %get-tuple-element.37), calls=%async_computation.8 | async-start | bytes 1048576 | tf_op jit(solution)/shard_map/all_to_all | solution.py:495
  182.9 2.9 %outputs.1 = (f32[64,2048]{1,0:T(8,128)}, f32[64,2048]{1,0:T(8,128)}) custom-call(f32[256,128]{1,0:T(8,128)} %copy-done.3, f32[64,2048]{1,0:T(8,128)} %bitcast.33, f32[64,2048]{1,0:T(8,128)} %bitcast.35, f32[64,2048]{1,0:T(8,128)} %bitcast.37, f32[16,128,128]{2,1,0:T(8,128)} %bitcast.39), custom_call_target="tpu_custom_call" | custom-call | flops 3000000000 | bytes 5242880 | tf_op jit(solution)/shard_map/outputs/pallas_call | solution.py:420
  185.8 8.8 %all-to-all-done.8 = f32[16,64,128]{2,1,0:T(8,128)S(1)} async-done(((f32[16,64,128]{2,1,0:T(8,128)}), f32[16,64,128]{2,1,0:T(8,128)S(1)}, u32[]{:S(2)}, u32[]{:S(2)}) %all-to-all-start.8) | async-done | bytes 524320 | tf_op jit(solution)/shard_map/all_to_all | solution.py:495
  194.6 0.8 bitcast_bitcast_fusion
  (30 shorter events, 4.6 us)
Async XLA Ops:
  17.7 27.7 %all-to-all-start = ((f32[8,384,128]{2,1,0:T(8,128)}), f32[8,384,128]{2,1,0:T(8,128)S(1)}, u32[]{:S(2)}, u32[]{:S(2)}) async-start(f32[8,384,128]{2,1,0:T(8,128)} %products.1), calls=%async_computation | async-start | bytes 3145728 | tf_op jit(solution)/shard_map/all_to_all | solution.py:455
  23.1 63.5 %all-gather.5.cloned.1.call-start = ((), (), s32[]{:S(2)}) async-start(), calls=%async_computation.9 | async-start | bytes 1769472 | tf_op jit(solution)/shard_map/all_gather | solution.py:460
  24.7 0.7 collective-permute-start
  76.5 10.2 %all-to-all-start.3 = ((f32[8,48,128]{2,1,0:T(8,128)}), f32[8,48,128]{2,1,0:T(8,128)S(1)}, u32[]{:S(2)}, u32[]{:S(2)}) async-start(f32[8,48,128]{2,1,0:T(8,128)} %broadcast_in_dim.9), calls=%async_computation.3 | async-start | bytes 393216 | tf_op jit(solution)/shard_map/all_to_all | solution.py:23
  79.9 30.7 %collective-permute-start.1 = (f32[384,128]{1,0:T(8,128)}, f32[384,128]{1,0:T(8,128)S(1)}, u32[]{:S(2)}, u32[]{:S(2)}) collective-permute-start(f32[384,128]{1,0:T(8,128)} %get-tuple-element.25), channel_id=1, source_target_pairs={{0,0},{16,1},{32,2},{48,3},{64,4},{80,5},{96,6},{112,7},{1,8},{17,... | collective-permute-start | bytes 589832 | tf_op jit(solution)/shard_map/ppermute | solution.py:459
  86.6 0.7 copy-start
  110.5 5.5 %copy-start.2 = (f32[192,128]{1,0:T(8,128)S(1)}, f32[192,128]{1,0:T(8,128)}, u32[]{:S(2)}) copy-start(f32[192,128]{1,0:T(8,128)} %get-tuple-element.26.basis_ref) | copy-start | bytes 294916
  110.5 5.5 %copy-start.4 = (f32[384,64]{1,0:T(8,128)S(1)}, f32[384,64]{1,0:T(8,128)}, u32[]{:S(2)}) copy-start(f32[384,64]{1,0:T(8,128)} %get-tuple-element.30.turn_ref) | copy-start | bytes 294916
  110.6 22.3 %all-to-all-start.4 = ((f32[16,128,128]{2,1,0:T(8,128)}), f32[16,128,128]{2,1,0:T(8,128)S(1)}, u32[]{:S(2)}, u32[]{:S(2)}) async-start(f32[16,128,128]{2,1,0:T(8,128)} %bitcast.31), calls=%async_computation.4 | async-start | bytes 2097152 | tf_op jit(solution)/shard_map/all_to_all | solution.py:464
  116.0 66.9 %all-gather.7.cloned.1.call-start = ((), (), s32[]{:S(2)}) async-start(), calls=%async_computation.10 | async-start | bytes 1114112 | tf_op jit(solution)/shard_map/all_gather | solution.py:481
  132.9 23.6 %copy-start.1 = (f32[8,48,128]{2,1,0:T(8,128)S(1)}, f32[8,48,128]{2,1,0:T(8,128)}, u32[]{:S(2)}) copy-start(f32[8,48,128]{2,1,0:T(8,128)} %copy-done) | copy-start | bytes 589828
  153.1 9.1 %all-to-all-start.7 = ((f32[8,24,128]{2,1,0:T(8,128)}), f32[8,24,128]{2,1,0:T(8,128)S(1)}, u32[]{:S(2)}, u32[]{:S(2)}) async-start(f32[8,24,128]{2,1,0:T(8,128)} %broadcast_in_dim.11), calls=%async_computation.7 | async-start | bytes 196608 | tf_op jit(solution)/shard_map/all_to_all | solution.py:23
  178.6 0.7 copy-start.3
  179.3 15.3 %all-to-all-start.8 = ((f32[16,64,128]{2,1,0:T(8,128)}), f32[16,64,128]{2,1,0:T(8,128)S(1)}, u32[]{:S(2)}, u32[]{:S(2)}) async-start(f32[16,64,128]{2,1,0:T(8,128)} %get-tuple-element.37), calls=%async_computation.8 | async-start | bytes 1048576 | tf_op jit(solution)/shard_map/all_to_all | solution.py:495
Sparse Core Ops, SparseCore 0:
  46.4 26.9 all-gather.4
  133.3 37.7 all-gather.6

commit v8 on v7

--- a/solution.py
+++ b/solution.py
@@ -146,10 +146,12 @@
     shift = total(jnp.where(diag, middle, 0.0)) * (1.0 / size)
     sign = middle - jnp.where(diag, shift, 0.0)
     sign = sign * (1.0 / jnp.sqrt(total(sign * sign) + 1e-06))
-    for turn in range(NS_STEPS):
+    for turn in range(NS_STEPS - 1):
         parts = split(sign)
         sign = 1.5 * sign - 0.5 * dot3(parts, split(dot3(parts, parts)))
-    filtered = 0.5 * (jnp.where(diag, 1.0, 0.0) - sign)[:, :k]
+    parts, first = split(sign), sign[:, :k]
+    first = 1.5 * first - 0.5 * dot3(parts, split(dot3(parts, split(first))))
+    filtered = 0.5 * (jnp.where(diag[:, :k], 1.0, 0.0) - first)
     coords = dot(inverse, filtered, TN) * math.sqrt(order)
     reduced = dot(filtered, dot(middle, filtered), TN)
     return coords, reduced
@@ -267,12 +269,11 @@
     more = more_ref[...].T
     mix_ref[: 3 * k] = jnp.concatenate([move_x, move_p], 1)
     mix_ref[3 * k :] = jnp.concatenate([from_r, from_r], 1)
-    resid = (
-        dot(move_x, prod_ref[: 3 * k], TN)
-        - dot(dot(move_x, reduced), prod_ref[3 * k :], TN)
-        + dot(from_r, more[:k], TN)
-        - dot(dot(from_r, reduced), more[k:], TN)
-    )
+    weights = jnp.concatenate(
+        [move_x, -dot(move_x, reduced), from_r, -dot(from_r, reduced)], 0
+    )
+    vectors = jnp.concatenate([prod_ref[...], more], 0)
+    resid = three(split(weights), split(vectors), TN)
     for i in range(r_ref.shape[0]):
         r_ref[i] = resid
 
@@ -429,7 +430,7 @@
         ],
         out_specs=(part, part),
         out_shape=(f32(k, rows), f32(k, rows)),
-        compiler_params=pltpu.CompilerParams(vmem_limit_bytes=60 * 2**20),
+        compiler_params=pltpu.CompilerParams(vmem_limit_bytes=16 * 2**20),
         cost_estimate=cost(3e9, 40 * rows * k),
         name="outputs",
     )(mix, x, r, p, resid)

time: 203 us -> 202 us (level)
  no operation moved by 1% of the time
where the time goes in v8:
time: 202 us; the launch traced here: 201 us
  waiting for transfers between devices  55.4 us (27%)
  Pallas kernels  55 us (27%)
  blocking collectives  48.6 us (24%)
  starting transfers between devices  23.6 us (12%)
  between operations  14.3 us (7%)
  local copies, waits for them, and re-layouts  4.16 us (2%)
    all_to_all x2, blocking collectives, share(): return lax.all_to_all(copies, axis, 0, 0)  28.7 us
    pallas_call x1, Pallas kernels, first_step(): pl.pallas_call(functools.partial(first_kernel, k, order), in_specs=[insid...  23.2 us
    all_to_all x1, waiting for transfers between devices, local(): prods = lax.all_to_all(prods, 'row', 0, 0)  21.4 us
    all_to_all x2, blocking collectives, sum_everywhere(): own = lax.all_to_all(parts, 'row', 0, 0).sum(0)  20 us
    pallas_call x5, Pallas kernels, call(): pl.pallas_call(kernel, out_shape=out_shape, scratch_shapes=[pltpu.VMEM(sh...  19.5 us
    all_to_all x1, waiting for transfers between devices, local(): parts = lax.all_to_all(parts.reshape(cols, piece, 2 * k), 'col', 0, 0)  15.8 us
    pallas_call x1, Pallas kernels, products(): pl.pallas_call(products_kernel, grid=(pieces // each,), in_specs=[block,...  10.5 us
    all_to_all x2, waiting for transfers between devices, share(): return lax.all_to_all(copies, axis, 0, 0)  9.38 us
  transfers between devices with their start and end apart: 9, of which 5 were waited for; matrix products, arithmetic and copies ran while one was open for 1% of the time, Pallas kernels for 22%

profile of v8, /device:TPU:0, one launch (start us, length us, event | category | flops | bytes accessed | tf_op | source)
XLA Modules:
  0.0 201.1 jit_solution(1739023223664680430)
XLA Ops:
  7.2 10.5 %products.1 = f32[8,384,128]{2,1,0:T(8,128)} custom-call(f32[64,2048]{1,0:T(8,128)} %bitcast.31, f32[64,2048]{1,0:T(8,128)} %bitcast.33, f32[64,2048]{1,0:T(8,128)} %bitcast.35, f32[2048,1024]{1,0:T(8,128)} %a_hbm.1, f32[2048,1024]{1,0:T(8,128)} %b_hbm.1), custom_call_target="tpu_custom_call" | custom-call | flops 10000000000 | bytes 16777216 | tf_op jit(solution)/shard_map/products/pallas_call | solution.py:384
  17.7 5.5 %all-to-all-start = ((f32[8,384,128]{2,1,0:T(8,128)}), f32[8,384,128]{2,1,0:T(8,128)S(1)}, u32[]{:S(2)}, u32[]{:S(2)}) async-start(f32[8,384,128]{2,1,0:T(8,128)} %products.1), calls=%async_computation | async-start | bytes 3145728 | tf_op jit(solution)/shard_map/all_to_all | solution.py:456
  24.1 21.4 %all-to-all-done.parts_ref = f32[8,384,128]{2,1,0:T(8,128)S(1)} async-done(((f32[8,384,128]{2,1,0:T(8,128)}), f32[8,384,128]{2,1,0:T(8,128)S(1)}, u32[]{:S(2)}, u32[]{:S(2)}) %all-to-all-start) | async-done | bytes 1572896 | tf_op jit(solution)/shard_map/all_to_all | solution.py:456
  45.5 0.9 gram.1
  46.4 11.8 %all_to_all.45 = f32[8,48,128]{2,1,0:T(8,128)S(1)} all-to-all(f32[8,48,128]{2,1,0:T(8,128)S(1)} %bitcast.29), channel_id=1, replica_groups=mesh['row'=8,'col'=16] {'row'}, dimensions={0} | all-to-all | bytes 393216 | tf_op jit(solution)/shard_map/all_to_all | solution.py:28
  58.3 17.6 %all_to_all.46 = f32[16,48,128]{2,1,0:T(8,128)S(1)} all-to-all(f32[16,48,128]{2,1,0:T(8,128)S(1)} %broadcast_in_dim.8), channel_id=1, replica_groups=mesh['row'=8,'col'=16] {'col'}, dimensions={0} | all-to-all | bytes 786432 | tf_op jit(solution)/shard_map/all_to_all | solution.py:23
  76.6 3.4 %all-to-all-start.3 = ((f32[8,48,128]{2,1,0:T(8,128)}), f32[8,48,128]{2,1,0:T(8,128)S(1)}, u32[]{:S(2)}, u32[]{:S(2)}) async-start(f32[8,48,128]{2,1,0:T(8,128)} %broadcast_in_dim.9), calls=%async_computation.3 | async-start | bytes 393216 | tf_op jit(solution)/shard_map/all_to_all | solution.py:23
  80.0 1.6 collective-permute-start.1
  81.6 5.2 %all-to-all-done.3 = f32[8,48,128]{2,1,0:T(8,128)S(1)} async-done(((f32[8,48,128]{2,1,0:T(8,128)}), f32[8,48,128]{2,1,0:T(8,128)S(1)}, u32[]{:S(2)}, u32[]{:S(2)}) %all-to-all-start.3) | async-done | bytes 196640 | tf_op jit(solution)/shard_map/all_to_all | solution.py:23
  87.4 23.2 %first_step.1 = (f32[384,64]{1,0:T(8,128)}, f32[192,128]{1,0:T(8,128)}, f32[2048,128]{1,0:T(8,128)}) custom-call(f32[384,128]{1,0:T(8,128)} %bitcast.27, f32[8,384,128]{2,1,0:T(8,128)} %bitcast.39, f32[2048,1024]{1,0:T(8,128)} %a_hbm.1, f32[2048,1024]{1,0:T(8,128)} %b_hbm.1), custom_call_target="tpu_custom_call" | custom-call | flops 16999999488 | bytes 16777216 | tf_op jit(solution)/shard_map/first_step/pallas_call | solution.py:401
  110.7 5.4 %all-to-all-start.4 = ((f32[16,128,128]{2,1,0:T(8,128)}), f32[16,128,128]{2,1,0:T(8,128)S(1)}, u32[]{:S(2)}, u32[]{:S(2)}) async-start(f32[16,128,128]{2,1,0:T(8,128)} %bitcast.38), calls=%async_computation.4 | async-start | bytes 2097152 | tf_op jit(solution)/shard_map/all_to_all | solution.py:465
  116.2 1.0 tests.1
  117.2 15.8 %all-to-all-done.4.parts_ref = f32[16,128,128]{2,1,0:T(8,128)S(1)} async-done(((f32[16,128,128]{2,1,0:T(8,128)}), f32[16,128,128]{2,1,0:T(8,128)S(1)}, u32[]{:S(2)}, u32[]{:S(2)}) %all-to-all-start.4) | async-done | bytes 1048608 | tf_op jit(solution)/shard_map/all_to_all | solution.py:465
  133.3 8.2 %all_to_all.47 = f32[8,24,128]{2,1,0:T(8,128)S(1)} all-to-all(f32[8,24,128]{2,1,0:T(8,128)S(1)} %bitcast.30), channel_id=1, replica_groups=mesh['row'=8,'col'=16] {'row'}, dimensions={0} | all-to-all | bytes 196608 | tf_op jit(solution)/shard_map/all_to_all | solution.py:28
  141.5 11.1 %all_to_all.48 = f32[16,24,128]{2,1,0:T(8,128)S(1)} all-to-all(f32[16,24,128]{2,1,0:T(8,128)S(1)} %broadcast_in_dim.10), channel_id=1, replica_groups=mesh['row'=8,'col'=16] {'col'}, dimensions={0} | all-to-all | bytes 393216 | tf_op jit(solution)/shard_map/all_to_all | solution.py:23
  153.2 3.4 %all-to-all-start.7 = ((f32[8,24,128]{2,1,0:T(8,128)}), f32[8,24,128]{2,1,0:T(8,128)S(1)}, u32[]{:S(2)}, u32[]{:S(2)}) async-start(f32[8,24,128]{2,1,0:T(8,128)} %broadcast_in_dim.11), calls=%async_computation.7 | async-start | bytes 196608 | tf_op jit(solution)/shard_map/all_to_all | solution.py:23
  156.6 1.5 kept.1.old_ref
  158.1 4.2 %all-to-all-done.7 = f32[8,24,128]{2,1,0:T(8,128)S(1)} async-done(((f32[8,24,128]{2,1,0:T(8,128)}), f32[8,24,128]{2,1,0:T(8,128)S(1)}, u32[]{:S(2)}, u32[]{:S(2)}) %all-to-all-start.7) | async-done | bytes 98336 | tf_op jit(solution)/shard_map/all_to_all | solution.py:23
  162.3 15.9 %ritz_second.1 = (f32[16,64,128]{2,1,0:T(8,128)}, f32[256,128]{1,0:T(8,128)S(1)}) custom-call(f32[256,128]{1,0:T(8,128)S(1)} %kept.1.old_ref, f32[192,128]{1,0:T(8,128)S(1)} %bitcast.26, f32[192,128]{1,0:T(8,128)S(1)} %copy-done.2, f32[384,128]{1,0:T(8,128)S(1)} %collective-permute-done.1.prods_ref.prod_ref, f32[128,128]{1,0:T(8,128)S(1)} %get-tuple-element.36.more_ref), custom_call_target="tpu_custom_call" | custom-call | flops 10000000 | bytes 1048576 | tf_op jit(solution)/shard_map/ritz_second/pallas_call | solution.py:290
  178.2 3.6 %all-to-all-start.8 = ((f32[16,64,128]{2,1,0:T(8,128)}), f32[16,64,128]{2,1,0:T(8,128)S(1)}, u32[]{:S(2)}, u32[]{:S(2)}) async-start(f32[16,64,128]{2,1,0:T(8,128)} %get-tuple-element.37), calls=%async_computation.8 | async-start | bytes 1048576 | tf_op jit(solution)/shard_map/all_to_all | solution.py:496
  181.8 1.2 copy-done.6
  183.0 1.8 outputs.1
  184.8 8.7 %all-to-all-done.8 = f32[16,64,128]{2,1,0:T(8,128)S(1)} async-done(((f32[16,64,128]{2,1,0:T(8,128)}), f32[16,64,128]{2,1,0:T(8,128)S(1)}, u32[]{:S(2)}, u32[]{:S(2)}) %all-to-all-start.8) | async-done | bytes 524320 | tf_op jit(solution)/shard_map/all_to_all | solution.py:496
  193.5 0.8 bitcast_bitcast_fusion
  (36 shorter events, 3.2 us)
Async XLA Ops:
  17.7 5.6 %copy-start.3 = (f32[2048,64]{0,1:T(8,128)S(1)}, f32[2048,64]{0,1:T(8,128)}, u32[]{:S(2)}) copy-start(f32[2048,64]{0,1:T(8,128)} %param.7) | copy-start | bytes 1572868
  17.7 5.6 %copy-start.4 = (f32[2048,64]{0,1:T(8,128)S(1)}, f32[2048,64]{0,1:T(8,128)}, u32[]{:S(2)}) copy-start(f32[2048,64]{0,1:T(8,128)} %param.8) | copy-start | bytes 1572868
  17.7 5.6 %copy-start.5 = (f32[2048,64]{0,1:T(8,128)S(1)}, f32[2048,64]{0,1:T(8,128)}, u32[]{:S(2)}) copy-start(f32[2048,64]{0,1:T(8,128)} %param.9) | copy-start | bytes 1572868
  17.7 27.8 %all-to-all-start = ((f32[8,384,128]{2,1,0:T(8,128)}), f32[8,384,128]{2,1,0:T(8,128)S(1)}, u32[]{:S(2)}, u32[]{:S(2)}) async-start(f32[8,384,128]{2,1,0:T(8,128)} %products.1), calls=%async_computation | async-start | bytes 3145728 | tf_op jit(solution)/shard_map/all_to_all | solution.py:456
  23.2 63.5 %all-gather.5.cloned.1.call-start = ((), (), s32[]{:S(2)}) async-start(), calls=%async_computation.9 | async-start | bytes 1769472 | tf_op jit(solution)/shard_map/all_gather | solution.py:461
  23.4 0.7 collective-permute-start
  76.6 10.2 %all-to-all-start.3 = ((f32[8,48,128]{2,1,0:T(8,128)}), f32[8,48,128]{2,1,0:T(8,128)S(1)}, u32[]{:S(2)}, u32[]{:S(2)}) async-start(f32[8,48,128]{2,1,0:T(8,128)} %broadcast_in_dim.9), calls=%async_computation.3 | async-start | bytes 393216 | tf_op jit(solution)/shard_map/all_to_all | solution.py:23
  80.0 30.7 %collective-permute-start.1 = (f32[384,128]{1,0:T(8,128)}, f32[384,128]{1,0:T(8,128)S(1)}, u32[]{:S(2)}, u32[]{:S(2)}) collective-permute-start(f32[384,128]{1,0:T(8,128)} %get-tuple-element.25), channel_id=1, source_target_pairs={{0,0},{16,1},{32,2},{48,3},{64,4},{80,5},{96,6},{112,7},{1,8},{17,... | collective-permute-start | bytes 589832 | tf_op jit(solution)/shard_map/ppermute | solution.py:460
  86.8 0.7 copy-start
  110.6 5.5 %copy-start.2 = (f32[192,128]{1,0:T(8,128)S(1)}, f32[192,128]{1,0:T(8,128)}, u32[]{:S(2)}) copy-start(f32[192,128]{1,0:T(8,128)} %get-tuple-element.26.basis_ref) | copy-start | bytes 294916
  110.7 5.5 %copy-start.7 = (f32[384,64]{1,0:T(8,128)S(1)}, f32[384,64]{1,0:T(8,128)}, u32[]{:S(2)}) copy-start(f32[384,64]{1,0:T(8,128)} %get-tuple-element.30.turn_ref) | copy-start | bytes 294916
  110.7 22.3 %all-to-all-start.4 = ((f32[16,128,128]{2,1,0:T(8,128)}), f32[16,128,128]{2,1,0:T(8,128)S(1)}, u32[]{:S(2)}, u32[]{:S(2)}) async-start(f32[16,128,128]{2,1,0:T(8,128)} %bitcast.38), calls=%async_computation.4 | async-start | bytes 2097152 | tf_op jit(solution)/shard_map/all_to_all | solution.py:465
  116.1 65.7 %all-gather.7.cloned.1.call-start = ((), (), s32[]{:S(2)}) async-start(), calls=%async_computation.10 | async-start | bytes 1114112 | tf_op jit(solution)/shard_map/all_gather | solution.py:482
  133.0 23.6 %copy-start.1 = (f32[8,48,128]{2,1,0:T(8,128)S(1)}, f32[8,48,128]{2,1,0:T(8,128)}, u32[]{:S(2)}) copy-start(f32[8,48,128]{2,1,0:T(8,128)} %copy-done) | copy-start | bytes 589828
  153.2 9.1 %all-to-all-start.7 = ((f32[8,24,128]{2,1,0:T(8,128)}), f32[8,24,128]{2,1,0:T(8,128)S(1)}, u32[]{:S(2)}, u32[]{:S(2)}) async-start(f32[8,24,128]{2,1,0:T(8,128)} %broadcast_in_dim.11), calls=%async_computation.7 | async-start | bytes 196608 | tf_op jit(solution)/shard_map/all_to_all | solution.py:23
  178.2 15.3 %all-to-all-start.8 = ((f32[16,64,128]{2,1,0:T(8,128)}), f32[16,64,128]{2,1,0:T(8,128)S(1)}, u32[]{:S(2)}, u32[]{:S(2)}) async-start(f32[16,64,128]{2,1,0:T(8,128)} %get-tuple-element.37), calls=%async_computation.8 | async-start | bytes 1048576 | tf_op jit(solution)/shard_map/all_to_all | solution.py:496
  181.8 1.2 copy-start.6
Sparse Core Ops, SparseCore 0:
  46.5 26.9 all-gather.4
  133.4 37.7 all-gather.6

commit v9 on v8

--- a/solution.py
+++ b/solution.py
@@ -407,7 +407,7 @@
         + [pltpu.VMEM((rows, cols), jnp.float32)] * 2
         + [pltpu.VMEM((cols, 2 * k), jnp.bfloat16)] * 2
         + [pltpu.SemaphoreType.DMA((2,))],
-        compiler_params=pltpu.CompilerParams(vmem_limit_bytes=56 * 2**20),
+        compiler_params=pltpu.CompilerParams(vmem_limit_bytes=44 * 2**20),
         cost_estimate=cost(1.7e10, 8 * rows * cols),
         name="first_step",
     )(packed, prods, a, b)

time: 202 us -> 206 us (1.020)
  Pallas kernels: 55 us -> 58.6 us
    pallas_call x1, Pallas kernels: 23.2 us -> 26.8 us  [first_step(): pl.pallas_call(functools.partial(first_kernel, k, order), in_specs=[insid...]
  transfers between devices with their start and end apart: 9 -> 9, of which waited for: 5 -> 5; matrix products, arithmetic and copies ran while one was open for 1% -> 1% of each run, Pallas kernels for 22% -> 23%
where the time goes in v9:
time: 206 us; the launch traced here: 205 us
  Pallas kernels  58.6 us (28%)
  waiting for transfers between devices  55.4 us (27%)
  blocking collectives  48.7 us (24%)
  starting transfers between devices  23.5 us (11%)
  between operations  14.2 us (7%)
  local copies, waits for them, and re-layouts  4.88 us (2%)
    all_to_all x2, blocking collectives, share(): return lax.all_to_all(copies, axis, 0, 0)  28.7 us
    pallas_call x1, Pallas kernels, first_step(): pl.pallas_call(functools.partial(first_kernel, k, order), in_specs=[insid...  26.8 us
    all_to_all x1, waiting for transfers between devices, local(): prods = lax.all_to_all(prods, 'row', 0, 0)  21.4 us
    all_to_all x2, blocking collectives, sum_everywhere(): own = lax.all_to_all(parts, 'row', 0, 0).sum(0)  20 us
    pallas_call x5, Pallas kernels, call(): pl.pallas_call(kernel, out_shape=out_shape, scratch_shapes=[pltpu.VMEM(sh...  19.5 us
    all_to_all x1, waiting for transfers between devices, local(): parts = lax.all_to_all(parts.reshape(cols, piece, 2 * k), 'col', 0, 0)  15.8 us
    pallas_call x1, Pallas kernels, products(): pl.pallas_call(products_kernel, grid=(pieces // each,), in_specs=[block,...  10.5 us
    all_to_all x2, waiting for transfers between devices, share(): return lax.all_to_all(copies, axis, 0, 0)  9.39 us
  transfers between devices with their start and end apart: 9, of which 5 were waited for; matrix products, arithmetic and copies ran while one was open for 1% of the time, Pallas kernels for 23%

profile of v9, /device:TPU:0, one launch (start us, length us, event | category | flops | bytes accessed | tf_op | source)
XLA Modules:
  0.0 205.3 jit_solution(17254422497028327748)
XLA Ops:
  7.2 10.5 %products.1 = f32[8,384,128]{2,1,0:T(8,128)} custom-call(f32[64,2048]{1,0:T(8,128)} %bitcast.31, f32[64,2048]{1,0:T(8,128)} %bitcast.33, f32[64,2048]{1,0:T(8,128)} %bitcast.35, f32[2048,1024]{1,0:T(8,128)} %a_hbm.1, f32[2048,1024]{1,0:T(8,128)} %b_hbm.1), custom_call_target="tpu_custom_call" | custom-call | flops 10000000000 | bytes 16777216 | tf_op jit(solution)/shard_map/products/pallas_call | solution.py:384
  17.7 5.5 %all-to-all-start = ((f32[8,384,128]{2,1,0:T(8,128)}), f32[8,384,128]{2,1,0:T(8,128)S(1)}, u32[]{:S(2)}, u32[]{:S(2)}) async-start(f32[8,384,128]{2,1,0:T(8,128)} %products.1), calls=%async_computation | async-start | bytes 3145728 | tf_op jit(solution)/shard_map/all_to_all | solution.py:456
  24.1 21.4 %all-to-all-done.parts_ref = f32[8,384,128]{2,1,0:T(8,128)S(1)} async-done(((f32[8,384,128]{2,1,0:T(8,128)}), f32[8,384,128]{2,1,0:T(8,128)S(1)}, u32[]{:S(2)}, u32[]{:S(2)}) %all-to-all-start) | async-done | bytes 1572896 | tf_op jit(solution)/shard_map/all_to_all | solution.py:456
  45.5 0.9 gram.1
  46.4 11.8 %all_to_all.45 = f32[8,48,128]{2,1,0:T(8,128)S(1)} all-to-all(f32[8,48,128]{2,1,0:T(8,128)S(1)} %bitcast.29), channel_id=1, replica_groups=mesh['row'=8,'col'=16] {'row'}, dimensions={0} | all-to-all | bytes 393216 | tf_op jit(solution)/shard_map/all_to_all | solution.py:28
  58.3 17.6 %all_to_all.46 = f32[16,48,128]{2,1,0:T(8,128)S(1)} all-to-all(f32[16,48,128]{2,1,0:T(8,128)S(1)} %broadcast_in_dim.8), channel_id=1, replica_groups=mesh['row'=8,'col'=16] {'col'}, dimensions={0} | all-to-all | bytes 786432 | tf_op jit(solution)/shard_map/all_to_all | solution.py:23
  76.6 3.4 %all-to-all-start.3 = ((f32[8,48,128]{2,1,0:T(8,128)}), f32[8,48,128]{2,1,0:T(8,128)S(1)}, u32[]{:S(2)}, u32[]{:S(2)}) async-start(f32[8,48,128]{2,1,0:T(8,128)} %broadcast_in_dim.9), calls=%async_computation.3 | async-start | bytes 393216 | tf_op jit(solution)/shard_map/all_to_all | solution.py:23
  80.0 1.6 collective-permute-start.1
  81.6 5.2 %all-to-all-done.3 = f32[8,48,128]{2,1,0:T(8,128)S(1)} async-done(((f32[8,48,128]{2,1,0:T(8,128)}), f32[8,48,128]{2,1,0:T(8,128)S(1)}, u32[]{:S(2)}, u32[]{:S(2)}) %all-to-all-start.3) | async-done | bytes 196640 | tf_op jit(solution)/shard_map/all_to_all | solution.py:23
  86.8 1.4 copy-done.3
  88.2 26.8 %first_step.1 = (f32[384,64]{1,0:T(8,128)S(1)}, f32[192,128]{1,0:T(8,128)S(1)}, f32[2048,128]{1,0:T(8,128)}) custom-call(f32[384,128]{1,0:T(8,128)S(1)} %bitcast.27, f32[8,384,128]{2,1,0:T(8,128)S(1)} %bitcast.37, f32[2048,1024]{1,0:T(8,128)} %a_hbm.1, f32[2048,1024]{1,0:T(8,128)} %b_hbm.1), custom_call_target="tpu_custom_call" | custom-call | flops 16999999488 | bytes 16777216 | tf_op jit(solution)/shard_map/first_step/pallas_call | solution.py:401
  115.0 5.3 %all-to-all-start.4 = ((f32[16,128,128]{2,1,0:T(8,128)}), f32[16,128,128]{2,1,0:T(8,128)S(1)}, u32[]{:S(2)}, u32[]{:S(2)}) async-start(f32[16,128,128]{2,1,0:T(8,128)} %bitcast.9), calls=%async_computation.4 | async-start | bytes 2097152 | tf_op jit(solution)/shard_map/all_to_all | solution.py:465
  120.4 1.0 tests.1
  121.4 15.8 %all-to-all-done.4.parts_ref = f32[16,128,128]{2,1,0:T(8,128)S(1)} async-done(((f32[16,128,128]{2,1,0:T(8,128)}), f32[16,128,128]{2,1,0:T(8,128)S(1)}, u32[]{:S(2)}, u32[]{:S(2)}) %all-to-all-start.4) | async-done | bytes 1048608 | tf_op jit(solution)/shard_map/all_to_all | solution.py:465
  137.5 8.2 %all_to_all.47 = f32[8,24,128]{2,1,0:T(8,128)S(1)} all-to-all(f32[8,24,128]{2,1,0:T(8,128)S(1)} %bitcast.30), channel_id=1, replica_groups=mesh['row'=8,'col'=16] {'row'}, dimensions={0} | all-to-all | bytes 196608 | tf_op jit(solution)/shard_map/all_to_all | solution.py:28
  145.7 11.1 %all_to_all.48 = f32[16,24,128]{2,1,0:T(8,128)S(1)} all-to-all(f32[16,24,128]{2,1,0:T(8,128)S(1)} %broadcast_in_dim.10), channel_id=1, replica_groups=mesh['row'=8,'col'=16] {'col'}, dimensions={0} | all-to-all | bytes 393216 | tf_op jit(solution)/shard_map/all_to_all | solution.py:23
  157.4 3.4 %all-to-all-start.7 = ((f32[8,24,128]{2,1,0:T(8,128)}), f32[8,24,128]{2,1,0:T(8,128)S(1)}, u32[]{:S(2)}, u32[]{:S(2)}) async-start(f32[8,24,128]{2,1,0:T(8,128)} %broadcast_in_dim.11), calls=%async_computation.7 | async-start | bytes 196608 | tf_op jit(solution)/shard_map/all_to_all | solution.py:23
  160.8 1.5 kept.1.old_ref
  162.3 4.2 %all-to-all-done.7 = f32[8,24,128]{2,1,0:T(8,128)S(1)} async-done(((f32[8,24,128]{2,1,0:T(8,128)}), f32[8,24,128]{2,1,0:T(8,128)S(1)}, u32[]{:S(2)}, u32[]{:S(2)}) %all-to-all-start.7) | async-done | bytes 98336 | tf_op jit(solution)/shard_map/all_to_all | solution.py:23
  166.5 15.9 %ritz_second.1 = (f32[16,64,128]{2,1,0:T(8,128)}, f32[256,128]{1,0:T(8,128)S(1)}) custom-call(f32[256,128]{1,0:T(8,128)S(1)} %kept.1.old_ref, f32[192,128]{1,0:T(8,128)S(1)} %bitcast.26, f32[192,128]{1,0:T(8,128)S(1)} %get-tuple-element.26.basis_ref, f32[384,128]{1,0:T(8,128)S(1)} %collective-permute-done.1.prods_ref.prod_ref, ...), custom_call_target="tpu_custom_call" | custom-call | flops 10000000 | bytes 1048576 | tf_op jit(solution)/shard_map/ritz_second/pallas_call | solution.py:290
  182.4 3.6 %all-to-all-start.8 = ((f32[16,64,128]{2,1,0:T(8,128)}), f32[16,64,128]{2,1,0:T(8,128)S(1)}, u32[]{:S(2)}, u32[]{:S(2)}) async-start(f32[16,64,128]{2,1,0:T(8,128)} %get-tuple-element.37), calls=%async_computation.8 | async-start | bytes 1048576 | tf_op jit(solution)/shard_map/all_to_all | solution.py:496
  186.0 1.2 copy-done.4
  187.2 1.8 outputs.1
  189.0 8.7 %all-to-all-done.8 = f32[16,64,128]{2,1,0:T(8,128)S(1)} async-done(((f32[16,64,128]{2,1,0:T(8,128)}), f32[16,64,128]{2,1,0:T(8,128)S(1)}, u32[]{:S(2)}, u32[]{:S(2)}) %all-to-all-start.8) | async-done | bytes 524320 | tf_op jit(solution)/shard_map/all_to_all | solution.py:496
  (30 shorter events, 3.4 us)
Async XLA Ops:
  17.7 5.6 %copy-start = (f32[2048,64]{0,1:T(8,128)S(1)}, f32[2048,64]{0,1:T(8,128)}, u32[]{:S(2)}) copy-start(f32[2048,64]{0,1:T(8,128)} %param.7) | copy-start | bytes 1572868
  17.7 5.6 %copy-start.1 = (f32[2048,64]{0,1:T(8,128)S(1)}, f32[2048,64]{0,1:T(8,128)}, u32[]{:S(2)}) copy-start(f32[2048,64]{0,1:T(8,128)} %param.8) | copy-start | bytes 1572868
  17.7 5.6 %copy-start.2 = (f32[2048,64]{0,1:T(8,128)S(1)}, f32[2048,64]{0,1:T(8,128)}, u32[]{:S(2)}) copy-start(f32[2048,64]{0,1:T(8,128)} %param.9) | copy-start | bytes 1572868
  17.7 27.8 %all-to-all-start = ((f32[8,384,128]{2,1,0:T(8,128)}), f32[8,384,128]{2,1,0:T(8,128)S(1)}, u32[]{:S(2)}, u32[]{:S(2)}) async-start(f32[8,384,128]{2,1,0:T(8,128)} %products.1), calls=%async_computation | async-start | bytes 3145728 | tf_op jit(solution)/shard_map/all_to_all | solution.py:456
  23.3 63.5 %all-gather.5.cloned.1.call-start = ((), (), s32[]{:S(2)}) async-start(), calls=%async_computation.9 | async-start | bytes 1769472 | tf_op jit(solution)/shard_map/all_gather | solution.py:461
  23.4 0.7 collective-permute-start
  76.6 10.2 %all-to-all-start.3 = ((f32[8,48,128]{2,1,0:T(8,128)}), f32[8,48,128]{2,1,0:T(8,128)S(1)}, u32[]{:S(2)}, u32[]{:S(2)}) async-start(f32[8,48,128]{2,1,0:T(8,128)} %broadcast_in_dim.9), calls=%async_computation.3 | async-start | bytes 393216 | tf_op jit(solution)/shard_map/all_to_all | solution.py:23
  80.0 35.0 %collective-permute-start.1 = (f32[384,128]{1,0:T(8,128)}, f32[384,128]{1,0:T(8,128)S(1)}, u32[]{:S(2)}, u32[]{:S(2)}) collective-permute-start(f32[384,128]{1,0:T(8,128)} %get-tuple-element.25), channel_id=1, source_target_pairs={{0,0},{16,1},{32,2},{48,3},{64,4},{80,5},{96,6},{112,7},{1,8},{17,... | collective-permute-start | bytes 589832 | tf_op jit(solution)/shard_map/ppermute | solution.py:460
  86.8 1.4 copy-start.3
  115.0 22.2 %all-to-all-start.4 = ((f32[16,128,128]{2,1,0:T(8,128)}), f32[16,128,128]{2,1,0:T(8,128)S(1)}, u32[]{:S(2)}, u32[]{:S(2)}) async-start(f32[16,128,128]{2,1,0:T(8,128)} %bitcast.9), calls=%async_computation.4 | async-start | bytes 2097152 | tf_op jit(solution)/shard_map/all_to_all | solution.py:465
  120.3 65.7 %all-gather.7.cloned.1.call-start = ((), (), s32[]{:S(2)}) async-start(), calls=%async_computation.10 | async-start | bytes 1114112 | tf_op jit(solution)/shard_map/all_gather | solution.py:482
  157.4 9.1 %all-to-all-start.7 = ((f32[8,24,128]{2,1,0:T(8,128)}), f32[8,24,128]{2,1,0:T(8,128)S(1)}, u32[]{:S(2)}, u32[]{:S(2)}) async-start(f32[8,24,128]{2,1,0:T(8,128)} %broadcast_in_dim.11), calls=%async_computation.7 | async-start | bytes 196608 | tf_op jit(solution)/shard_map/all_to_all | solution.py:23
  182.4 15.3 %all-to-all-start.8 = ((f32[16,64,128]{2,1,0:T(8,128)}), f32[16,64,128]{2,1,0:T(8,128)S(1)}, u32[]{:S(2)}, u32[]{:S(2)}) async-start(f32[16,64,128]{2,1,0:T(8,128)} %get-tuple-element.37), calls=%async_computation.8 | async-start | bytes 1048576 | tf_op jit(solution)/shard_map/all_to_all | solution.py:496
  186.0 1.2 copy-start.4
Sparse Core Ops, SparseCore 0:
  46.5 26.9 all-gather.4
  137.6 37.7 all-gather.6
